TPU v7x, 32 devices: a whole 2x2x4 slice. The times are simulated.
32 devices in a mesh: slab: 4 (over y, core), grp: 8 (over z, x).
Axes of the slice: x: 2, y: 2, z: 4, core: 2. Of those that a mesh axis runs over, the one named last changes fastest.
Arguments:
- diag_jac: bfloat16 [384, 625, 625], P(('slab', 'grp')), may hold values from -0.75 to 0.75
- xface_jac: bfloat16 [384, 2, 15625], P(('slab', 'grp')), may hold values from -1.5 to 1.5
- side_jac: bfloat16 [384, 4, 15625], P(('slab', 'grp')), may hold values from -1.5 to 1.5
- orient: int32 [384], P(('slab', 'grp')), may hold values from 0 to 3
- owner: int32 [384], P(('slab', 'grp')), may hold values from 0 to 1, as said below
Outputs:
- agglomerated: bfloat16 [2304, 7, 1600], P(('slab', 'grp'))
Inputs may be any that keep to these rules, and one draw needn't show every extreme that they name: An element's owner is a grp index below 2 on its own slab. Among the 12 elements of one device at most 9 share an owner; on every slab one owner receives exactly 9 elements from every device of that slab.
All inputs are finite; a program needn't handle non-finite values.
Results may differ from a plain program's by a relative error of at most 0.001.
Values may be sent and summed in bfloat16 or wider, within the bound.
No kernel may reach another device: no remote copies, remote signals or barrier semaphores. Data moves between devices by JAX's collectives and lax.ppermute only.
A program may use at most 64 MiB of HBM per device.

v0:
```python
import functools

import jax
import jax.numpy as jnp
import numpy as np
from jax import lax
from jax.experimental import pallas as pl
from jax.experimental.pallas import tpu as pltpu
from jax.sharding import PartitionSpec as P


NV = 5
PF = 4
PM = 2
PC = 1
LANES = 128
F32 = jnp.float32
BF16 = jnp.bfloat16


def gll_points(degree):
    if degree == 1:
        return np.array([-1.0, 1.0])
    if degree == 2:
        return np.array([-1.0, 0.0, 1.0])
    inner_pt = np.sqrt(3.0 / 7.0)
    return np.array([-1.0, -inner_pt, 0.0, inner_pt, 1.0])


def lagrange(source_deg, target_deg):
    source = gll_points(source_deg)
    target = gll_points(target_deg)
    result = np.ones((target_deg + 1, source_deg + 1))
    for j in range(source_deg + 1):
        for m in range(source_deg + 1):
            if m != j:
                result[:, j] = result[:, j] * (target - source[m]) / (source[j] - source[m])
    return result


def round_up(value, step):
    return -(-value // step) * step


def split(table):
    leading = table.astype(np.float32).astype(BF16)
    remainder = (table - leading.astype(np.float64)).astype(np.float32).astype(BF16)
    return leading, remainder


LINE = lagrange(PM, PF) @ lagrange(PC, PM)
SIDE = PC + 1
NCOARSE = NV * SIDE**3
PLANE = SIDE**2
UNIT = PLANE * NV * PLANE
FACE = NV * UNIT
VROW = SIDE**3 * NCOARSE
NFACES = 6
DIAG_AT = round_up(NFACES * FACE, LANES)
ROW_TILES = round_up(DIAG_AT + NCOARSE * NCOARSE, LANES) // LANES
LEFT_TILES = round_up(VROW, LANES) // LANES


def face_table():
    face = np.kron(LINE, LINE)
    table = np.kron(face, np.kron(np.eye(NV), face))
    leading, remainder = split(table)
    out = np.zeros((table.shape[0], 2 * LANES), BF16)
    out[:, :UNIT] = leading
    out[:, LANES : LANES + UNIT] = remainder
    return out


def diag_tables():
    table = np.kron(np.eye(NV), np.kron(np.kron(LINE, LINE), LINE))
    leading, remainder = split(table)
    right = np.zeros((table.shape[0], LANES), BF16)
    right[:, :NCOARSE] = leading
    right[:, LANES // 2 : LANES // 2 + NCOARSE] = remainder
    left = np.concatenate([leading.T, remainder.T], axis=0)
    return right, left


def plane_turns():
    flat = np.arange(PLANE)
    first, second = flat // SIDE, flat % SIDE
    tables = []
    for _ in range(4):
        tables.append(first * SIDE + second)
        first, second = SIDE - 1 - second, first
    return tables


def turn_tables():
    out = np.zeros((2, UNIT, 4 * LANES), BF16)
    for o, table in enumerate(plane_turns()):
        for c in range(PLANE):
            for w in range(NV):
                for d in range(PLANE):
                    new = (c * NV + w) * PLANE + d
                    out[0, (c * NV + w) * PLANE + table[d], o * LANES + new] = 1
                    out[1, (table[c] * NV + w) * PLANE + d, o * LANES + new] = 1
    return out


def spread_tables():
    half = VROW % LANES
    out = np.zeros((NFACES, UNIT, 2 * LEFT_TILES * LANES), BF16)

    def full(plane, axis, level):
        pair = [plane // SIDE, plane % SIDE]
        pair.insert(axis, level)
        return (pair[0] * SIDE + pair[1]) * SIDE + pair[2]

    for face in range(NFACES):
        axis, high = face // 2, face % 2
        for c in range(PLANE):
            for w in range(NV):
                for d in range(PLANE):
                    row = full(c, axis, high)
                    col = w * SIDE**3 + full(d, axis, 1 - high)
                    unit = (c * NV + w) * PLANE + d
                    out[face, unit, row * NCOARSE + col] = 1
                    out[face, unit, LEFT_TILES * LANES + half + row * NCOARSE + col] = 1
    return out


def face_kernel(x_ref, table_ref, out_ref, scratch, *, rows):
    width = table_ref.shape[0]
    parts = [x_ref[:, v * width : (v + 1) * width] for v in range(NV)]
    y = jnp.dot(jnp.concatenate(parts, axis=0), table_ref[...], preferred_element_type=F32)
    y = y[:, :LANES] + y[:, LANES:]
    for v in range(NV):
        scratch[:, v * UNIT : (v + 1) * UNIT] = y[v * rows : (v + 1) * rows, :UNIT]
    out_ref[...] = scratch[...].astype(BF16)


def xface_kernel(x_ref, table_ref, turn_ref, orient_ref, plus_ref, sent_ref, scratch, *, elems):
    width = table_ref.shape[0]
    rows = 2 * elems
    parts = [x_ref[:, v * width : (v + 1) * width] for v in range(NV)]
    y = jnp.dot(jnp.concatenate(parts, axis=0), table_ref[...], preferred_element_type=F32)
    y = (y[:, :LANES] + y[:, LANES:])[:, :UNIT].astype(BF16)
    for which, out_ref in enumerate((plus_ref, sent_ref)):
        start = which * elems
        mine = jnp.concatenate([y[v * rows + start : v * rows + start + elems] for v in range(NV)], axis=0)
        turned = jnp.dot(mine, turn_ref[which], preferred_element_type=F32)
        for v in range(NV):
            piece = turned[v * elems : (v + 1) * elems]
            total = jnp.zeros((elems, LANES), F32)
            for o in range(4):
                total = jnp.where(orient_ref[...] == o, piece[:, o * LANES : (o + 1) * LANES], total)
            scratch[:, v * UNIT : (v + 1) * UNIT] = total[:, :UNIT]
        out_ref[...] = scratch[...].astype(BF16)


def coarse_block(block, right, left):
    half = LANES // 2
    y = jnp.dot(block, right, preferred_element_type=F32)
    z = y + pltpu.roll(y, half, 1)
    lane = lax.broadcasted_iota(jnp.int32, z.shape, 1)
    high = z.astype(BF16).astype(F32)
    parts = jnp.where(lane < half, z, z - high).astype(BF16)
    g = jnp.dot(left, parts, preferred_element_type=F32)
    return g[:NCOARSE] + g[NCOARSE:] + pltpu.roll(g[:NCOARSE], half, 1)


def diag_kernel(
    block_ref, right_ref, left_ref, minus_ref, plus_ref, side_ref, placer_ref,
    keep_ref, send_ref, coarse, rows, packed_scr, *, elems, pad,
):
    step = pl.program_id(0)
    many = block_ref.shape[0]
    for i in range(many):
        g = coarse_block(block_ref[i], right_ref[...], left_ref[...])
        coarse[pl.ds((step * many + i) * NCOARSE, NCOARSE), :] = g

    @pl.when(step == 0)
    def _():
        rows[...] = jnp.zeros_like(rows)
        rows[:, :FACE] = minus_ref[...].astype(F32)
        rows[:, FACE : 2 * FACE] = plus_ref[...].astype(F32)
        for f in range(NFACES - 2):
            start = (2 + f) * FACE
            rows[:, start : start + FACE] = side_ref[f * pad : (f + 1) * pad].astype(F32)

    @pl.when(step == pl.num_programs(0) - 1)
    def _():
        for c in range(NCOARSE):
            piece = coarse[pl.ds(c, elems, stride=NCOARSE), :]
            start = DIAG_AT + c * NCOARSE
            rows[:elems, start : start + NCOARSE] = piece[:, :NCOARSE]
        slots = placer_ref.shape[0]
        packed = jnp.dot(placer_ref[...], rows[...].astype(BF16), preferred_element_type=F32)
        for j in range(ROW_TILES):
            packed_scr[pl.ds(j, slots, stride=ROW_TILES), :] = packed[:, j * LANES : (j + 1) * LANES]
        kept = keep_ref.shape[1] * ROW_TILES
        keep_ref[...] = packed_scr[:kept].astype(BF16).reshape(keep_ref.shape)
        send_ref[...] = packed_scr[kept:].astype(BF16).reshape(send_ref.shape)


def unpack_kernel(where_ref, *refs, owners_n, most):
    spread_ref, out_ref, tiles, flat = refs[-4:]
    kept = refs[: (len(refs) - 4) // 2]
    others = refs[(len(refs) - 4) // 2 : -4]
    slots = out_ref.shape[1]
    me = where_ref[0]

    @pl.when(me >= owners_n)
    def _():
        out_ref[...] = jnp.zeros_like(out_ref)

    @pl.when(me < owners_n)
    def _():
        step = most * ROW_TILES
        for a in range(len(kept)):
            for j in range(owners_n):
                chunk = kept[a][0] if j == 0 else others[a][j - 1]
                source = a * owners_n + lax.rem(me - j + owners_n, owners_n)
                tiles[pl.ds(source * step, step), :] = chunk.astype(F32).reshape(step, LANES)
        for j in range(ROW_TILES):
            flat[:, j * LANES : (j + 1) * LANES] = tiles[pl.ds(j, slots, stride=ROW_TILES), :]
        width = NCOARSE * NCOARSE
        out_ref[0] = flat[:, DIAG_AT : DIAG_AT + width].astype(BF16)
        half = LEFT_TILES * LANES
        for f in range(NFACES):
            sums = {}
            for parity in range(2):
                vs = list(range(parity, NV, 2))
                cuts = [f * FACE + v * UNIT for v in vs]
                units = jnp.concatenate([flat[:, c : c + UNIT] for c in cuts], axis=0).astype(BF16)
                table = spread_ref[f, :, parity * half : (parity + 1) * half]
                spread = jnp.dot(units, table, preferred_element_type=F32)
                for row, v in enumerate(vs):
                    for t in range(LEFT_TILES):
                        tile = v * VROW // LANES + t
                        if tile * LANES >= width:
                            continue
                        value = spread[row * slots : (row + 1) * slots, t * LANES : (t + 1) * LANES]
                        sums[tile] = sums[tile] + value if tile in sums else value
            for tile, value in sums.items():
                cut = min(LANES, width - tile * LANES)
                out_ref[f + 1, :, tile * LANES : tile * LANES + cut] = value[:, :cut].astype(BF16)


def call(kernel, out_shape, scratch, *args, **kwargs):
    return pl.pallas_call(kernel, out_shape=out_shape, scratch_shapes=scratch, **kwargs)(*args)


def shards(diag_jac, xface_jac, side_jac, orient, owner):
    elems = diag_jac.shape[0]
    nf = diag_jac.shape[1]
    length = xface_jac.shape[2]
    pad = round_up(elems, 16)
    grp_size = lax.axis_size("grp")
    slab_size = lax.axis_size("slab")
    owners_n = grp_size // 4
    most = max(2, 3 * elems // (2 * owners_n))
    me = lax.axis_index("grp")
    table = jnp.asarray(face_table())
    right, left = (jnp.asarray(t) for t in diag_tables())

    def by_face(array):
        turned = jnp.transpose(array, (1, 0, 2))
        turned = jnp.pad(turned, ((0, 0), (0, pad - elems), (0, 0)))
        return turned.reshape(-1, length)

    orient_col = jnp.pad(orient, (0, pad - elems))[:, None]
    sds = jax.ShapeDtypeStruct
    plus, sent = call(
        functools.partial(xface_kernel, elems=pad),
        (sds((pad, FACE), BF16), sds((pad, FACE), BF16)),
        [pltpu.VMEM((pad, FACE), F32)],
        by_face(xface_jac), table, jnp.asarray(turn_tables()), orient_col, name="xface",
    )
    minus = lax.ppermute(sent, "slab", [(i, (i + 1) % slab_size) for i in range(slab_size)])
    side = call(
        functools.partial(face_kernel, rows=4 * pad),
        sds((4 * pad, FACE), BF16),
        [pltpu.VMEM((4 * pad, FACE), F32)],
        by_face(side_jac), table, name="side",
    )
    earlier = jnp.arange(elems)[None, :] < jnp.arange(elems)[:, None]
    same = owner[:, None] == owner[None, :]
    rank = jnp.sum((same & earlier).astype(jnp.int32), axis=1)
    dest = (owner - me) % owners_n * most + rank
    dest = jnp.pad(dest, (0, pad - elems), constant_values=-1)
    placer = (jnp.arange(owners_n * most, dtype=jnp.int32)[:, None] == dest[None, :]).astype(BF16)

    many = max(n for n in range(1, 4) if elems % n == 0)
    small = [right, left, minus, plus, side, placer]
    chunk = (most, ROW_TILES, LANES)
    keep, send = pl.pallas_call(
        functools.partial(diag_kernel, elems=elems, pad=pad),
        grid=(elems // many,),
        in_specs=[pl.BlockSpec((many, nf, nf), lambda e: (e, 0, 0))]
        + [pl.BlockSpec(array.shape, lambda e: (0, 0)) for array in small],
        out_specs=[
            pl.BlockSpec((1,) + chunk, lambda e: (0, 0, 0, 0)),
            pl.BlockSpec((owners_n - 1,) + chunk, lambda e: (0, 0, 0, 0)),
        ],
        out_shape=[sds((1,) + chunk, BF16), sds((owners_n - 1,) + chunk, BF16)],
        scratch_shapes=[
            pltpu.VMEM((elems * NCOARSE, LANES), F32),
            pltpu.VMEM((pad, ROW_TILES * LANES), F32),
            pltpu.VMEM((owners_n * most * ROW_TILES, LANES), F32),
        ],
        name="diag",
    )(diag_jac, *small)

    groups = grp_size // owners_n
    arrived = []
    for j in range(1, owners_n):
        pairs = [(a * owners_n + o, a * owners_n + (o + j) % owners_n) for a in range(groups) for o in range(owners_n)]
        arrived.append(lax.ppermute(send[j - 1 : j], "grp", pairs))
    arrived = jnp.concatenate(arrived, axis=0) if len(arrived) > 1 else arrived[0]

    def to_owners(array):
        return [array] + [
            lax.ppermute(array, "grp", [(a * owners_n + o, o) for o in range(owners_n)]) for a in range(1, groups)
        ]

    kept = to_owners(keep)
    others = to_owners(arrived)
    sources = kept + others

    slots = grp_size * most
    rows = call(
        functools.partial(unpack_kernel, owners_n=owners_n, most=most),
        sds((NFACES + 1, slots, NCOARSE * NCOARSE), BF16),
        [pltpu.VMEM((slots * ROW_TILES, LANES), F32), pltpu.VMEM((slots, ROW_TILES * LANES), F32)],
        me.astype(jnp.int32)[None], *sources, jnp.asarray(spread_tables()),
        in_specs=[pl.BlockSpec(memory_space=pltpu.SMEM)] + [pl.BlockSpec(memory_space=pltpu.VMEM)] * (len(sources) + 1),
        name="unpack",
    )
    return jnp.transpose(rows, (1, 0, 2))


def solution(mesh):
    in_specs = (
        P(("slab", "grp"), None, None),
        P(("slab", "grp"), None, None),
        P(("slab", "grp"), None, None),
        P(("slab", "grp")),
        P(("slab", "grp")),
    )
    out_specs = P(("slab", "grp"), None, None)
    return jax.shard_map(shards, mesh=mesh, in_specs=in_specs, out_specs=out_specs, check_vma=False)
```

profile of v0, /device:TPU:0, one launch (start us, length us, event | category | flops | bytes accessed | tf_op | source)
XLA Modules:
  0.0 46.1 jit_solution(3222420321171724932)
XLA Ops:
  0.0 1.2 %copy.17 = bf16[2,12,15625]{2,1,0:T(8,128)(2,1)S(1)} copy(bf16[2,12,15625]{2,0,1:T(2,128)(2,1)} %bitcast.11) | data formatting | bytes 1500000
  1.2 0.7 %pad_bitcast_fusion = s32[16,1]{0,1:T(1,128)S(1)} fusion(s32[12]{0:T(128)} %param.13), kind=kLoop, calls=%fused_computation.11 | loop fusion | bytes 112 | tf_op jit(solution)/shard_map/broadcast_in_dim | solution.py:268
  1.9 0.7 %copy.15.orient_ref = s32[16,1]{1,0:T(8,128)} copy(s32[16,1]{0,1:T(1,128)S(1)} %pad_bitcast_fusion) | data formatting | bytes 128 | tf_op jit(solution)/shard_map/broadcast_in_dim | solution.py:268
  2.6 1.0 %pad.15.clone = bf16[2,16,15625]{2,1,0:T(8,128)(2,1)} pad(bf16[2,12,15625]{2,1,0:T(8,128)(2,1)S(1)} %copy.17, bf16[]{:T(256)} %constant.30.clone.1), padding=0_0x0_4x0_0 | pad | bytes 1750002 | tf_op jit(solution)/shard_map/jit(_pad)/pad | solution.py:265
  3.6 3.1 %xface.1 = (bf16[16,400]{1,0:T(8,128)(2,1)}, bf16[16,400]{1,0:T(8,128)(2,1)}) custom-call(bf16[32,15625]{1,0:T(8,128)(2,1)} %bitcast.9, bf16[3125,256]{1,0:T(8,128)(2,1)} %constant.36.clone.table_ref, bf16[2,80,512]{2,1,0:T(8,128)(2,1)} %constant.39.clone.turn_ref, s32[16,1]{1,0:T(8,128)} %copy.15.orient_ref), custom_call_target="tpu_custom_call" | custom-call | tf_op jit(solution)/shard_map/xface/pallas_call | solution.py:247
  6.7 0.5 %collective-permute-start = (bf16[16,400]{1,0:T(8,128)(2,1)}, bf16[16,400]{1,0:T(8,128)(2,1)S(1)}, u32[]{:S(2)}, u32[]{:S(2)}) collective-permute-start(bf16[16,400]{1,0:T(8,128)(2,1)} %get-tuple-element.9), channel_id=1, source_target_pairs={{0,8},{8,16},{16,24},{24,0},{1,9},{9,17},{17,25},{25,1},{2,10},{10... | collective-permute-start | bytes 38408 | tf_op jit(solution)/shard_map/ppermute | solution.py:276
  7.2 0.0 copy-done.9
  7.2 0.2 convert_reduce_fusion
  7.4 0.6 %fusion.placer_ref = bf16[18,16]{1,0:T(8,128)(2,1)} fusion(s32[16]{0:T(128)S(1)} %pad.18), kind=kLoop, calls=%fused_computation.1 | loop fusion | flops 576 | bytes 640 | tf_op jit(solution)/shard_map/convert_element_type | solution.py:288
  8.0 0.0 copy-done
  8.0 0.2 copy.18
  8.2 1.5 %pad.17.clone = bf16[4,16,15625]{2,1,0:T(8,128)(2,1)} pad(bf16[4,12,15625]{2,1,0:T(8,128)(2,1)S(1)} %copy.18, bf16[]{:T(256)} %constant.30.clone.1), padding=0_0x0_4x0_0 | pad | bytes 3500002 | tf_op jit(solution)/shard_map/jit(_pad)/pad | solution.py:265
  9.6 3.5 %side.1.side_ref = bf16[64,400]{1,0:T(8,128)(2,1)} custom-call(bf16[64,15625]{1,0:T(8,128)(2,1)} %bitcast.8, bf16[3125,256]{1,0:T(8,128)(2,1)} %constant.36.clone.table_ref), custom_call_target="tpu_custom_call" | custom-call | tf_op jit(solution)/shard_map/side/pallas_call | solution.py:247
  13.1 0.0 collective-permute-done.minus_ref
  13.1 0.6 %copy-done.8 = bf16[16,400]{1,0:T(8,128)(2,1)} copy-done((bf16[16,400]{1,0:T(8,128)(2,1)}, bf16[16,400]{1,0:T(8,128)(2,1)S(1)}, u32[]{:S(2)}) %copy-start.8) | copy-done | bytes 12824
  13.7 9.4 %diag.1 = (bf16[1,9,32,128]{3,2,1,0:T(8,128)(2,1)}, bf16[1,9,32,128]{3,2,1,0:T(8,128)(2,1)}) custom-call(bf16[12,625,625]{2,1,0:T(8,128)(2,1)} %block_ref.1, bf16[625,128]{1,0:T(8,128)(2,1)} %constant.37.clone.right_ref, bf16[80,625]{1,0:T(8,128)(2,1)} %constant.38.clone.left_ref, bf16[16,400]{1,0:T(8,128)(2,1)} %copy-done.8, ...), custom_call_target="tpu_custom_call" | custom-call | tf_op jit(solution)/shard_map/diag/pallas_call | solution.py:293
  23.1 2.5 %collective-permute-start.4 = (bf16[1,9,32,128]{3,2,1,0:T(8,128)(2,1)}, bf16[1,9,32,128]{3,2,1,0:T(8,128)(2,1)S(1)}, u32[]{:S(2)}, u32[]{:S(2)}) collective-permute-start(bf16[1,9,32,128]{3,2,1,0:T(8,128)(2,1)} %get-tuple-element.12), channel_id=1, source_target_pairs={{0,1},{1,0},{2,3},{3,2},{4,5},{5,4},{6,7},{7,6},{8,9},{9,8},{10,11... | collective-permute-start | bytes 221192 | tf_op jit(solution)/shard_map/ppermute | solution.py:315
  25.6 1.3 %collective-permute-start.1 = (bf16[1,9,32,128]{3,2,1,0:T(8,128)(2,1)}, bf16[1,9,32,128]{3,2,1,0:T(8,128)(2,1)S(1)}, u32[]{:S(2)}, u32[]{:S(2)}) collective-permute-start(bf16[1,9,32,128]{3,2,1,0:T(8,128)(2,1)} %get-tuple-element.11.refs_0_), channel_id=1, source_target_pairs={{2,0},{3,1},{10,8},{11,9},{18,16},{19,17},{26,24},{27,25}} | collective-permute-start | bytes 221192 | tf_op jit(solution)/shard_map/ppermute | solution.py:320
  26.9 1.3 %collective-permute-start.2 = (bf16[1,9,32,128]{3,2,1,0:T(8,128)(2,1)}, bf16[1,9,32,128]{3,2,1,0:T(8,128)(2,1)S(1)}, u32[]{:S(2)}, u32[]{:S(2)}) collective-permute-start(bf16[1,9,32,128]{3,2,1,0:T(8,128)(2,1)} %get-tuple-element.11.refs_0_), channel_id=1, source_target_pairs={{4,0},{5,1},{12,8},{13,9},{20,16},{21,17},{28,24},{29,25}} | collective-permute-start | bytes 221192 | tf_op jit(solution)/shard_map/ppermute | solution.py:320
  28.2 1.3 %collective-permute-start.3 = (bf16[1,9,32,128]{3,2,1,0:T(8,128)(2,1)}, bf16[1,9,32,128]{3,2,1,0:T(8,128)(2,1)S(1)}, u32[]{:S(2)}, u32[]{:S(2)}) collective-permute-start(bf16[1,9,32,128]{3,2,1,0:T(8,128)(2,1)} %get-tuple-element.11.refs_0_), channel_id=1, source_target_pairs={{6,0},{7,1},{14,8},{15,9},{22,16},{23,17},{30,24},{31,25}} | collective-permute-start | bytes 221192 | tf_op jit(solution)/shard_map/ppermute | solution.py:320
  29.5 0.0 collective-permute-done.4.refs_4_
  29.5 1.3 %collective-permute-start.5 = (bf16[1,9,32,128]{3,2,1,0:T(8,128)(2,1)S(1)}, bf16[1,9,32,128]{3,2,1,0:T(8,128)(2,1)S(1)}, u32[]{:S(2)}, u32[]{:S(2)}) collective-permute-start(bf16[1,9,32,128]{3,2,1,0:T(8,128)(2,1)S(1)} %collective-permute-done.4.refs_4_), channel_id=1, source_target_pairs={{2,0},{3,1},{10,8},{11,9},{18,16},{19,17},{26,24},{27,25}} | collective-permute-start | bytes 221192 | tf_op jit(solution)/shard_map/ppermute | solution.py:320
  30.8 1.3 %collective-permute-start.6 = (bf16[1,9,32,128]{3,2,1,0:T(8,128)(2,1)S(1)}, bf16[1,9,32,128]{3,2,1,0:T(8,128)(2,1)S(1)}, u32[]{:S(2)}, u32[]{:S(2)}) collective-permute-start(bf16[1,9,32,128]{3,2,1,0:T(8,128)(2,1)S(1)} %collective-permute-done.4.refs_4_), channel_id=1, source_target_pairs={{4,0},{5,1},{12,8},{13,9},{20,16},{21,17},{28,24},{29,25}} | collective-permute-start | bytes 221192 | tf_op jit(solution)/shard_map/ppermute | solution.py:320
  32.1 0.3 collective-permute-done.1.refs_1_
  32.4 1.3 %collective-permute-start.7 = (bf16[1,9,32,128]{3,2,1,0:T(8,128)(2,1)S(1)}, bf16[1,9,32,128]{3,2,1,0:T(8,128)(2,1)S(1)}, u32[]{:S(2)}, u32[]{:S(2)}) collective-permute-start(bf16[1,9,32,128]{3,2,1,0:T(8,128)(2,1)S(1)} %collective-permute-done.4.refs_4_), channel_id=1, source_target_pairs={{6,0},{7,1},{14,8},{15,9},{22,16},{23,17},{30,24},{31,25}} | collective-permute-start | bytes 221192 | tf_op jit(solution)/shard_map/ppermute | solution.py:320
  33.7 0.9 %collective-permute-done.2.refs_2_ = bf16[1,9,32,128]{3,2,1,0:T(8,128)(2,1)S(1)} collective-permute-done((bf16[1,9,32,128]{3,2,1,0:T(8,128)(2,1)}, bf16[1,9,32,128]{3,2,1,0:T(8,128)(2,1)S(1)}, u32[]{:S(2)}, u32[]{:S(2)}) %collective-permute-start.2) | collective-permute-done | bytes 73760 | tf_op jit(solution)/shard_map/ppermute | solution.py:320
  34.6 2.3 %collective-permute-done.3.refs_3_ = bf16[1,9,32,128]{3,2,1,0:T(8,128)(2,1)S(1)} collective-permute-done((bf16[1,9,32,128]{3,2,1,0:T(8,128)(2,1)}, bf16[1,9,32,128]{3,2,1,0:T(8,128)(2,1)S(1)}, u32[]{:S(2)}, u32[]{:S(2)}) %collective-permute-start.3) | collective-permute-done | bytes 73760 | tf_op jit(solution)/shard_map/ppermute | solution.py:320
  36.9 2.5 %collective-permute-done.5.refs_5_ = bf16[1,9,32,128]{3,2,1,0:T(8,128)(2,1)S(1)} collective-permute-done((bf16[1,9,32,128]{3,2,1,0:T(8,128)(2,1)S(1)}, bf16[1,9,32,128]{3,2,1,0:T(8,128)(2,1)S(1)}, u32[]{:S(2)}, u32[]{:S(2)}) %collective-permute-start.5) | collective-permute-done | bytes 73760 | tf_op jit(solution)/shard_map/ppermute | solution.py:320
  39.4 0.0 collective-permute-done.6.refs_6_
  39.5 1.8 %collective-permute-done.7.refs_7_ = bf16[1,9,32,128]{3,2,1,0:T(8,128)(2,1)S(1)} collective-permute-done((bf16[1,9,32,128]{3,2,1,0:T(8,128)(2,1)S(1)}, bf16[1,9,32,128]{3,2,1,0:T(8,128)(2,1)S(1)}, u32[]{:S(2)}, u32[]{:S(2)}) %collective-permute-start.7) | collective-permute-done | bytes 73760 | tf_op jit(solution)/shard_map/ppermute | solution.py:320
  41.3 0.6 %copy-done.7 = bf16[1,9,32,128]{3,2,1,0:T(8,128)(2,1)} copy-done((bf16[1,9,32,128]{3,2,1,0:T(8,128)(2,1)}, bf16[1,9,32,128]{3,2,1,0:T(8,128)(2,1)S(1)}, u32[]{:S(2)}) %copy-start.7) | copy-done | bytes 73752
  41.9 4.2 %unpack.1 = bf16[7,72,1600]{2,1,0:T(8,128)(2,1)} custom-call(s32[1]{0:T(128)} %bitcast.where_ref, bf16[1,9,32,128]{3,2,1,0:T(8,128)(2,1)} %get-tuple-element.11.refs_0_, bf16[1,9,32,128]{3,2,1,0:T(8,128)(2,1)} %copy-done.2, bf16[1,9,32,128]{3,2,1,0:T(8,128)(2,1)} %copy-done.3, bf16[1,9,32,128]{3,2,1,0:T(8,128)(2,1)} %copy-done.4, ...), custom_call_target="tpu_custom_call" | custom-call | tf_op jit(solution)/shard_map/unpack/pallas_call | solution.py:247
  (18 shorter events, 0.0 us)
Async XLA Ops:
  2.6 4.6 %copy-start.9 = (s32[12]{0:T(128)S(1)}, s32[12]{0:T(128)}, u32[]{:S(2)}) copy-start(s32[12]{0:T(128)} %param.14) | copy-start | bytes 148
  2.6 5.4 %copy-start = (bf16[12,4,15625]{2,1,0:T(4,128)(2,1)S(1)}, bf16[12,4,15625]{2,1,0:T(4,128)(2,1)}, u32[]{:S(2)}) copy-start(bf16[12,4,15625]{2,1,0:T(4,128)(2,1)} %param.12) | copy-start | bytes 4500004
  6.7 6.5 %collective-permute-start = (bf16[16,400]{1,0:T(8,128)(2,1)}, bf16[16,400]{1,0:T(8,128)(2,1)S(1)}, u32[]{:S(2)}, u32[]{:S(2)}) collective-permute-start(bf16[16,400]{1,0:T(8,128)(2,1)} %get-tuple-element.9), channel_id=1, source_target_pairs={{0,8},{8,16},{16,24},{24,0},{1,9},{9,17},{17,25},{25,1},{2,10},{10... | collective-permute-start | bytes 38408 | tf_op jit(solution)/shard_map/ppermute | solution.py:276
  13.1 0.6 %copy-start.8 = (bf16[16,400]{1,0:T(8,128)(2,1)}, bf16[16,400]{1,0:T(8,128)(2,1)S(1)}, u32[]{:S(2)}) copy-start(bf16[16,400]{1,0:T(8,128)(2,1)S(1)} %collective-permute-done.minus_ref) | copy-start | bytes 38404
  23.1 6.4 %collective-permute-start.4 = (bf16[1,9,32,128]{3,2,1,0:T(8,128)(2,1)}, bf16[1,9,32,128]{3,2,1,0:T(8,128)(2,1)S(1)}, u32[]{:S(2)}, u32[]{:S(2)}) collective-permute-start(bf16[1,9,32,128]{3,2,1,0:T(8,128)(2,1)} %get-tuple-element.12), channel_id=1, source_target_pairs={{0,1},{1,0},{2,3},{3,2},{4,5},{5,4},{6,7},{7,6},{8,9},{9,8},{10,11... | collective-permute-start | bytes 221192 | tf_op jit(solution)/shard_map/ppermute | solution.py:315
  25.6 6.9 %collective-permute-start.1 = (bf16[1,9,32,128]{3,2,1,0:T(8,128)(2,1)}, bf16[1,9,32,128]{3,2,1,0:T(8,128)(2,1)S(1)}, u32[]{:S(2)}, u32[]{:S(2)}) collective-permute-start(bf16[1,9,32,128]{3,2,1,0:T(8,128)(2,1)} %get-tuple-element.11.refs_0_), channel_id=1, source_target_pairs={{2,0},{3,1},{10,8},{11,9},{18,16},{19,17},{26,24},{27,25}} | collective-permute-start | bytes 221192 | tf_op jit(solution)/shard_map/ppermute | solution.py:320
  26.9 7.8 %collective-permute-start.2 = (bf16[1,9,32,128]{3,2,1,0:T(8,128)(2,1)}, bf16[1,9,32,128]{3,2,1,0:T(8,128)(2,1)S(1)}, u32[]{:S(2)}, u32[]{:S(2)}) collective-permute-start(bf16[1,9,32,128]{3,2,1,0:T(8,128)(2,1)} %get-tuple-element.11.refs_0_), channel_id=1, source_target_pairs={{4,0},{5,1},{12,8},{13,9},{20,16},{21,17},{28,24},{29,25}} | collective-permute-start | bytes 221192 | tf_op jit(solution)/shard_map/ppermute | solution.py:320
  28.2 8.8 %collective-permute-start.3 = (bf16[1,9,32,128]{3,2,1,0:T(8,128)(2,1)}, bf16[1,9,32,128]{3,2,1,0:T(8,128)(2,1)S(1)}, u32[]{:S(2)}, u32[]{:S(2)}) collective-permute-start(bf16[1,9,32,128]{3,2,1,0:T(8,128)(2,1)} %get-tuple-element.11.refs_0_), channel_id=1, source_target_pairs={{6,0},{7,1},{14,8},{15,9},{22,16},{23,17},{30,24},{31,25}} | collective-permute-start | bytes 221192 | tf_op jit(solution)/shard_map/ppermute | solution.py:320
  29.5 11.8 %copy-start.1 = (bf16[1,9,32,128]{3,2,1,0:T(8,128)(2,1)}, bf16[1,9,32,128]{3,2,1,0:T(8,128)(2,1)S(1)}, u32[]{:S(2)}) copy-start(bf16[1,9,32,128]{3,2,1,0:T(8,128)(2,1)S(1)} %collective-permute-done.4.refs_4_) | copy-start | bytes 221188
  29.5 9.9 %collective-permute-start.5 = (bf16[1,9,32,128]{3,2,1,0:T(8,128)(2,1)S(1)}, bf16[1,9,32,128]{3,2,1,0:T(8,128)(2,1)S(1)}, u32[]{:S(2)}, u32[]{:S(2)}) collective-permute-start(bf16[1,9,32,128]{3,2,1,0:T(8,128)(2,1)S(1)} %collective-permute-done.4.refs_4_), channel_id=1, source_target_pairs={{2,0},{3,1},{10,8},{11,9},{18,16},{19,17},{26,24},{27,25}} | collective-permute-start | bytes 221192 | tf_op jit(solution)/shard_map/ppermute | solution.py:320
  30.8 8.7 %collective-permute-start.6 = (bf16[1,9,32,128]{3,2,1,0:T(8,128)(2,1)S(1)}, bf16[1,9,32,128]{3,2,1,0:T(8,128)(2,1)S(1)}, u32[]{:S(2)}, u32[]{:S(2)}) collective-permute-start(bf16[1,9,32,128]{3,2,1,0:T(8,128)(2,1)S(1)} %collective-permute-done.4.refs_4_), channel_id=1, source_target_pairs={{4,0},{5,1},{12,8},{13,9},{20,16},{21,17},{28,24},{29,25}} | collective-permute-start | bytes 221192 | tf_op jit(solution)/shard_map/ppermute | solution.py:320
  32.4 8.8 %copy-start.2 = (bf16[1,9,32,128]{3,2,1,0:T(8,128)(2,1)}, bf16[1,9,32,128]{3,2,1,0:T(8,128)(2,1)S(1)}, u32[]{:S(2)}) copy-start(bf16[1,9,32,128]{3,2,1,0:T(8,128)(2,1)S(1)} %collective-permute-done.1.refs_1_) | copy-start | bytes 221188
  32.4 8.8 %collective-permute-start.7 = (bf16[1,9,32,128]{3,2,1,0:T(8,128)(2,1)S(1)}, bf16[1,9,32,128]{3,2,1,0:T(8,128)(2,1)S(1)}, u32[]{:S(2)}, u32[]{:S(2)}) collective-permute-start(bf16[1,9,32,128]{3,2,1,0:T(8,128)(2,1)S(1)} %collective-permute-done.4.refs_4_), channel_id=1, source_target_pairs={{6,0},{7,1},{14,8},{15,9},{22,16},{23,17},{30,24},{31,25}} | collective-permute-start | bytes 221192 | tf_op jit(solution)/shard_map/ppermute | solution.py:320
  34.6 6.6 %copy-start.3 = (bf16[1,9,32,128]{3,2,1,0:T(8,128)(2,1)}, bf16[1,9,32,128]{3,2,1,0:T(8,128)(2,1)S(1)}, u32[]{:S(2)}) copy-start(bf16[1,9,32,128]{3,2,1,0:T(8,128)(2,1)S(1)} %collective-permute-done.2.refs_2_) | copy-start | bytes 221188
  36.9 4.3 %copy-start.4 = (bf16[1,9,32,128]{3,2,1,0:T(8,128)(2,1)}, bf16[1,9,32,128]{3,2,1,0:T(8,128)(2,1)S(1)}, u32[]{:S(2)}) copy-start(bf16[1,9,32,128]{3,2,1,0:T(8,128)(2,1)S(1)} %collective-permute-done.3.refs_3_) | copy-start | bytes 221188
  39.4 1.9 %copy-start.5 = (bf16[1,9,32,128]{3,2,1,0:T(8,128)(2,1)}, bf16[1,9,32,128]{3,2,1,0:T(8,128)(2,1)S(1)}, u32[]{:S(2)}) copy-start(bf16[1,9,32,128]{3,2,1,0:T(8,128)(2,1)S(1)} %collective-permute-done.5.refs_5_) | copy-start | bytes 221188
  39.5 1.9 %copy-start.6 = (bf16[1,9,32,128]{3,2,1,0:T(8,128)(2,1)}, bf16[1,9,32,128]{3,2,1,0:T(8,128)(2,1)S(1)}, u32[]{:S(2)}) copy-start(bf16[1,9,32,128]{3,2,1,0:T(8,128)(2,1)S(1)} %collective-permute-done.6.refs_6_) | copy-start | bytes 221188
  41.3 0.6 %copy-start.7 = (bf16[1,9,32,128]{3,2,1,0:T(8,128)(2,1)}, bf16[1,9,32,128]{3,2,1,0:T(8,128)(2,1)S(1)}, u32[]{:S(2)}) copy-start(bf16[1,9,32,128]{3,2,1,0:T(8,128)(2,1)S(1)} %collective-permute-done.7.refs_7_) | copy-start | bytes 221188
where the time goes:
time: 46.5 us; the launch traced here: 46.1 us
  Pallas kernels  20.1 us (43%)
  starting transfers between devices  10.7 us (23%)
  waiting for transfers between devices  7.88 us (17%)
  local copies, waits for them, and re-layouts  6.5 us (14%)
  other arithmetic  0.79 us (2%)
    pallas_call x3, Pallas kernels, call(): pl.pallas_call(kernel, out_shape=out_shape, scratch_shapes=scratch, **kwa...  10.7 us
    pallas_call x1, Pallas kernels, shards(): pl.pallas_call(functools.partial(diag_kernel, elems=elems, pad=pad), grid...  9.37 us
    ppermute x6, waiting for transfers between devices, to_owners(): lax.ppermute(array, 'grp', [(a * owners_n + o, o) for o in range(owners_n)])  7.87 us
    ppermute x6, starting transfers between devices, to_owners(): lax.ppermute(array, 'grp', [(a * owners_n + o, o) for o in range(owners_n)])  7.73 us
    unnamed x22, local copies, waits for them, and re-layouts  2.63 us
    pad x2, local copies, waits for them, and re-layouts, by_face(): turned = jnp.pad(turned, ((0, 0), (0, pad - elems), (0, 0)))  2.52 us
    ppermute x1, starting transfers between devices, shards(): arrived.append(lax.ppermute(send[j - 1:j], 'grp', pairs))  2.47 us
    broadcast_in_dim x2, local copies, waits for them, and re-layouts, shards(): orient_col = jnp.pad(orient, (0, pad - elems))[:, None]  1.35 us
  transfers between devices with their start and end apart: 8, of which 5 were waited for; matrix products, arithmetic and copies ran while one was open for 5% of the time, Pallas kernels for 8%

commit v1 on v0

--- a/solution.py
+++ b/solution.py
@@ -16,6 +16,8 @@
 LANES = 128
 F32 = jnp.float32
 BF16 = jnp.bfloat16
+VMEM = pl.BlockSpec(memory_space=pltpu.VMEM)
+SMALL = pl.BlockSpec(memory_space=pltpu.SMEM)
 
 
 def gll_points(degree):
@@ -135,12 +137,30 @@
     out_ref[...] = scratch[...].astype(BF16)
 
 
+def as_column(row, count):
+    shape = (count, row.shape[1])
+    diagonal = lax.broadcasted_iota(jnp.int32, shape, 0) == lax.broadcasted_iota(jnp.int32, shape, 1)
+    return jnp.sum(jnp.where(diagonal, row, 0), axis=1, keepdims=True)
+
+
+def placement(owner, me, owners_n, most):
+    elems = owner.shape[1]
+    shape = (elems, elems)
+    earlier = lax.broadcasted_iota(jnp.int32, shape, 0) < lax.broadcasted_iota(jnp.int32, shape, 1)
+    same = as_column(owner, elems) == owner
+    rank = jnp.sum(jnp.where(same & earlier, 1, 0), axis=0, keepdims=True)
+    dest = lax.rem(owner - lax.rem(me, owners_n) + owners_n, owners_n) * most + rank
+    slot = lax.broadcasted_iota(jnp.int32, (owners_n * most, elems), 0)
+    return jnp.where(slot == dest, 1.0, 0.0).astype(BF16)
+
+
 def xface_kernel(x_ref, table_ref, turn_ref, orient_ref, plus_ref, sent_ref, scratch, *, elems):
     width = table_ref.shape[0]
     rows = 2 * elems
     parts = [x_ref[:, v * width : (v + 1) * width] for v in range(NV)]
     y = jnp.dot(jnp.concatenate(parts, axis=0), table_ref[...], preferred_element_type=F32)
     y = (y[:, :LANES] + y[:, LANES:])[:, :UNIT].astype(BF16)
+    orient = as_column(orient_ref[...], elems)
     for which, out_ref in enumerate((plus_ref, sent_ref)):
         start = which * elems
         mine = jnp.concatenate([y[v * rows + start : v * rows + start + elems] for v in range(NV)], axis=0)
@@ -149,7 +169,7 @@
             piece = turned[v * elems : (v + 1) * elems]
             total = jnp.zeros((elems, LANES), F32)
             for o in range(4):
-                total = jnp.where(orient_ref[...] == o, piece[:, o * LANES : (o + 1) * LANES], total)
+                total = jnp.where(orient == o, piece[:, o * LANES : (o + 1) * LANES], total)
             scratch[:, v * UNIT : (v + 1) * UNIT] = total[:, :UNIT]
         out_ref[...] = scratch[...].astype(BF16)
 
@@ -166,8 +186,8 @@
 
 
 def diag_kernel(
-    block_ref, right_ref, left_ref, minus_ref, plus_ref, side_ref, placer_ref,
-    keep_ref, send_ref, coarse, rows, packed_scr, *, elems, pad,
+    block_ref, where_ref, right_ref, left_ref, minus_ref, plus_ref, side_ref, owner_ref,
+    keep_ref, send_ref, coarse, rows, packed_scr, *, elems, pad, owners_n,
 ):
     step = pl.program_id(0)
     many = block_ref.shape[0]
@@ -190,11 +210,13 @@
             piece = coarse[pl.ds(c, elems, stride=NCOARSE), :]
             start = DIAG_AT + c * NCOARSE
             rows[:elems, start : start + NCOARSE] = piece[:, :NCOARSE]
-        slots = placer_ref.shape[0]
-        packed = jnp.dot(placer_ref[...], rows[...].astype(BF16), preferred_element_type=F32)
+        most = keep_ref.shape[1]
+        slots = owners_n * most
+        placer = placement(owner_ref[...], where_ref[0], owners_n, most)
+        packed = jnp.dot(placer, rows[:elems].astype(BF16), preferred_element_type=F32)
         for j in range(ROW_TILES):
             packed_scr[pl.ds(j, slots, stride=ROW_TILES), :] = packed[:, j * LANES : (j + 1) * LANES]
-        kept = keep_ref.shape[1] * ROW_TILES
+        kept = most * ROW_TILES
         keep_ref[...] = packed_scr[:kept].astype(BF16).reshape(keep_ref.shape)
         send_ref[...] = packed_scr[kept:].astype(BF16).reshape(send_ref.shape)
 
@@ -210,7 +232,11 @@
     def _():
         out_ref[...] = jnp.zeros_like(out_ref)
 
-    @pl.when(me < owners_n)
+    width = NCOARSE * NCOARSE
+    half = LEFT_TILES * LANES
+    block = pl.program_id(0)
+
+    @pl.when((me < owners_n) & (block == 0))
     def _():
         step = most * ROW_TILES
         for a in range(len(kept)):
@@ -220,27 +246,29 @@
                 tiles[pl.ds(source * step, step), :] = chunk.astype(F32).reshape(step, LANES)
         for j in range(ROW_TILES):
             flat[:, j * LANES : (j + 1) * LANES] = tiles[pl.ds(j, slots, stride=ROW_TILES), :]
-        width = NCOARSE * NCOARSE
         out_ref[0] = flat[:, DIAG_AT : DIAG_AT + width].astype(BF16)
-        half = LEFT_TILES * LANES
-        for f in range(NFACES):
-            sums = {}
-            for parity in range(2):
-                vs = list(range(parity, NV, 2))
-                cuts = [f * FACE + v * UNIT for v in vs]
-                units = jnp.concatenate([flat[:, c : c + UNIT] for c in cuts], axis=0).astype(BF16)
-                table = spread_ref[f, :, parity * half : (parity + 1) * half]
-                spread = jnp.dot(units, table, preferred_element_type=F32)
-                for row, v in enumerate(vs):
-                    for t in range(LEFT_TILES):
-                        tile = v * VROW // LANES + t
-                        if tile * LANES >= width:
-                            continue
-                        value = spread[row * slots : (row + 1) * slots, t * LANES : (t + 1) * LANES]
-                        sums[tile] = sums[tile] + value if tile in sums else value
-            for tile, value in sums.items():
-                cut = min(LANES, width - tile * LANES)
-                out_ref[f + 1, :, tile * LANES : tile * LANES + cut] = value[:, :cut].astype(BF16)
+
+    def spread_face(f):
+        sums = {}
+        for parity in range(2):
+            vs = list(range(parity, NV, 2))
+            cuts = [f * FACE + v * UNIT for v in vs]
+            units = jnp.concatenate([flat[:, c : c + UNIT] for c in cuts], axis=0).astype(BF16)
+            table = spread_ref[f, :, parity * half : (parity + 1) * half]
+            spread = jnp.dot(units, table, preferred_element_type=F32)
+            for row, v in enumerate(vs):
+                for t in range(LEFT_TILES):
+                    tile = v * VROW // LANES + t
+                    if tile * LANES >= width:
+                        continue
+                    value = spread[row * slots : (row + 1) * slots, t * LANES : (t + 1) * LANES]
+                    sums[tile] = sums[tile] + value if tile in sums else value
+        for tile, value in sums.items():
+            cut = min(LANES, width - tile * LANES)
+            out_ref[0, :, tile * LANES : tile * LANES + cut] = value[:, :cut].astype(BF16)
+
+    for f in range(NFACES):
+        pl.when((me < owners_n) & (block == f + 1))(functools.partial(spread_face, f))
 
 
 def call(kernel, out_shape, scratch, *args, **kwargs):
@@ -256,7 +284,7 @@
     slab_size = lax.axis_size("slab")
     owners_n = grp_size // 4
     most = max(2, 3 * elems // (2 * owners_n))
-    me = lax.axis_index("grp")
+    where = lax.axis_index("grp").astype(jnp.int32)[None]
     table = jnp.asarray(face_table())
     right, left = (jnp.asarray(t) for t in diag_tables())
 
@@ -265,36 +293,29 @@
         turned = jnp.pad(turned, ((0, 0), (0, pad - elems), (0, 0)))
         return turned.reshape(-1, length)
 
-    orient_col = jnp.pad(orient, (0, pad - elems))[:, None]
     sds = jax.ShapeDtypeStruct
     plus, sent = call(
         functools.partial(xface_kernel, elems=pad),
         (sds((pad, FACE), BF16), sds((pad, FACE), BF16)),
         [pltpu.VMEM((pad, FACE), F32)],
-        by_face(xface_jac), table, jnp.asarray(turn_tables()), orient_col, name="xface",
+        by_face(xface_jac), table, jnp.asarray(turn_tables()), orient[None, :],
+        in_specs=[VMEM] * 4, out_specs=(VMEM, VMEM), name="xface",
     )
     minus = lax.ppermute(sent, "slab", [(i, (i + 1) % slab_size) for i in range(slab_size)])
     side = call(
         functools.partial(face_kernel, rows=4 * pad),
         sds((4 * pad, FACE), BF16),
         [pltpu.VMEM((4 * pad, FACE), F32)],
-        by_face(side_jac), table, name="side",
+        by_face(side_jac), table,
+        in_specs=[VMEM] * 2, out_specs=VMEM, name="side",
     )
-    earlier = jnp.arange(elems)[None, :] < jnp.arange(elems)[:, None]
-    same = owner[:, None] == owner[None, :]
-    rank = jnp.sum((same & earlier).astype(jnp.int32), axis=1)
-    dest = (owner - me) % owners_n * most + rank
-    dest = jnp.pad(dest, (0, pad - elems), constant_values=-1)
-    placer = (jnp.arange(owners_n * most, dtype=jnp.int32)[:, None] == dest[None, :]).astype(BF16)
-
     many = max(n for n in range(1, 4) if elems % n == 0)
-    small = [right, left, minus, plus, side, placer]
+    small = [right, left, minus, plus, side, owner[None, :]]
     chunk = (most, ROW_TILES, LANES)
     keep, send = pl.pallas_call(
-        functools.partial(diag_kernel, elems=elems, pad=pad),
+        functools.partial(diag_kernel, elems=elems, pad=pad, owners_n=owners_n),
         grid=(elems // many,),
-        in_specs=[pl.BlockSpec((many, nf, nf), lambda e: (e, 0, 0))]
-        + [pl.BlockSpec(array.shape, lambda e: (0, 0)) for array in small],
+        in_specs=[pl.BlockSpec((many, nf, nf), lambda e: (e, 0, 0)), SMALL] + [VMEM] * len(small),
         out_specs=[
             pl.BlockSpec((1,) + chunk, lambda e: (0, 0, 0, 0)),
             pl.BlockSpec((owners_n - 1,) + chunk, lambda e: (0, 0, 0, 0)),
@@ -306,7 +327,7 @@
             pltpu.VMEM((owners_n * most * ROW_TILES, LANES), F32),
         ],
         name="diag",
-    )(diag_jac, *small)
+    )(diag_jac, where, *small)
 
     groups = grp_size // owners_n
     arrived = []
@@ -315,10 +336,14 @@
         arrived.append(lax.ppermute(send[j - 1 : j], "grp", pairs))
     arrived = jnp.concatenate(arrived, axis=0) if len(arrived) > 1 else arrived[0]
 
+    def exchange(a):
+        place = list(range(grp_size))
+        for o in range(owners_n):
+            place[o], place[a * owners_n + o] = a * owners_n + o, o
+        return list(enumerate(place))
+
     def to_owners(array):
-        return [array] + [
-            lax.ppermute(array, "grp", [(a * owners_n + o, o) for o in range(owners_n)]) for a in range(1, groups)
-        ]
+        return [array] + [lax.ppermute(array, "grp", exchange(a)) for a in range(1, groups)]
 
     kept = to_owners(keep)
     others = to_owners(arrived)
@@ -329,8 +354,10 @@
         functools.partial(unpack_kernel, owners_n=owners_n, most=most),
         sds((NFACES + 1, slots, NCOARSE * NCOARSE), BF16),
         [pltpu.VMEM((slots * ROW_TILES, LANES), F32), pltpu.VMEM((slots, ROW_TILES * LANES), F32)],
-        me.astype(jnp.int32)[None], *sources, jnp.asarray(spread_tables()),
-        in_specs=[pl.BlockSpec(memory_space=pltpu.SMEM)] + [pl.BlockSpec(memory_space=pltpu.VMEM)] * (len(sources) + 1),
+        where, *sources, jnp.asarray(spread_tables()),
+        grid=(NFACES + 1,),
+        in_specs=[SMALL] + [VMEM] * (len(sources) + 1),
+        out_specs=pl.BlockSpec((1, slots, NCOARSE * NCOARSE), lambda i: (i, 0, 0)),
         name="unpack",
     )
     return jnp.transpose(rows, (1, 0, 2))

time: 46.5 us -> 52.1 us (1.12)
  starting transfers between devices: 10.7 us -> 19.3 us
  waiting for transfers between devices: 7.88 us -> 4.92 us
  Pallas kernels: 20.1 us -> 22.1 us
  local copies, waits for them, and re-layouts: 6.5 us -> 5.18 us
  other arithmetic: 0.79 us -> 0 us
    ppermute x6, starting transfers between devices: 7.73 us -> 16.3 us  [to_owners(): lax.ppermute(array, 'grp', exchange(a))]
    ppermute x6, waiting for transfers between devices: 7.87 us -> 4.92 us  [to_owners(): lax.ppermute(array, 'grp', exchange(a))]
    pallas_call x3, Pallas kernels: 10.7 us -> 12.7 us  [call(): pl.pallas_call(kernel, out_shape=out_shape, scratch_shapes=scratch, **kwa...]
    broadcast_in_dim x2 -> x0, local copies, waits for them, and re-layouts: 1.35 us -> none  [shards(): orient_col = jnp.pad(orient, (0, pad - elems))[:, None]]
    convert_element_type x1 -> x0, other arithmetic: 0.6 us -> none  [shards(): (jnp.arange(owners_n * most, dtype=jnp.int32)[:, None] == dest[None, :])....]
    unnamed x22 -> x20, local copies, waits for them, and re-layouts: 2.63 us -> 2.67 us
  transfers between devices with their start and end apart: 8 -> 8, of which waited for: 5 -> 3; matrix products, arithmetic and copies ran while one was open for 5% -> 3% of each run, Pallas kernels for 8% -> 7%
where the time goes in v1:
time: 52.1 us; the launch traced here: 51.7 us
  Pallas kernels  22.1 us (42%)
  starting transfers between devices  19.3 us (37%)
  local copies, waits for them, and re-layouts  5.18 us (10%)
  waiting for transfers between devices  4.92 us (9%)
    ppermute x6, starting transfers between devices, to_owners(): lax.ppermute(array, 'grp', exchange(a))  16.3 us
    pallas_call x3, Pallas kernels, call(): pl.pallas_call(kernel, out_shape=out_shape, scratch_shapes=scratch, **kwa...  12.7 us
    pallas_call x1, Pallas kernels, shards(): pl.pallas_call(functools.partial(diag_kernel, elems=elems, pad=pad, owner...  9.4 us
    ppermute x6, waiting for transfers between devices, to_owners(): lax.ppermute(array, 'grp', exchange(a))  4.92 us
    unnamed x20, local copies, waits for them, and re-layouts  2.67 us
    pad x2, local copies, waits for them, and re-layouts, by_face(): turned = jnp.pad(turned, ((0, 0), (0, pad - elems), (0, 0)))  2.51 us
    ppermute x1, starting transfers between devices, shards(): arrived.append(lax.ppermute(send[j - 1:j], 'grp', pairs))  2.48 us
  transfers between devices with their start and end apart: 8, of which 3 were waited for; matrix products, arithmetic and copies ran while one was open for 3% of the time, Pallas kernels for 7%

profile of v1, /device:TPU:0, one launch (start us, length us, event | category | flops | bytes accessed | tf_op | source)
XLA Modules:
  0.0 51.7 jit_solution(7012588445271246306)
XLA Ops:
  0.0 1.2 %copy.13 = bf16[2,12,15625]{2,1,0:T(8,128)(2,1)S(1)} copy(bf16[2,12,15625]{2,0,1:T(2,128)(2,1)} %bitcast.11) | data formatting | bytes 1500000
  1.2 0.0 copy-start
  1.2 1.0 %pad.8.clone = bf16[2,16,15625]{2,1,0:T(8,128)(2,1)} pad(bf16[2,12,15625]{2,1,0:T(8,128)(2,1)S(1)} %copy.13, bf16[]{:T(256)} %constant.16.clone.1), padding=0_0x0_4x0_0 | pad | bytes 1750002 | tf_op jit(solution)/shard_map/jit(_pad)/pad | solution.py:293
  2.3 3.1 %xface.1 = (bf16[16,400]{1,0:T(8,128)(2,1)}, bf16[16,400]{1,0:T(8,128)(2,1)}) custom-call(bf16[32,15625]{1,0:T(8,128)(2,1)} %bitcast.9, bf16[3125,256]{1,0:T(8,128)(2,1)} %constant.17.clone.table_ref, bf16[2,80,512]{2,1,0:T(8,128)(2,1)} %constant.20.clone.turn_ref, s32[1,12]{1,0:T(1,128)} %bitcast.12), custom_call_target="tpu_custom_call" | custom-call | tf_op jit(solution)/shard_map/xface/pallas_call | solution.py:275
  5.3 0.5 collective-permute-start
  5.8 0.2 copy.14
  6.0 1.5 %pad.9.clone = bf16[4,16,15625]{2,1,0:T(8,128)(2,1)} pad(bf16[4,12,15625]{2,1,0:T(8,128)(2,1)S(1)} %copy.14, bf16[]{:T(256)} %constant.16.clone.1), padding=0_0x0_4x0_0 | pad | bytes 3500002 | tf_op jit(solution)/shard_map/jit(_pad)/pad | solution.py:293
  7.5 3.5 %side.1.side_ref = bf16[64,400]{1,0:T(8,128)(2,1)} custom-call(bf16[64,15625]{1,0:T(8,128)(2,1)} %bitcast.8, bf16[3125,256]{1,0:T(8,128)(2,1)} %constant.17.clone.table_ref), custom_call_target="tpu_custom_call" | custom-call | tf_op jit(solution)/shard_map/side/pallas_call | solution.py:275
  11.0 0.0 collective-permute-done.minus_ref
  11.0 0.6 %copy-done.8 = bf16[16,400]{1,0:T(8,128)(2,1)} copy-done((bf16[16,400]{1,0:T(8,128)(2,1)}, bf16[16,400]{1,0:T(8,128)(2,1)S(1)}, u32[]{:S(2)}) %copy-start.8) | copy-done | bytes 12824
  11.6 9.4 %diag.1 = (bf16[1,9,32,128]{3,2,1,0:T(8,128)(2,1)}, bf16[1,9,32,128]{3,2,1,0:T(8,128)(2,1)}) custom-call(bf16[12,625,625]{2,1,0:T(8,128)(2,1)} %block_ref.1, s32[1]{0:T(128)} %bitcast.where_ref, bf16[625,128]{1,0:T(8,128)(2,1)} %constant.18.clone.right_ref, bf16[80,625]{1,0:T(8,128)(2,1)} %constant.19.clone.left_ref, bf16[16,400]{1,0:T(8,128)(2,1)} %copy-done.8, ...), custom_call_target="tpu_custom_call" | custom-call | tf_op jit(solution)/shard_map/diag/pallas_call | solution.py:315
  21.0 2.5 %collective-permute-start.4 = (bf16[1,9,32,128]{3,2,1,0:T(8,128)(2,1)}, bf16[1,9,32,128]{3,2,1,0:T(8,128)(2,1)S(1)}, u32[]{:S(2)}, u32[]{:S(2)}) collective-permute-start(bf16[1,9,32,128]{3,2,1,0:T(8,128)(2,1)} %get-tuple-element.12), channel_id=1, source_target_pairs={{0,1},{1,0},{2,3},{3,2},{4,5},{5,4},{6,7},{7,6},{8,9},{9,8},{10,11... | collective-permute-start | bytes 221192 | tf_op jit(solution)/shard_map/ppermute | solution.py:336
  23.5 5.5 %collective-permute-start.3 = (bf16[1,9,32,128]{3,2,1,0:T(8,128)(2,1)}, bf16[1,9,32,128]{3,2,1,0:T(8,128)(2,1)S(1)}, u32[]{:S(2)}, u32[]{:S(2)}) collective-permute-start(bf16[1,9,32,128]{3,2,1,0:T(8,128)(2,1)} %get-tuple-element.11.refs_0_), channel_id=1, source_target_pairs={{0,6},{1,7},{2,2},{3,3},{4,4},{5,5},{6,0},{7,1},{8,14},{9,15},{10,... | collective-permute-start | bytes 221192 | tf_op jit(solution)/shard_map/ppermute | solution.py:346
  29.0 1.9 %collective-permute-start.2 = (bf16[1,9,32,128]{3,2,1,0:T(8,128)(2,1)}, bf16[1,9,32,128]{3,2,1,0:T(8,128)(2,1)S(1)}, u32[]{:S(2)}, u32[]{:S(2)}) collective-permute-start(bf16[1,9,32,128]{3,2,1,0:T(8,128)(2,1)} %get-tuple-element.11.refs_0_), channel_id=1, source_target_pairs={{0,4},{1,5},{2,2},{3,3},{4,0},{5,1},{6,6},{7,7},{8,12},{9,13},{10,... | collective-permute-start | bytes 221192 | tf_op jit(solution)/shard_map/ppermute | solution.py:346
  30.9 1.9 %collective-permute-start.1 = (bf16[1,9,32,128]{3,2,1,0:T(8,128)(2,1)}, bf16[1,9,32,128]{3,2,1,0:T(8,128)(2,1)S(1)}, u32[]{:S(2)}, u32[]{:S(2)}) collective-permute-start(bf16[1,9,32,128]{3,2,1,0:T(8,128)(2,1)} %get-tuple-element.11.refs_0_), channel_id=1, source_target_pairs={{0,2},{1,3},{2,0},{3,1},{4,4},{5,5},{6,6},{7,7},{8,10},{9,11},{10,... | collective-permute-start | bytes 221192 | tf_op jit(solution)/shard_map/ppermute | solution.py:346
  32.8 0.0 collective-permute-done.4.refs_4_
  32.9 1.9 %collective-permute-start.7 = (bf16[1,9,32,128]{3,2,1,0:T(8,128)(2,1)S(1)}, bf16[1,9,32,128]{3,2,1,0:T(8,128)(2,1)S(1)}, u32[]{:S(2)}, u32[]{:S(2)}) collective-permute-start(bf16[1,9,32,128]{3,2,1,0:T(8,128)(2,1)S(1)} %collective-permute-done.4.refs_4_), channel_id=1, source_target_pairs={{0,6},{1,7},{2,2},{3,3},{4,4},{5,5},{6,0},{7,1},{8,14},{9,15},{10,... | collective-permute-start | bytes 221192 | tf_op jit(solution)/shard_map/ppermute | solution.py:346
  34.8 3.2 %collective-permute-start.6 = (bf16[1,9,32,128]{3,2,1,0:T(8,128)(2,1)S(1)}, bf16[1,9,32,128]{3,2,1,0:T(8,128)(2,1)S(1)}, u32[]{:S(2)}, u32[]{:S(2)}) collective-permute-start(bf16[1,9,32,128]{3,2,1,0:T(8,128)(2,1)S(1)} %collective-permute-done.4.refs_4_), channel_id=1, source_target_pairs={{0,4},{1,5},{2,2},{3,3},{4,0},{5,1},{6,6},{7,7},{8,12},{9,13},{10,... | collective-permute-start | bytes 221192 | tf_op jit(solution)/shard_map/ppermute | solution.py:346
  38.0 0.0 collective-permute-done.3.refs_3_
  38.0 1.9 %collective-permute-start.5 = (bf16[1,9,32,128]{3,2,1,0:T(8,128)(2,1)S(1)}, bf16[1,9,32,128]{3,2,1,0:T(8,128)(2,1)S(1)}, u32[]{:S(2)}, u32[]{:S(2)}) collective-permute-start(bf16[1,9,32,128]{3,2,1,0:T(8,128)(2,1)S(1)} %collective-permute-done.4.refs_4_), channel_id=1, source_target_pairs={{0,2},{1,3},{2,0},{3,1},{4,4},{5,5},{6,6},{7,7},{8,10},{9,11},{10,... | collective-permute-start | bytes 221192 | tf_op jit(solution)/shard_map/ppermute | solution.py:346
  39.9 0.0 collective-permute-done.2.refs_2_
  39.9 0.0 collective-permute-done.1.refs_1_
  39.9 0.0 copy-start.4
  39.9 1.7 %collective-permute-done.7.refs_7_ = bf16[1,9,32,128]{3,2,1,0:T(8,128)(2,1)S(1)} collective-permute-done((bf16[1,9,32,128]{3,2,1,0:T(8,128)(2,1)S(1)}, bf16[1,9,32,128]{3,2,1,0:T(8,128)(2,1)S(1)}, u32[]{:S(2)}, u32[]{:S(2)}) %collective-permute-start.7) | collective-permute-done | bytes 73760 | tf_op jit(solution)/shard_map/ppermute | solution.py:346
  41.6 1.7 %collective-permute-done.6.refs_6_ = bf16[1,9,32,128]{3,2,1,0:T(8,128)(2,1)S(1)} collective-permute-done((bf16[1,9,32,128]{3,2,1,0:T(8,128)(2,1)S(1)}, bf16[1,9,32,128]{3,2,1,0:T(8,128)(2,1)S(1)}, u32[]{:S(2)}, u32[]{:S(2)}) %collective-permute-start.6) | collective-permute-done | bytes 73760 | tf_op jit(solution)/shard_map/ppermute | solution.py:346
  43.3 1.6 %collective-permute-done.5.refs_5_ = bf16[1,9,32,128]{3,2,1,0:T(8,128)(2,1)S(1)} collective-permute-done((bf16[1,9,32,128]{3,2,1,0:T(8,128)(2,1)S(1)}, bf16[1,9,32,128]{3,2,1,0:T(8,128)(2,1)S(1)}, u32[]{:S(2)}, u32[]{:S(2)}) %collective-permute-start.5) | collective-permute-done | bytes 73760 | tf_op jit(solution)/shard_map/ppermute | solution.py:346
  44.9 0.0 copy-done.3
  44.9 0.0 copy-done.4
  44.9 0.0 copy-done.5
  44.9 0.0 copy-done.6
  44.9 0.6 %copy-done.7 = bf16[1,9,32,128]{3,2,1,0:T(8,128)(2,1)} copy-done((bf16[1,9,32,128]{3,2,1,0:T(8,128)(2,1)}, bf16[1,9,32,128]{3,2,1,0:T(8,128)(2,1)S(1)}, u32[]{:S(2)}) %copy-start.7) | copy-done | bytes 73752
  45.5 6.1 %unpack.1 = bf16[7,72,1600]{2,1,0:T(8,128)(2,1)} custom-call(s32[1]{0:T(128)} %bitcast.where_ref, bf16[1,9,32,128]{3,2,1,0:T(8,128)(2,1)} %get-tuple-element.11.refs_0_, bf16[1,9,32,128]{3,2,1,0:T(8,128)(2,1)} %copy-done.4, bf16[1,9,32,128]{3,2,1,0:T(8,128)(2,1)} %copy-done.3, bf16[1,9,32,128]{3,2,1,0:T(8,128)(2,1)} %copy-done.2, ...), custom_call_target="tpu_custom_call" | custom-call | tf_op jit(solution)/shard_map/unpack/pallas_call | solution.py:275
  (10 shorter events, 0.0 us)
Async XLA Ops:
  1.2 4.6 %copy-start = (bf16[12,4,15625]{2,1,0:T(4,128)(2,1)S(1)}, bf16[12,4,15625]{2,1,0:T(4,128)(2,1)}, u32[]{:S(2)}) copy-start(bf16[12,4,15625]{2,1,0:T(4,128)(2,1)} %param.12) | copy-start | bytes 4500004
  5.3 5.7 %collective-permute-start = (bf16[16,400]{1,0:T(8,128)(2,1)}, bf16[16,400]{1,0:T(8,128)(2,1)S(1)}, u32[]{:S(2)}, u32[]{:S(2)}) collective-permute-start(bf16[16,400]{1,0:T(8,128)(2,1)} %get-tuple-element.9), channel_id=1, source_target_pairs={{0,8},{8,16},{16,24},{24,0},{1,9},{9,17},{17,25},{25,1},{2,10},{10... | collective-permute-start | bytes 38408 | tf_op jit(solution)/shard_map/ppermute | solution.py:304
  11.0 0.6 %copy-start.8 = (bf16[16,400]{1,0:T(8,128)(2,1)}, bf16[16,400]{1,0:T(8,128)(2,1)S(1)}, u32[]{:S(2)}) copy-start(bf16[16,400]{1,0:T(8,128)(2,1)S(1)} %collective-permute-done.minus_ref) | copy-start | bytes 38404
  21.0 11.8 %collective-permute-start.4 = (bf16[1,9,32,128]{3,2,1,0:T(8,128)(2,1)}, bf16[1,9,32,128]{3,2,1,0:T(8,128)(2,1)S(1)}, u32[]{:S(2)}, u32[]{:S(2)}) collective-permute-start(bf16[1,9,32,128]{3,2,1,0:T(8,128)(2,1)} %get-tuple-element.12), channel_id=1, source_target_pairs={{0,1},{1,0},{2,3},{3,2},{4,5},{5,4},{6,7},{7,6},{8,9},{9,8},{10,11... | collective-permute-start | bytes 221192 | tf_op jit(solution)/shard_map/ppermute | solution.py:336
  23.5 14.5 %collective-permute-start.3 = (bf16[1,9,32,128]{3,2,1,0:T(8,128)(2,1)}, bf16[1,9,32,128]{3,2,1,0:T(8,128)(2,1)S(1)}, u32[]{:S(2)}, u32[]{:S(2)}) collective-permute-start(bf16[1,9,32,128]{3,2,1,0:T(8,128)(2,1)} %get-tuple-element.11.refs_0_), channel_id=1, source_target_pairs={{0,6},{1,7},{2,2},{3,3},{4,4},{5,5},{6,0},{7,1},{8,14},{9,15},{10,... | collective-permute-start | bytes 221192 | tf_op jit(solution)/shard_map/ppermute | solution.py:346
  29.0 10.9 %collective-permute-start.2 = (bf16[1,9,32,128]{3,2,1,0:T(8,128)(2,1)}, bf16[1,9,32,128]{3,2,1,0:T(8,128)(2,1)S(1)}, u32[]{:S(2)}, u32[]{:S(2)}) collective-permute-start(bf16[1,9,32,128]{3,2,1,0:T(8,128)(2,1)} %get-tuple-element.11.refs_0_), channel_id=1, source_target_pairs={{0,4},{1,5},{2,2},{3,3},{4,0},{5,1},{6,6},{7,7},{8,12},{9,13},{10,... | collective-permute-start | bytes 221192 | tf_op jit(solution)/shard_map/ppermute | solution.py:346
  30.9 9.0 %collective-permute-start.1 = (bf16[1,9,32,128]{3,2,1,0:T(8,128)(2,1)}, bf16[1,9,32,128]{3,2,1,0:T(8,128)(2,1)S(1)}, u32[]{:S(2)}, u32[]{:S(2)}) collective-permute-start(bf16[1,9,32,128]{3,2,1,0:T(8,128)(2,1)} %get-tuple-element.11.refs_0_), channel_id=1, source_target_pairs={{0,2},{1,3},{2,0},{3,1},{4,4},{5,5},{6,6},{7,7},{8,10},{9,11},{10,... | collective-permute-start | bytes 221192 | tf_op jit(solution)/shard_map/ppermute | solution.py:346
  32.9 12.0 %copy-start.1 = (bf16[1,9,32,128]{3,2,1,0:T(8,128)(2,1)}, bf16[1,9,32,128]{3,2,1,0:T(8,128)(2,1)S(1)}, u32[]{:S(2)}) copy-start(bf16[1,9,32,128]{3,2,1,0:T(8,128)(2,1)S(1)} %collective-permute-done.4.refs_4_) | copy-start | bytes 221188
  32.9 8.8 %collective-permute-start.7 = (bf16[1,9,32,128]{3,2,1,0:T(8,128)(2,1)S(1)}, bf16[1,9,32,128]{3,2,1,0:T(8,128)(2,1)S(1)}, u32[]{:S(2)}, u32[]{:S(2)}) collective-permute-start(bf16[1,9,32,128]{3,2,1,0:T(8,128)(2,1)S(1)} %collective-permute-done.4.refs_4_), channel_id=1, source_target_pairs={{0,6},{1,7},{2,2},{3,3},{4,4},{5,5},{6,0},{7,1},{8,14},{9,15},{10,... | collective-permute-start | bytes 221192 | tf_op jit(solution)/shard_map/ppermute | solution.py:346
  34.8 8.5 %collective-permute-start.6 = (bf16[1,9,32,128]{3,2,1,0:T(8,128)(2,1)S(1)}, bf16[1,9,32,128]{3,2,1,0:T(8,128)(2,1)S(1)}, u32[]{:S(2)}, u32[]{:S(2)}) collective-permute-start(bf16[1,9,32,128]{3,2,1,0:T(8,128)(2,1)S(1)} %collective-permute-done.4.refs_4_), channel_id=1, source_target_pairs={{0,4},{1,5},{2,2},{3,3},{4,0},{5,1},{6,6},{7,7},{8,12},{9,13},{10,... | collective-permute-start | bytes 221192 | tf_op jit(solution)/shard_map/ppermute | solution.py:346
  38.0 6.9 %copy-start.2 = (bf16[1,9,32,128]{3,2,1,0:T(8,128)(2,1)}, bf16[1,9,32,128]{3,2,1,0:T(8,128)(2,1)S(1)}, u32[]{:S(2)}) copy-start(bf16[1,9,32,128]{3,2,1,0:T(8,128)(2,1)S(1)} %collective-permute-done.3.refs_3_) | copy-start | bytes 221188
  38.0 6.9 %collective-permute-start.5 = (bf16[1,9,32,128]{3,2,1,0:T(8,128)(2,1)S(1)}, bf16[1,9,32,128]{3,2,1,0:T(8,128)(2,1)S(1)}, u32[]{:S(2)}, u32[]{:S(2)}) collective-permute-start(bf16[1,9,32,128]{3,2,1,0:T(8,128)(2,1)S(1)} %collective-permute-done.4.refs_4_), channel_id=1, source_target_pairs={{0,2},{1,3},{2,0},{3,1},{4,4},{5,5},{6,6},{7,7},{8,10},{9,11},{10,... | collective-permute-start | bytes 221192 | tf_op jit(solution)/shard_map/ppermute | solution.py:346
  39.9 5.0 %copy-start.3 = (bf16[1,9,32,128]{3,2,1,0:T(8,128)(2,1)}, bf16[1,9,32,128]{3,2,1,0:T(8,128)(2,1)S(1)}, u32[]{:S(2)}) copy-start(bf16[1,9,32,128]{3,2,1,0:T(8,128)(2,1)S(1)} %collective-permute-done.2.refs_2_) | copy-start | bytes 221188
  39.9 4.9 %copy-start.4 = (bf16[1,9,32,128]{3,2,1,0:T(8,128)(2,1)}, bf16[1,9,32,128]{3,2,1,0:T(8,128)(2,1)S(1)}, u32[]{:S(2)}) copy-start(bf16[1,9,32,128]{3,2,1,0:T(8,128)(2,1)S(1)} %collective-permute-done.1.refs_1_) | copy-start | bytes 221188
  41.6 3.2 %copy-start.5 = (bf16[1,9,32,128]{3,2,1,0:T(8,128)(2,1)}, bf16[1,9,32,128]{3,2,1,0:T(8,128)(2,1)S(1)}, u32[]{:S(2)}) copy-start(bf16[1,9,32,128]{3,2,1,0:T(8,128)(2,1)S(1)} %collective-permute-done.7.refs_7_) | copy-start | bytes 221188
  43.3 1.6 %copy-start.6 = (bf16[1,9,32,128]{3,2,1,0:T(8,128)(2,1)}, bf16[1,9,32,128]{3,2,1,0:T(8,128)(2,1)S(1)}, u32[]{:S(2)}) copy-start(bf16[1,9,32,128]{3,2,1,0:T(8,128)(2,1)S(1)} %collective-permute-done.6.refs_6_) | copy-start | bytes 221188
  44.9 0.6 %copy-start.7 = (bf16[1,9,32,128]{3,2,1,0:T(8,128)(2,1)}, bf16[1,9,32,128]{3,2,1,0:T(8,128)(2,1)S(1)}, u32[]{:S(2)}) copy-start(bf16[1,9,32,128]{3,2,1,0:T(8,128)(2,1)S(1)} %collective-permute-done.5.refs_5_) | copy-start | bytes 221188

commit v2 on v0

--- a/solution.py
+++ b/solution.py
@@ -16,6 +16,8 @@
 LANES = 128
 F32 = jnp.float32
 BF16 = jnp.bfloat16
+VMEM = pl.BlockSpec(memory_space=pltpu.VMEM)
+SMALL = pl.BlockSpec(memory_space=pltpu.SMEM)
 
 
 def gll_points(degree):
@@ -125,31 +127,49 @@
     return out
 
 
-def face_kernel(x_ref, table_ref, out_ref, scratch, *, rows):
-    width = table_ref.shape[0]
-    parts = [x_ref[:, v * width : (v + 1) * width] for v in range(NV)]
-    y = jnp.dot(jnp.concatenate(parts, axis=0), table_ref[...], preferred_element_type=F32)
-    y = y[:, :LANES] + y[:, LANES:]
+def face_product(x, table, stacked, products):
+    width = table.shape[0]
+    count = x.shape[0]
+    pitch = stacked.shape[0] // NV
     for v in range(NV):
-        scratch[:, v * UNIT : (v + 1) * UNIT] = y[v * rows : (v + 1) * rows, :UNIT]
-    out_ref[...] = scratch[...].astype(BF16)
-
-
-def xface_kernel(x_ref, table_ref, turn_ref, orient_ref, plus_ref, sent_ref, scratch, *, elems):
-    width = table_ref.shape[0]
-    rows = 2 * elems
-    parts = [x_ref[:, v * width : (v + 1) * width] for v in range(NV)]
-    y = jnp.dot(jnp.concatenate(parts, axis=0), table_ref[...], preferred_element_type=F32)
-    y = (y[:, :LANES] + y[:, LANES:])[:, :UNIT].astype(BF16)
+        stacked[v * pitch : v * pitch + count, :] = x[:, v * width : (v + 1) * width]
+        if pitch > count:
+            stacked[v * pitch + count : (v + 1) * pitch, :] = jnp.zeros((pitch - count, width), BF16)
+    y = jnp.dot(stacked[...], table[...], preferred_element_type=F32)
+    products[...] = y[:, :LANES] + y[:, LANES:]
+
+
+def as_column(row, count):
+    shape = (count, row.shape[1])
+    diagonal = lax.broadcasted_iota(jnp.int32, shape, 0) == lax.broadcasted_iota(jnp.int32, shape, 1)
+    return jnp.sum(jnp.where(diagonal, row, 0), axis=1, keepdims=True)
+
+
+def placement(owner, me, owners_n, most):
+    elems = owner.shape[1]
+    shape = (elems, elems)
+    earlier = lax.broadcasted_iota(jnp.int32, shape, 0) < lax.broadcasted_iota(jnp.int32, shape, 1)
+    same = as_column(owner, elems) == owner
+    rank = jnp.sum(jnp.where(same & earlier, 1, 0), axis=0, keepdims=True)
+    dest = lax.rem(owner - lax.rem(me, owners_n) + owners_n, owners_n) * most + rank
+    slot = lax.broadcasted_iota(jnp.int32, (owners_n * most, elems), 0)
+    return jnp.where(slot == dest, 1.0, 0.0).astype(BF16)
+
+
+def xface_kernel(x_ref, table_ref, turn_ref, orient_ref, plus_ref, sent_ref, stacked, products, scratch):
+    face_product(x_ref, table_ref, stacked, products)
+    pitch = stacked.shape[0] // NV
+    elems = pitch // 2
+    orient = as_column(orient_ref[...], elems)
     for which, out_ref in enumerate((plus_ref, sent_ref)):
-        start = which * elems
-        mine = jnp.concatenate([y[v * rows + start : v * rows + start + elems] for v in range(NV)], axis=0)
+        units = [products[pl.ds(v * pitch + which, elems, stride=2), :] for v in range(NV)]
+        mine = jnp.concatenate(units, axis=0)[:, :UNIT].astype(BF16)
         turned = jnp.dot(mine, turn_ref[which], preferred_element_type=F32)
         for v in range(NV):
             piece = turned[v * elems : (v + 1) * elems]
             total = jnp.zeros((elems, LANES), F32)
             for o in range(4):
-                total = jnp.where(orient_ref[...] == o, piece[:, o * LANES : (o + 1) * LANES], total)
+                total = jnp.where(orient == o, piece[:, o * LANES : (o + 1) * LANES], total)
             scratch[:, v * UNIT : (v + 1) * UNIT] = total[:, :UNIT]
         out_ref[...] = scratch[...].astype(BF16)
 
@@ -165,38 +185,58 @@
     return g[:NCOARSE] + g[NCOARSE:] + pltpu.roll(g[:NCOARSE], half, 1)
 
 
-def diag_kernel(
-    block_ref, right_ref, left_ref, minus_ref, plus_ref, side_ref, placer_ref,
-    keep_ref, send_ref, coarse, rows, packed_scr, *, elems, pad,
+def main_kernel(
+    where_ref, diag_hbm, side_hbm, table_hbm, right_ref, left_ref, minus_ref, plus_ref, owner_ref,
+    keep_ref, send_ref, blocks, side, table, stacked, products, coarse, rows, packed_scr, sems, *, many, owners_n,
 ):
-    step = pl.program_id(0)
-    many = block_ref.shape[0]
-    for i in range(many):
-        g = coarse_block(block_ref[i], right_ref[...], left_ref[...])
-        coarse[pl.ds((step * many + i) * NCOARSE, NCOARSE), :] = g
-
-    @pl.when(step == 0)
-    def _():
-        rows[...] = jnp.zeros_like(rows)
-        rows[:, :FACE] = minus_ref[...].astype(F32)
-        rows[:, FACE : 2 * FACE] = plus_ref[...].astype(F32)
-        for f in range(NFACES - 2):
-            start = (2 + f) * FACE
-            rows[:, start : start + FACE] = side_ref[f * pad : (f + 1) * pad].astype(F32)
-
-    @pl.when(step == pl.num_programs(0) - 1)
-    def _():
-        for c in range(NCOARSE):
-            piece = coarse[pl.ds(c, elems, stride=NCOARSE), :]
-            start = DIAG_AT + c * NCOARSE
-            rows[:elems, start : start + NCOARSE] = piece[:, :NCOARSE]
-        slots = placer_ref.shape[0]
-        packed = jnp.dot(placer_ref[...], rows[...].astype(BF16), preferred_element_type=F32)
-        for j in range(ROW_TILES):
-            packed_scr[pl.ds(j, slots, stride=ROW_TILES), :] = packed[:, j * LANES : (j + 1) * LANES]
-        kept = keep_ref.shape[1] * ROW_TILES
-        keep_ref[...] = packed_scr[:kept].astype(BF16).reshape(keep_ref.shape)
-        send_ref[...] = packed_scr[kept:].astype(BF16).reshape(send_ref.shape)
+    elems = blocks.shape[0]
+    n_side = side.shape[0] // elems
+    side_copy = pltpu.make_async_copy(side_hbm, side, sems.at[elems])
+    table_copy = pltpu.make_async_copy(table_hbm, table, sems.at[elems + 1])
+
+    def block_copy(e):
+        return pltpu.make_async_copy(diag_hbm.at[e], blocks.at[e], sems.at[e])
+
+    side_copy.start()
+    table_copy.start()
+    for e in range(elems):
+        block_copy(e).start()
+    rows[...] = jnp.zeros_like(rows)
+    rows[:, :FACE] = minus_ref[...].astype(F32)
+    rows[:, FACE : 2 * FACE] = plus_ref[...].astype(F32)
+    side_copy.wait()
+    table_copy.wait()
+    face_product(side, table, stacked, products)
+    pitch = stacked.shape[0] // NV
+    for f in range(n_side):
+        for v in range(NV):
+            start = (2 + f) * FACE + v * UNIT
+            unit = products[pl.ds(v * pitch + f, elems, stride=n_side), :]
+            rows[:elems, start : start + UNIT] = unit[:, :UNIT]
+
+    def some_blocks(step, carry):
+        for i in range(many):
+            block_copy(step * many + i).wait()
+        for i in range(many):
+            e = step * many + i
+            g = coarse_block(blocks[e], right_ref[...], left_ref[...])
+            coarse[pl.ds(e * NCOARSE, NCOARSE), :] = g
+        return carry
+
+    lax.fori_loop(0, elems // many, some_blocks, 0)
+    for c in range(NCOARSE):
+        piece = coarse[pl.ds(c, elems, stride=NCOARSE), :]
+        start = DIAG_AT + c * NCOARSE
+        rows[:elems, start : start + NCOARSE] = piece[:, :NCOARSE]
+    most = keep_ref.shape[1]
+    slots = owners_n * most
+    placer = placement(owner_ref[...], where_ref[0], owners_n, most)
+    packed = jnp.dot(placer, rows[:elems].astype(BF16), preferred_element_type=F32)
+    for j in range(ROW_TILES):
+        packed_scr[pl.ds(j, slots, stride=ROW_TILES), :] = packed[:, j * LANES : (j + 1) * LANES]
+    kept = most * ROW_TILES
+    keep_ref[...] = packed_scr[:kept].astype(BF16).reshape(keep_ref.shape)
+    send_ref[...] = packed_scr[kept:].astype(BF16).reshape(send_ref.shape)
 
 
 def unpack_kernel(where_ref, *refs, owners_n, most):
@@ -256,57 +296,46 @@
     slab_size = lax.axis_size("slab")
     owners_n = grp_size // 4
     most = max(2, 3 * elems // (2 * owners_n))
-    me = lax.axis_index("grp")
+    where = lax.axis_index("grp").astype(jnp.int32)[None]
     table = jnp.asarray(face_table())
     right, left = (jnp.asarray(t) for t in diag_tables())
 
-    def by_face(array):
-        turned = jnp.transpose(array, (1, 0, 2))
-        turned = jnp.pad(turned, ((0, 0), (0, pad - elems), (0, 0)))
-        return turned.reshape(-1, length)
-
-    orient_col = jnp.pad(orient, (0, pad - elems))[:, None]
     sds = jax.ShapeDtypeStruct
+    width = table.shape[0]
     plus, sent = call(
-        functools.partial(xface_kernel, elems=pad),
+        xface_kernel,
         (sds((pad, FACE), BF16), sds((pad, FACE), BF16)),
-        [pltpu.VMEM((pad, FACE), F32)],
-        by_face(xface_jac), table, jnp.asarray(turn_tables()), orient_col, name="xface",
+        [
+            pltpu.VMEM((NV * 2 * pad, width), BF16),
+            pltpu.VMEM((NV * 2 * pad, LANES), F32),
+            pltpu.VMEM((pad, FACE), F32),
+        ],
+        xface_jac.reshape(2 * elems, length), table, jnp.asarray(turn_tables()), orient[None, :], name="xface",
     )
     minus = lax.ppermute(sent, "slab", [(i, (i + 1) % slab_size) for i in range(slab_size)])
-    side = call(
-        functools.partial(face_kernel, rows=4 * pad),
-        sds((4 * pad, FACE), BF16),
-        [pltpu.VMEM((4 * pad, FACE), F32)],
-        by_face(side_jac), table, name="side",
-    )
-    earlier = jnp.arange(elems)[None, :] < jnp.arange(elems)[:, None]
-    same = owner[:, None] == owner[None, :]
-    rank = jnp.sum((same & earlier).astype(jnp.int32), axis=1)
-    dest = (owner - me) % owners_n * most + rank
-    dest = jnp.pad(dest, (0, pad - elems), constant_values=-1)
-    placer = (jnp.arange(owners_n * most, dtype=jnp.int32)[:, None] == dest[None, :]).astype(BF16)
 
     many = max(n for n in range(1, 4) if elems % n == 0)
-    small = [right, left, minus, plus, side, placer]
+    n_side = side_jac.shape[1]
+    pitch = round_up(n_side * elems, 16)
     chunk = (most, ROW_TILES, LANES)
-    keep, send = pl.pallas_call(
-        functools.partial(diag_kernel, elems=elems, pad=pad),
-        grid=(elems // many,),
-        in_specs=[pl.BlockSpec((many, nf, nf), lambda e: (e, 0, 0))]
-        + [pl.BlockSpec(array.shape, lambda e: (0, 0)) for array in small],
-        out_specs=[
-            pl.BlockSpec((1,) + chunk, lambda e: (0, 0, 0, 0)),
-            pl.BlockSpec((owners_n - 1,) + chunk, lambda e: (0, 0, 0, 0)),
-        ],
-        out_shape=[sds((1,) + chunk, BF16), sds((owners_n - 1,) + chunk, BF16)],
-        scratch_shapes=[
+    keep, send = call(
+        functools.partial(main_kernel, many=many, owners_n=owners_n),
+        (sds((1,) + chunk, BF16), sds((owners_n - 1,) + chunk, BF16)),
+        [
+            pltpu.VMEM((elems, nf, nf), BF16),
+            pltpu.VMEM((n_side * elems, length), BF16),
+            pltpu.VMEM(table.shape, BF16),
+            pltpu.VMEM((NV * pitch, width), BF16),
+            pltpu.VMEM((NV * pitch, LANES), F32),
             pltpu.VMEM((elems * NCOARSE, LANES), F32),
             pltpu.VMEM((pad, ROW_TILES * LANES), F32),
             pltpu.VMEM((owners_n * most * ROW_TILES, LANES), F32),
+            pltpu.SemaphoreType.DMA((elems + 2,)),
         ],
-        name="diag",
-    )(diag_jac, *small)
+        where, diag_jac, side_jac.reshape(n_side * elems, length), table, right, left, minus, plus, owner[None, :],
+        in_specs=[SMALL] + [pl.BlockSpec(memory_space=pl.ANY)] * 3 + [VMEM] * 5,
+        name="main",
+    )
 
     groups = grp_size // owners_n
     arrived = []
@@ -329,8 +358,8 @@
         functools.partial(unpack_kernel, owners_n=owners_n, most=most),
         sds((NFACES + 1, slots, NCOARSE * NCOARSE), BF16),
         [pltpu.VMEM((slots * ROW_TILES, LANES), F32), pltpu.VMEM((slots, ROW_TILES * LANES), F32)],
-        me.astype(jnp.int32)[None], *sources, jnp.asarray(spread_tables()),
-        in_specs=[pl.BlockSpec(memory_space=pltpu.SMEM)] + [pl.BlockSpec(memory_space=pltpu.VMEM)] * (len(sources) + 1),
+        where, *sources, jnp.asarray(spread_tables()),
+        in_specs=[SMALL] + [VMEM] * (len(sources) + 1),
         name="unpack",
     )
     return jnp.transpose(rows, (1, 0, 2))

time: 46.5 us -> 44.6 us (0.959)
  waiting for transfers between devices: 7.88 us -> 9.68 us
  Pallas kernels: 20.1 us -> 18.5 us
  local copies, waits for them, and re-layouts: 6.5 us -> 5.36 us
  other arithmetic: 0.79 us -> 0 us
    pallas_call x1 -> x0, Pallas kernels: 9.37 us -> none  [shards(): pl.pallas_call(functools.partial(diag_kernel, elems=elems, pad=pad), grid...]
    pallas_call x3, Pallas kernels: 10.7 us -> 18.5 us  [call(): pl.pallas_call(kernel, out_shape=out_shape, scratch_shapes=scratch, **kwa...]
    reshape x0 -> x2, local copies, waits for them, and re-layouts: none -> 4.12 us  [the longest x1 2.55 us: shards(): xface_jac.reshape(2 * elems, length)]
    pad x3 -> x0, local copies, waits for them, and re-layouts: 2.52 us -> none  [the longest x2 2.52 us: by_face(): turned = jnp.pad(turned, ((0, 0), (0, pad - elems), (0, 0)))]
    ppermute x1, waiting for transfers between devices: 0.01 us -> 2 us  [shards(): lax.ppermute(sent, 'slab', [(i, (i + 1) % slab_size) for i in range(slab_...]
    unnamed x22 -> x18, local copies, waits for them, and re-layouts: 2.63 us -> 1.24 us
    broadcast_in_dim x2 -> x0, local copies, waits for them, and re-layouts: 1.35 us -> none  [shards(): orient_col = jnp.pad(orient, (0, pad - elems))[:, None]]
    convert_element_type x1 -> x0, other arithmetic: 0.6 us -> none  [shards(): (jnp.arange(owners_n * most, dtype=jnp.int32)[:, None] == dest[None, :])....]
  transfers between devices with their start and end apart: 8 -> 8, of which waited for: 5 -> 4; matrix products, arithmetic and copies ran while one was open for 5% -> 4% of each run, Pallas kernels for 8% -> 0%
where the time goes in v2:
time: 44.6 us; the launch traced here: 44.3 us
  Pallas kernels  18.5 us (41%)
  starting transfers between devices  10.6 us (24%)
  waiting for transfers between devices  9.68 us (22%)
  local copies, waits for them, and re-layouts  5.36 us (12%)
    pallas_call x3, Pallas kernels, call(): pl.pallas_call(kernel, out_shape=out_shape, scratch_shapes=scratch, **kwa...  18.5 us
    ppermute x6, starting transfers between devices, to_owners(): lax.ppermute(array, 'grp', [(a * owners_n + o, o) for o in range(owners_n)])  7.73 us
    ppermute x6, waiting for transfers between devices, to_owners(): lax.ppermute(array, 'grp', [(a * owners_n + o, o) for o in range(owners_n)])  7.68 us
    reshape x1, local copies, waits for them, and re-layouts, shards(): xface_jac.reshape(2 * elems, length)  2.55 us
    ppermute x1, starting transfers between devices, shards(): arrived.append(lax.ppermute(send[j - 1:j], 'grp', pairs))  2.34 us
    ppermute x1, waiting for transfers between devices, shards(): lax.ppermute(sent, 'slab', [(i, (i + 1) % slab_size) for i in range(slab_...  2 us
    reshape x1, local copies, waits for them, and re-layouts, shards(): side_jac.reshape(n_side * elems, length)  1.57 us
    unnamed x18, local copies, waits for them, and re-layouts  1.24 us
  transfers between devices with their start and end apart: 8, of which 4 were waited for; matrix products, arithmetic and copies ran while one was open for 4% of the time, Pallas kernels for 0%

profile of v2, /device:TPU:0, one launch (start us, length us, event | category | flops | bytes accessed | tf_op | source)
XLA Modules:
  0.0 44.3 jit_solution(17747082639111981509)
XLA Ops:
  0.0 2.6 %reshape.7.x_ref = bf16[24,15625]{1,0:T(8,128)(2,1)} reshape(bf16[12,2,15625]{2,1,0:T(2,128)(2,1)} %param.11) | data formatting | bytes 1500000 | tf_op jit(solution)/shard_map/reshape | solution.py:313
  2.6 3.1 %xface.1 = (bf16[16,400]{1,0:T(8,128)(2,1)}, bf16[16,400]{1,0:T(8,128)(2,1)}) custom-call(bf16[24,15625]{1,0:T(8,128)(2,1)} %reshape.7.x_ref, bf16[3125,256]{1,0:T(8,128)(2,1)} %constant.14.clone.table_ref.table_hbm, bf16[2,80,512]{2,1,0:T(8,128)(2,1)} %constant.17.clone.turn_ref, s32[1,12]{1,0:T(1,128)} %bitcast.4), custom_call_target="tpu_custom_call" | custom-call | tf_op jit(solution)/shard_map/xface/pallas_call | solution.py:287
  5.7 0.5 %collective-permute-start = (bf16[16,400]{1,0:T(8,128)(2,1)}, bf16[16,400]{1,0:T(8,128)(2,1)S(1)}, u32[]{:S(2)}, u32[]{:S(2)}) collective-permute-start(bf16[16,400]{1,0:T(8,128)(2,1)} %get-tuple-element.9), channel_id=1, source_target_pairs={{0,8},{8,16},{16,24},{24,0},{1,9},{9,17},{17,25},{25,1},{2,10},{10... | collective-permute-start | bytes 38408 | tf_op jit(solution)/shard_map/ppermute | solution.py:315
  6.2 0.0 copy-done
  6.2 1.6 %reshape.6.side_hbm = bf16[48,15625]{1,0:T(8,128)(2,1)} reshape(bf16[12,4,15625]{2,1,0:T(4,128)(2,1)S(1)} %copy-done) | data formatting | bytes 3000000 | tf_op jit(solution)/shard_map/reshape | solution.py:335
  7.8 2.0 %collective-permute-done.minus_ref = bf16[16,400]{1,0:T(8,128)(2,1)S(1)} collective-permute-done((bf16[16,400]{1,0:T(8,128)(2,1)}, bf16[16,400]{1,0:T(8,128)(2,1)S(1)}, u32[]{:S(2)}, u32[]{:S(2)}) %collective-permute-start) | collective-permute-done | bytes 12832 | tf_op jit(solution)/shard_map/ppermute | solution.py:315
  9.8 0.6 %copy-done.8 = bf16[16,400]{1,0:T(8,128)(2,1)} copy-done((bf16[16,400]{1,0:T(8,128)(2,1)}, bf16[16,400]{1,0:T(8,128)(2,1)S(1)}, u32[]{:S(2)}) %copy-start.8) | copy-done | bytes 12824
  10.3 11.2 %main.1 = (bf16[1,9,32,128]{3,2,1,0:T(8,128)(2,1)}, bf16[1,9,32,128]{3,2,1,0:T(8,128)(2,1)}) custom-call(s32[1]{0:T(128)} %bitcast.where_ref, bf16[12,625,625]{2,1,0:T(8,128)(2,1)} %diag_hbm.1, bf16[48,15625]{1,0:T(8,128)(2,1)} %reshape.6.side_hbm, bf16[3125,256]{1,0:T(8,128)(2,1)} %constant.14.clone.table_ref.table_hbm, ...), custom_call_target="tpu_custom_call" | custom-call | tf_op jit(solution)/shard_map/main/pallas_call | solution.py:287
  21.6 2.3 %collective-permute-start.4 = (bf16[1,9,32,128]{3,2,1,0:T(8,128)(2,1)}, bf16[1,9,32,128]{3,2,1,0:T(8,128)(2,1)S(1)}, u32[]{:S(2)}, u32[]{:S(2)}) collective-permute-start(bf16[1,9,32,128]{3,2,1,0:T(8,128)(2,1)} %get-tuple-element.12), channel_id=1, source_target_pairs={{0,1},{1,0},{2,3},{3,2},{4,5},{5,4},{6,7},{7,6},{8,9},{9,8},{10,11... | collective-permute-start | bytes 221192 | tf_op jit(solution)/shard_map/ppermute | solution.py:344
  23.9 1.3 %collective-permute-start.3 = (bf16[1,9,32,128]{3,2,1,0:T(8,128)(2,1)}, bf16[1,9,32,128]{3,2,1,0:T(8,128)(2,1)S(1)}, u32[]{:S(2)}, u32[]{:S(2)}) collective-permute-start(bf16[1,9,32,128]{3,2,1,0:T(8,128)(2,1)} %get-tuple-element.11.refs_0_), channel_id=1, source_target_pairs={{6,0},{7,1},{14,8},{15,9},{22,16},{23,17},{30,24},{31,25}} | collective-permute-start | bytes 221192 | tf_op jit(solution)/shard_map/ppermute | solution.py:349
  25.2 1.3 %collective-permute-start.2 = (bf16[1,9,32,128]{3,2,1,0:T(8,128)(2,1)}, bf16[1,9,32,128]{3,2,1,0:T(8,128)(2,1)S(1)}, u32[]{:S(2)}, u32[]{:S(2)}) collective-permute-start(bf16[1,9,32,128]{3,2,1,0:T(8,128)(2,1)} %get-tuple-element.11.refs_0_), channel_id=1, source_target_pairs={{4,0},{5,1},{12,8},{13,9},{20,16},{21,17},{28,24},{29,25}} | collective-permute-start | bytes 221192 | tf_op jit(solution)/shard_map/ppermute | solution.py:349
  26.5 1.3 %collective-permute-start.1 = (bf16[1,9,32,128]{3,2,1,0:T(8,128)(2,1)}, bf16[1,9,32,128]{3,2,1,0:T(8,128)(2,1)S(1)}, u32[]{:S(2)}, u32[]{:S(2)}) collective-permute-start(bf16[1,9,32,128]{3,2,1,0:T(8,128)(2,1)} %get-tuple-element.11.refs_0_), channel_id=1, source_target_pairs={{2,0},{3,1},{10,8},{11,9},{18,16},{19,17},{26,24},{27,25}} | collective-permute-start | bytes 221192 | tf_op jit(solution)/shard_map/ppermute | solution.py:349
  27.8 0.0 collective-permute-done.4.refs_4_
  27.8 0.0 copy-start.1
  27.9 1.3 %collective-permute-start.7 = (bf16[1,9,32,128]{3,2,1,0:T(8,128)(2,1)S(1)}, bf16[1,9,32,128]{3,2,1,0:T(8,128)(2,1)S(1)}, u32[]{:S(2)}, u32[]{:S(2)}) collective-permute-start(bf16[1,9,32,128]{3,2,1,0:T(8,128)(2,1)S(1)} %collective-permute-done.4.refs_4_), channel_id=1, source_target_pairs={{6,0},{7,1},{14,8},{15,9},{22,16},{23,17},{30,24},{31,25}} | collective-permute-start | bytes 221192 | tf_op jit(solution)/shard_map/ppermute | solution.py:349
  29.2 1.3 %collective-permute-start.6 = (bf16[1,9,32,128]{3,2,1,0:T(8,128)(2,1)S(1)}, bf16[1,9,32,128]{3,2,1,0:T(8,128)(2,1)S(1)}, u32[]{:S(2)}, u32[]{:S(2)}) collective-permute-start(bf16[1,9,32,128]{3,2,1,0:T(8,128)(2,1)S(1)} %collective-permute-done.4.refs_4_), channel_id=1, source_target_pairs={{4,0},{5,1},{12,8},{13,9},{20,16},{21,17},{28,24},{29,25}} | collective-permute-start | bytes 221192 | tf_op jit(solution)/shard_map/ppermute | solution.py:349
  30.5 1.9 %collective-permute-done.3.refs_3_ = bf16[1,9,32,128]{3,2,1,0:T(8,128)(2,1)S(1)} collective-permute-done((bf16[1,9,32,128]{3,2,1,0:T(8,128)(2,1)}, bf16[1,9,32,128]{3,2,1,0:T(8,128)(2,1)S(1)}, u32[]{:S(2)}, u32[]{:S(2)}) %collective-permute-start.3) | collective-permute-done | bytes 73760 | tf_op jit(solution)/shard_map/ppermute | solution.py:349
  32.4 1.3 %collective-permute-start.5 = (bf16[1,9,32,128]{3,2,1,0:T(8,128)(2,1)S(1)}, bf16[1,9,32,128]{3,2,1,0:T(8,128)(2,1)S(1)}, u32[]{:S(2)}, u32[]{:S(2)}) collective-permute-start(bf16[1,9,32,128]{3,2,1,0:T(8,128)(2,1)S(1)} %collective-permute-done.4.refs_4_), channel_id=1, source_target_pairs={{2,0},{3,1},{10,8},{11,9},{18,16},{19,17},{26,24},{27,25}} | collective-permute-start | bytes 221192 | tf_op jit(solution)/shard_map/ppermute | solution.py:349
  33.7 0.0 collective-permute-done.2.refs_2_
  33.7 0.0 copy-start.3
  33.7 4.3 %collective-permute-done.1.refs_1_ = bf16[1,9,32,128]{3,2,1,0:T(8,128)(2,1)S(1)} collective-permute-done((bf16[1,9,32,128]{3,2,1,0:T(8,128)(2,1)}, bf16[1,9,32,128]{3,2,1,0:T(8,128)(2,1)S(1)}, u32[]{:S(2)}, u32[]{:S(2)}) %collective-permute-start.1) | collective-permute-done | bytes 73760 | tf_op jit(solution)/shard_map/ppermute | solution.py:349
  38.0 0.0 collective-permute-done.7.refs_7_
  38.0 0.0 collective-permute-done.6.refs_6_
  38.0 0.0 copy-start.6
  38.0 1.5 %collective-permute-done.5.refs_5_ = bf16[1,9,32,128]{3,2,1,0:T(8,128)(2,1)S(1)} collective-permute-done((bf16[1,9,32,128]{3,2,1,0:T(8,128)(2,1)S(1)}, bf16[1,9,32,128]{3,2,1,0:T(8,128)(2,1)S(1)}, u32[]{:S(2)}, u32[]{:S(2)}) %collective-permute-start.5) | collective-permute-done | bytes 73760 | tf_op jit(solution)/shard_map/ppermute | solution.py:349
  39.5 0.0 copy-done.1
  39.5 0.0 copy-done.4
  39.5 0.0 copy-done.5
  39.5 0.0 copy-done.6
  39.5 0.0 copy-start.7
  39.5 0.6 %copy-done.7 = bf16[1,9,32,128]{3,2,1,0:T(8,128)(2,1)} copy-done((bf16[1,9,32,128]{3,2,1,0:T(8,128)(2,1)}, bf16[1,9,32,128]{3,2,1,0:T(8,128)(2,1)S(1)}, u32[]{:S(2)}) %copy-start.7) | copy-done | bytes 73752
  40.1 4.1 %unpack.1 = bf16[7,72,1600]{2,1,0:T(8,128)(2,1)} custom-call(s32[1]{0:T(128)} %bitcast.where_ref, bf16[1,9,32,128]{3,2,1,0:T(8,128)(2,1)} %get-tuple-element.11.refs_0_, bf16[1,9,32,128]{3,2,1,0:T(8,128)(2,1)} %copy-done.4, bf16[1,9,32,128]{3,2,1,0:T(8,128)(2,1)} %copy-done.3, bf16[1,9,32,128]{3,2,1,0:T(8,128)(2,1)} %copy-done.2, ...), custom_call_target="tpu_custom_call" | custom-call | tf_op jit(solution)/shard_map/unpack/pallas_call | solution.py:287
  (7 shorter events, 0.0 us)
Async XLA Ops:
  2.6 3.6 %copy-start = (bf16[12,4,15625]{2,1,0:T(4,128)(2,1)S(1)}, bf16[12,4,15625]{2,1,0:T(4,128)(2,1)}, u32[]{:S(2)}) copy-start(bf16[12,4,15625]{2,1,0:T(4,128)(2,1)} %param.12) | copy-start | bytes 4500004
  5.7 4.1 %collective-permute-start = (bf16[16,400]{1,0:T(8,128)(2,1)}, bf16[16,400]{1,0:T(8,128)(2,1)S(1)}, u32[]{:S(2)}, u32[]{:S(2)}) collective-permute-start(bf16[16,400]{1,0:T(8,128)(2,1)} %get-tuple-element.9), channel_id=1, source_target_pairs={{0,8},{8,16},{16,24},{24,0},{1,9},{9,17},{17,25},{25,1},{2,10},{10... | collective-permute-start | bytes 38408 | tf_op jit(solution)/shard_map/ppermute | solution.py:315
  9.8 0.6 %copy-start.8 = (bf16[16,400]{1,0:T(8,128)(2,1)}, bf16[16,400]{1,0:T(8,128)(2,1)S(1)}, u32[]{:S(2)}) copy-start(bf16[16,400]{1,0:T(8,128)(2,1)S(1)} %collective-permute-done.minus_ref) | copy-start | bytes 38404
  21.6 6.2 %collective-permute-start.4 = (bf16[1,9,32,128]{3,2,1,0:T(8,128)(2,1)}, bf16[1,9,32,128]{3,2,1,0:T(8,128)(2,1)S(1)}, u32[]{:S(2)}, u32[]{:S(2)}) collective-permute-start(bf16[1,9,32,128]{3,2,1,0:T(8,128)(2,1)} %get-tuple-element.12), channel_id=1, source_target_pairs={{0,1},{1,0},{2,3},{3,2},{4,5},{5,4},{6,7},{7,6},{8,9},{9,8},{10,11... | collective-permute-start | bytes 221192 | tf_op jit(solution)/shard_map/ppermute | solution.py:344
  23.9 8.4 %collective-permute-start.3 = (bf16[1,9,32,128]{3,2,1,0:T(8,128)(2,1)}, bf16[1,9,32,128]{3,2,1,0:T(8,128)(2,1)S(1)}, u32[]{:S(2)}, u32[]{:S(2)}) collective-permute-start(bf16[1,9,32,128]{3,2,1,0:T(8,128)(2,1)} %get-tuple-element.11.refs_0_), channel_id=1, source_target_pairs={{6,0},{7,1},{14,8},{15,9},{22,16},{23,17},{30,24},{31,25}} | collective-permute-start | bytes 221192 | tf_op jit(solution)/shard_map/ppermute | solution.py:349
  25.2 8.4 %collective-permute-start.2 = (bf16[1,9,32,128]{3,2,1,0:T(8,128)(2,1)}, bf16[1,9,32,128]{3,2,1,0:T(8,128)(2,1)S(1)}, u32[]{:S(2)}, u32[]{:S(2)}) collective-permute-start(bf16[1,9,32,128]{3,2,1,0:T(8,128)(2,1)} %get-tuple-element.11.refs_0_), channel_id=1, source_target_pairs={{4,0},{5,1},{12,8},{13,9},{20,16},{21,17},{28,24},{29,25}} | collective-permute-start | bytes 221192 | tf_op jit(solution)/shard_map/ppermute | solution.py:349
  26.5 11.4 %collective-permute-start.1 = (bf16[1,9,32,128]{3,2,1,0:T(8,128)(2,1)}, bf16[1,9,32,128]{3,2,1,0:T(8,128)(2,1)S(1)}, u32[]{:S(2)}, u32[]{:S(2)}) collective-permute-start(bf16[1,9,32,128]{3,2,1,0:T(8,128)(2,1)} %get-tuple-element.11.refs_0_), channel_id=1, source_target_pairs={{2,0},{3,1},{10,8},{11,9},{18,16},{19,17},{26,24},{27,25}} | collective-permute-start | bytes 221192 | tf_op jit(solution)/shard_map/ppermute | solution.py:349
  27.8 11.6 %copy-start.1 = (bf16[1,9,32,128]{3,2,1,0:T(8,128)(2,1)}, bf16[1,9,32,128]{3,2,1,0:T(8,128)(2,1)S(1)}, u32[]{:S(2)}) copy-start(bf16[1,9,32,128]{3,2,1,0:T(8,128)(2,1)S(1)} %collective-permute-done.4.refs_4_) | copy-start | bytes 221188
  27.9 10.1 %collective-permute-start.7 = (bf16[1,9,32,128]{3,2,1,0:T(8,128)(2,1)S(1)}, bf16[1,9,32,128]{3,2,1,0:T(8,128)(2,1)S(1)}, u32[]{:S(2)}, u32[]{:S(2)}) collective-permute-start(bf16[1,9,32,128]{3,2,1,0:T(8,128)(2,1)S(1)} %collective-permute-done.4.refs_4_), channel_id=1, source_target_pairs={{6,0},{7,1},{14,8},{15,9},{22,16},{23,17},{30,24},{31,25}} | collective-permute-start | bytes 221192 | tf_op jit(solution)/shard_map/ppermute | solution.py:349
  29.2 8.8 %collective-permute-start.6 = (bf16[1,9,32,128]{3,2,1,0:T(8,128)(2,1)S(1)}, bf16[1,9,32,128]{3,2,1,0:T(8,128)(2,1)S(1)}, u32[]{:S(2)}, u32[]{:S(2)}) collective-permute-start(bf16[1,9,32,128]{3,2,1,0:T(8,128)(2,1)S(1)} %collective-permute-done.4.refs_4_), channel_id=1, source_target_pairs={{4,0},{5,1},{12,8},{13,9},{20,16},{21,17},{28,24},{29,25}} | collective-permute-start | bytes 221192 | tf_op jit(solution)/shard_map/ppermute | solution.py:349
  32.4 7.1 %copy-start.2 = (bf16[1,9,32,128]{3,2,1,0:T(8,128)(2,1)}, bf16[1,9,32,128]{3,2,1,0:T(8,128)(2,1)S(1)}, u32[]{:S(2)}) copy-start(bf16[1,9,32,128]{3,2,1,0:T(8,128)(2,1)S(1)} %collective-permute-done.3.refs_3_) | copy-start | bytes 221188
  32.4 7.1 %collective-permute-start.5 = (bf16[1,9,32,128]{3,2,1,0:T(8,128)(2,1)S(1)}, bf16[1,9,32,128]{3,2,1,0:T(8,128)(2,1)S(1)}, u32[]{:S(2)}, u32[]{:S(2)}) collective-permute-start(bf16[1,9,32,128]{3,2,1,0:T(8,128)(2,1)S(1)} %collective-permute-done.4.refs_4_), channel_id=1, source_target_pairs={{2,0},{3,1},{10,8},{11,9},{18,16},{19,17},{26,24},{27,25}} | collective-permute-start | bytes 221192 | tf_op jit(solution)/shard_map/ppermute | solution.py:349
  33.7 5.8 %copy-start.3 = (bf16[1,9,32,128]{3,2,1,0:T(8,128)(2,1)}, bf16[1,9,32,128]{3,2,1,0:T(8,128)(2,1)S(1)}, u32[]{:S(2)}) copy-start(bf16[1,9,32,128]{3,2,1,0:T(8,128)(2,1)S(1)} %collective-permute-done.2.refs_2_) | copy-start | bytes 221188
  38.0 1.5 %copy-start.4 = (bf16[1,9,32,128]{3,2,1,0:T(8,128)(2,1)}, bf16[1,9,32,128]{3,2,1,0:T(8,128)(2,1)S(1)}, u32[]{:S(2)}) copy-start(bf16[1,9,32,128]{3,2,1,0:T(8,128)(2,1)S(1)} %collective-permute-done.1.refs_1_) | copy-start | bytes 221188
  38.0 1.5 %copy-start.5 = (bf16[1,9,32,128]{3,2,1,0:T(8,128)(2,1)}, bf16[1,9,32,128]{3,2,1,0:T(8,128)(2,1)S(1)}, u32[]{:S(2)}) copy-start(bf16[1,9,32,128]{3,2,1,0:T(8,128)(2,1)S(1)} %collective-permute-done.7.refs_7_) | copy-start | bytes 221188
  38.0 1.5 %copy-start.6 = (bf16[1,9,32,128]{3,2,1,0:T(8,128)(2,1)}, bf16[1,9,32,128]{3,2,1,0:T(8,128)(2,1)S(1)}, u32[]{:S(2)}) copy-start(bf16[1,9,32,128]{3,2,1,0:T(8,128)(2,1)S(1)} %collective-permute-done.6.refs_6_) | copy-start | bytes 221188
  39.5 0.6 %copy-start.7 = (bf16[1,9,32,128]{3,2,1,0:T(8,128)(2,1)}, bf16[1,9,32,128]{3,2,1,0:T(8,128)(2,1)S(1)}, u32[]{:S(2)}) copy-start(bf16[1,9,32,128]{3,2,1,0:T(8,128)(2,1)S(1)} %collective-permute-done.5.refs_5_) | copy-start | bytes 221188

commit v3 on v2

--- a/solution.py
+++ b/solution.py
@@ -127,14 +127,14 @@
     return out
 
 
-def face_product(x, table, stacked, products):
+def face_product(pieces, pitch, table, stacked, products):
     width = table.shape[0]
-    count = x.shape[0]
-    pitch = stacked.shape[0] // NV
+    if sum(x.shape[0] for _, x in pieces) < pitch:
+        stacked[...] = jnp.zeros_like(stacked)
     for v in range(NV):
-        stacked[v * pitch : v * pitch + count, :] = x[:, v * width : (v + 1) * width]
-        if pitch > count:
-            stacked[v * pitch + count : (v + 1) * pitch, :] = jnp.zeros((pitch - count, width), BF16)
+        for start, x in pieces:
+            at = v * pitch + start
+            stacked[at : at + x.shape[0], :] = x[:, v * width : (v + 1) * width]
     y = jnp.dot(stacked[...], table[...], preferred_element_type=F32)
     products[...] = y[:, :LANES] + y[:, LANES:]
 
@@ -157,12 +157,13 @@
 
 
 def xface_kernel(x_ref, table_ref, turn_ref, orient_ref, plus_ref, sent_ref, stacked, products, scratch):
-    face_product(x_ref, table_ref, stacked, products)
     pitch = stacked.shape[0] // NV
     elems = pitch // 2
+    face_product([(f * elems, x_ref.at[f]) for f in range(2)], pitch, table_ref, stacked, products)
     orient = as_column(orient_ref[...], elems)
     for which, out_ref in enumerate((plus_ref, sent_ref)):
-        units = [products[pl.ds(v * pitch + which, elems, stride=2), :] for v in range(NV)]
+        starts = [v * pitch + which * elems for v in range(NV)]
+        units = [products[s : s + elems, :] for s in starts]
         mine = jnp.concatenate(units, axis=0)[:, :UNIT].astype(BF16)
         turned = jnp.dot(mine, turn_ref[which], preferred_element_type=F32)
         for v in range(NV):
@@ -197,17 +198,27 @@
     def block_copy(e):
         return pltpu.make_async_copy(diag_hbm.at[e], blocks.at[e], sems.at[e])
 
+    for e in range(many):
+        block_copy(e).start()
     side_copy.start()
     table_copy.start()
-    for e in range(elems):
+    for e in range(many, elems):
         block_copy(e).start()
     rows[...] = jnp.zeros_like(rows)
     rows[:, :FACE] = minus_ref[...].astype(F32)
     rows[:, FACE : 2 * FACE] = plus_ref[...].astype(F32)
+
+    def coarse_at(e):
+        g = coarse_block(blocks[e], right_ref[...], left_ref[...])
+        coarse[pl.ds(e * NCOARSE, NCOARSE), :] = g
+
+    for e in range(many):
+        block_copy(e).wait()
+        coarse_at(e)
     side_copy.wait()
     table_copy.wait()
-    face_product(side, table, stacked, products)
     pitch = stacked.shape[0] // NV
+    face_product([(0, side)], pitch, table, stacked, products)
     for f in range(n_side):
         for v in range(NV):
             start = (2 + f) * FACE + v * UNIT
@@ -218,12 +229,10 @@
         for i in range(many):
             block_copy(step * many + i).wait()
         for i in range(many):
-            e = step * many + i
-            g = coarse_block(blocks[e], right_ref[...], left_ref[...])
-            coarse[pl.ds(e * NCOARSE, NCOARSE), :] = g
+            coarse_at(step * many + i)
         return carry
 
-    lax.fori_loop(0, elems // many, some_blocks, 0)
+    lax.fori_loop(1, elems // many, some_blocks, 0)
     for c in range(NCOARSE):
         piece = coarse[pl.ds(c, elems, stride=NCOARSE), :]
         start = DIAG_AT + c * NCOARSE
@@ -240,15 +249,22 @@
 
 
 def unpack_kernel(where_ref, *refs, owners_n, most):
-    spread_ref, out_ref, tiles, flat = refs[-4:]
-    kept = refs[: (len(refs) - 4) // 2]
-    others = refs[(len(refs) - 4) // 2 : -4]
-    slots = out_ref.shape[1]
+    spread_ref, out_hbm, tiles, flat, out, sems = refs[-6:]
+    kept = refs[: (len(refs) - 6) // 2]
+    others = refs[(len(refs) - 6) // 2 : -6]
+    slots = out.shape[1]
     me = where_ref[0]
+    width = NCOARSE * NCOARSE
+    half = LEFT_TILES * LANES
+
+    def copy_out(block):
+        return pltpu.make_async_copy(out.at[block], out_hbm.at[block], sems.at[block])
 
     @pl.when(me >= owners_n)
     def _():
-        out_ref[...] = jnp.zeros_like(out_ref)
+        for block in range(NFACES + 1):
+            out[block] = jnp.zeros(out.shape[1:], BF16)
+            copy_out(block).start()
 
     @pl.when(me < owners_n)
     def _():
@@ -260,9 +276,8 @@
                 tiles[pl.ds(source * step, step), :] = chunk.astype(F32).reshape(step, LANES)
         for j in range(ROW_TILES):
             flat[:, j * LANES : (j + 1) * LANES] = tiles[pl.ds(j, slots, stride=ROW_TILES), :]
-        width = NCOARSE * NCOARSE
-        out_ref[0] = flat[:, DIAG_AT : DIAG_AT + width].astype(BF16)
-        half = LEFT_TILES * LANES
+        out[0] = flat[:, DIAG_AT : DIAG_AT + width].astype(BF16)
+        copy_out(0).start()
         for f in range(NFACES):
             sums = {}
             for parity in range(2):
@@ -280,7 +295,11 @@
                         sums[tile] = sums[tile] + value if tile in sums else value
             for tile, value in sums.items():
                 cut = min(LANES, width - tile * LANES)
-                out_ref[f + 1, :, tile * LANES : tile * LANES + cut] = value[:, :cut].astype(BF16)
+                out[f + 1, :, tile * LANES : tile * LANES + cut] = value[:, :cut].astype(BF16)
+            copy_out(f + 1).start()
+
+    for block in range(NFACES + 1):
+        copy_out(block).wait()
 
 
 def call(kernel, out_shape, scratch, *args, **kwargs):
@@ -310,7 +329,7 @@
             pltpu.VMEM((NV * 2 * pad, LANES), F32),
             pltpu.VMEM((pad, FACE), F32),
         ],
-        xface_jac.reshape(2 * elems, length), table, jnp.asarray(turn_tables()), orient[None, :], name="xface",
+        jnp.transpose(xface_jac, (1, 0, 2)), table, jnp.asarray(turn_tables()), orient[None, :], name="xface",
     )
     minus = lax.ppermute(sent, "slab", [(i, (i + 1) % slab_size) for i in range(slab_size)])
 
@@ -357,9 +376,15 @@
     rows = call(
         functools.partial(unpack_kernel, owners_n=owners_n, most=most),
         sds((NFACES + 1, slots, NCOARSE * NCOARSE), BF16),
-        [pltpu.VMEM((slots * ROW_TILES, LANES), F32), pltpu.VMEM((slots, ROW_TILES * LANES), F32)],
+        [
+            pltpu.VMEM((slots * ROW_TILES, LANES), F32),
+            pltpu.VMEM((slots, ROW_TILES * LANES), F32),
+            pltpu.VMEM((NFACES + 1, slots, NCOARSE * NCOARSE), BF16),
+            pltpu.SemaphoreType.DMA((NFACES + 1,)),
+        ],
         where, *sources, jnp.asarray(spread_tables()),
         in_specs=[SMALL] + [VMEM] * (len(sources) + 1),
+        out_specs=pl.BlockSpec(memory_space=pl.ANY),
         name="unpack",
     )
     return jnp.transpose(rows, (1, 0, 2))

time: 44.6 us -> 44.2 us (level)
    reshape x1 -> x0, local copies, waits for them, and re-layouts: 2.55 us -> none  [shards(): xface_jac.reshape(2 * elems, length)]
    unnamed x18 -> x19, local copies, waits for them, and re-layouts: 1.24 us -> 3.41 us
where the time goes in v3:
time: 44.2 us; the launch traced here: 43.9 us
  Pallas kernels  18.5 us (42%)
  starting transfers between devices  10.6 us (24%)
  waiting for transfers between devices  9.69 us (22%)
  local copies, waits for them, and re-layouts  4.98 us (11%)
    pallas_call x3, Pallas kernels, call(): pl.pallas_call(kernel, out_shape=out_shape, scratch_shapes=scratch, **kwa...  18.5 us
    ppermute x6, starting transfers between devices, to_owners(): lax.ppermute(array, 'grp', [(a * owners_n + o, o) for o in range(owners_n)])  7.73 us
    ppermute x6, waiting for transfers between devices, to_owners(): lax.ppermute(array, 'grp', [(a * owners_n + o, o) for o in range(owners_n)])  7.68 us
    unnamed x19, local copies, waits for them, and re-layouts  3.41 us
    ppermute x1, starting transfers between devices, shards(): arrived.append(lax.ppermute(send[j - 1:j], 'grp', pairs))  2.34 us
    ppermute x1, waiting for transfers between devices, shards(): lax.ppermute(sent, 'slab', [(i, (i + 1) % slab_size) for i in range(slab_...  2 us
    reshape x1, local copies, waits for them, and re-layouts, shards(): side_jac.reshape(n_side * elems, length)  1.57 us
  transfers between devices with their start and end apart: 8, of which 4 were waited for; matrix products, arithmetic and copies ran while one was open for 4% of the time, Pallas kernels for 0%

profile of v3, /device:TPU:0, one launch (start us, length us, event | category | flops | bytes accessed | tf_op | source)
XLA Modules:
  0.0 43.9 jit_solution(3478628232604050234)
XLA Ops:
  0.0 2.2 %copy.13 = bf16[12,2,15625]{2,0,1:T(8,128)(2,1)} copy(bf16[12,2,15625]{2,1,0:T(2,128)(2,1)} %param.11) | data formatting | bytes 1500000 | tf_op args[1]
  2.2 3.2 %xface.1 = (bf16[16,400]{1,0:T(8,128)(2,1)}, bf16[16,400]{1,0:T(8,128)(2,1)}) custom-call(bf16[2,12,15625]{2,1,0:T(8,128)(2,1)} %bitcast.7, bf16[3125,256]{1,0:T(8,128)(2,1)} %constant.14.clone.table_ref.table_hbm, bf16[2,80,512]{2,1,0:T(8,128)(2,1)} %constant.17.clone.turn_ref, s32[1,12]{1,0:T(1,128)} %bitcast.8), custom_call_target="tpu_custom_call" | custom-call | tf_op jit(solution)/shard_map/xface/pallas_call | solution.py:306
  5.4 0.5 %collective-permute-start = (bf16[16,400]{1,0:T(8,128)(2,1)}, bf16[16,400]{1,0:T(8,128)(2,1)S(1)}, u32[]{:S(2)}, u32[]{:S(2)}) collective-permute-start(bf16[16,400]{1,0:T(8,128)(2,1)} %get-tuple-element.9), channel_id=1, source_target_pairs={{0,8},{8,16},{16,24},{24,0},{1,9},{9,17},{17,25},{25,1},{2,10},{10... | collective-permute-start | bytes 38408 | tf_op jit(solution)/shard_map/ppermute | solution.py:334
  5.9 0.0 copy-done
  5.9 1.6 %reshape.3.side_hbm = bf16[48,15625]{1,0:T(8,128)(2,1)} reshape(bf16[12,4,15625]{2,1,0:T(4,128)(2,1)S(1)} %copy-done) | data formatting | bytes 3000000 | tf_op jit(solution)/shard_map/reshape | solution.py:354
  7.4 2.0 %collective-permute-done.minus_ref = bf16[16,400]{1,0:T(8,128)(2,1)S(1)} collective-permute-done((bf16[16,400]{1,0:T(8,128)(2,1)}, bf16[16,400]{1,0:T(8,128)(2,1)S(1)}, u32[]{:S(2)}, u32[]{:S(2)}) %collective-permute-start) | collective-permute-done | bytes 12832 | tf_op jit(solution)/shard_map/ppermute | solution.py:334
  9.5 0.6 %copy-done.8 = bf16[16,400]{1,0:T(8,128)(2,1)} copy-done((bf16[16,400]{1,0:T(8,128)(2,1)}, bf16[16,400]{1,0:T(8,128)(2,1)S(1)}, u32[]{:S(2)}) %copy-start.8) | copy-done | bytes 12824
  10.0 11.6 %main.1 = (bf16[1,9,32,128]{3,2,1,0:T(8,128)(2,1)}, bf16[1,9,32,128]{3,2,1,0:T(8,128)(2,1)}) custom-call(s32[1]{0:T(128)} %bitcast.where_ref, bf16[12,625,625]{2,1,0:T(8,128)(2,1)} %diag_hbm.1, bf16[48,15625]{1,0:T(8,128)(2,1)} %reshape.3.side_hbm, bf16[3125,256]{1,0:T(8,128)(2,1)} %constant.14.clone.table_ref.table_hbm, ...), custom_call_target="tpu_custom_call" | custom-call | tf_op jit(solution)/shard_map/main/pallas_call | solution.py:306
  21.7 2.3 %collective-permute-start.4 = (bf16[1,9,32,128]{3,2,1,0:T(8,128)(2,1)}, bf16[1,9,32,128]{3,2,1,0:T(8,128)(2,1)S(1)}, u32[]{:S(2)}, u32[]{:S(2)}) collective-permute-start(bf16[1,9,32,128]{3,2,1,0:T(8,128)(2,1)} %get-tuple-element.12), channel_id=1, source_target_pairs={{0,1},{1,0},{2,3},{3,2},{4,5},{5,4},{6,7},{7,6},{8,9},{9,8},{10,11... | collective-permute-start | bytes 221192 | tf_op jit(solution)/shard_map/ppermute | solution.py:363
  24.0 1.3 %collective-permute-start.3 = (bf16[1,9,32,128]{3,2,1,0:T(8,128)(2,1)}, bf16[1,9,32,128]{3,2,1,0:T(8,128)(2,1)S(1)}, u32[]{:S(2)}, u32[]{:S(2)}) collective-permute-start(bf16[1,9,32,128]{3,2,1,0:T(8,128)(2,1)} %get-tuple-element.11.refs_0_), channel_id=1, source_target_pairs={{6,0},{7,1},{14,8},{15,9},{22,16},{23,17},{30,24},{31,25}} | collective-permute-start | bytes 221192 | tf_op jit(solution)/shard_map/ppermute | solution.py:368
  25.3 1.3 %collective-permute-start.2 = (bf16[1,9,32,128]{3,2,1,0:T(8,128)(2,1)}, bf16[1,9,32,128]{3,2,1,0:T(8,128)(2,1)S(1)}, u32[]{:S(2)}, u32[]{:S(2)}) collective-permute-start(bf16[1,9,32,128]{3,2,1,0:T(8,128)(2,1)} %get-tuple-element.11.refs_0_), channel_id=1, source_target_pairs={{4,0},{5,1},{12,8},{13,9},{20,16},{21,17},{28,24},{29,25}} | collective-permute-start | bytes 221192 | tf_op jit(solution)/shard_map/ppermute | solution.py:368
  26.6 1.3 %collective-permute-start.1 = (bf16[1,9,32,128]{3,2,1,0:T(8,128)(2,1)}, bf16[1,9,32,128]{3,2,1,0:T(8,128)(2,1)S(1)}, u32[]{:S(2)}, u32[]{:S(2)}) collective-permute-start(bf16[1,9,32,128]{3,2,1,0:T(8,128)(2,1)} %get-tuple-element.11.refs_0_), channel_id=1, source_target_pairs={{2,0},{3,1},{10,8},{11,9},{18,16},{19,17},{26,24},{27,25}} | collective-permute-start | bytes 221192 | tf_op jit(solution)/shard_map/ppermute | solution.py:368
  27.9 0.0 collective-permute-done.4.refs_4_
  27.9 0.0 copy-start.1
  27.9 1.3 %collective-permute-start.7 = (bf16[1,9,32,128]{3,2,1,0:T(8,128)(2,1)S(1)}, bf16[1,9,32,128]{3,2,1,0:T(8,128)(2,1)S(1)}, u32[]{:S(2)}, u32[]{:S(2)}) collective-permute-start(bf16[1,9,32,128]{3,2,1,0:T(8,128)(2,1)S(1)} %collective-permute-done.4.refs_4_), channel_id=1, source_target_pairs={{6,0},{7,1},{14,8},{15,9},{22,16},{23,17},{30,24},{31,25}} | collective-permute-start | bytes 221192 | tf_op jit(solution)/shard_map/ppermute | solution.py:368
  29.2 1.3 %collective-permute-start.6 = (bf16[1,9,32,128]{3,2,1,0:T(8,128)(2,1)S(1)}, bf16[1,9,32,128]{3,2,1,0:T(8,128)(2,1)S(1)}, u32[]{:S(2)}, u32[]{:S(2)}) collective-permute-start(bf16[1,9,32,128]{3,2,1,0:T(8,128)(2,1)S(1)} %collective-permute-done.4.refs_4_), channel_id=1, source_target_pairs={{4,0},{5,1},{12,8},{13,9},{20,16},{21,17},{28,24},{29,25}} | collective-permute-start | bytes 221192 | tf_op jit(solution)/shard_map/ppermute | solution.py:368
  30.5 1.9 %collective-permute-done.3.refs_3_ = bf16[1,9,32,128]{3,2,1,0:T(8,128)(2,1)S(1)} collective-permute-done((bf16[1,9,32,128]{3,2,1,0:T(8,128)(2,1)}, bf16[1,9,32,128]{3,2,1,0:T(8,128)(2,1)S(1)}, u32[]{:S(2)}, u32[]{:S(2)}) %collective-permute-start.3) | collective-permute-done | bytes 73760 | tf_op jit(solution)/shard_map/ppermute | solution.py:368
  32.5 1.3 %collective-permute-start.5 = (bf16[1,9,32,128]{3,2,1,0:T(8,128)(2,1)S(1)}, bf16[1,9,32,128]{3,2,1,0:T(8,128)(2,1)S(1)}, u32[]{:S(2)}, u32[]{:S(2)}) collective-permute-start(bf16[1,9,32,128]{3,2,1,0:T(8,128)(2,1)S(1)} %collective-permute-done.4.refs_4_), channel_id=1, source_target_pairs={{2,0},{3,1},{10,8},{11,9},{18,16},{19,17},{26,24},{27,25}} | collective-permute-start | bytes 221192 | tf_op jit(solution)/shard_map/ppermute | solution.py:368
  33.8 0.0 collective-permute-done.2.refs_2_
  33.8 0.0 copy-start.3
  33.8 4.3 %collective-permute-done.1.refs_1_ = bf16[1,9,32,128]{3,2,1,0:T(8,128)(2,1)S(1)} collective-permute-done((bf16[1,9,32,128]{3,2,1,0:T(8,128)(2,1)}, bf16[1,9,32,128]{3,2,1,0:T(8,128)(2,1)S(1)}, u32[]{:S(2)}, u32[]{:S(2)}) %collective-permute-start.1) | collective-permute-done | bytes 73760 | tf_op jit(solution)/shard_map/ppermute | solution.py:368
  38.1 0.0 collective-permute-done.7.refs_7_
  38.1 0.0 collective-permute-done.6.refs_6_
  38.1 0.0 copy-start.6
  38.1 1.5 %collective-permute-done.5.refs_5_ = bf16[1,9,32,128]{3,2,1,0:T(8,128)(2,1)S(1)} collective-permute-done((bf16[1,9,32,128]{3,2,1,0:T(8,128)(2,1)S(1)}, bf16[1,9,32,128]{3,2,1,0:T(8,128)(2,1)S(1)}, u32[]{:S(2)}, u32[]{:S(2)}) %collective-permute-start.5) | collective-permute-done | bytes 73760 | tf_op jit(solution)/shard_map/ppermute | solution.py:368
  39.6 0.0 copy-done.1
  39.6 0.0 copy-done.2
  39.6 0.0 copy-done.3
  39.6 0.0 copy-done.4
  39.6 0.0 copy-done.5
  39.6 0.6 %copy-done.7 = bf16[1,9,32,128]{3,2,1,0:T(8,128)(2,1)} copy-done((bf16[1,9,32,128]{3,2,1,0:T(8,128)(2,1)}, bf16[1,9,32,128]{3,2,1,0:T(8,128)(2,1)S(1)}, u32[]{:S(2)}) %copy-start.7) | copy-done | bytes 73752
  40.2 3.7 %unpack.1 = bf16[7,72,1600]{2,1,0:T(8,128)(2,1)} custom-call(s32[1]{0:T(128)} %bitcast.where_ref, bf16[1,9,32,128]{3,2,1,0:T(8,128)(2,1)} %get-tuple-element.11.refs_0_, bf16[1,9,32,128]{3,2,1,0:T(8,128)(2,1)} %copy-done.4, bf16[1,9,32,128]{3,2,1,0:T(8,128)(2,1)} %copy-done.3, bf16[1,9,32,128]{3,2,1,0:T(8,128)(2,1)} %copy-done.2, ...), custom_call_target="tpu_custom_call" | custom-call | tf_op jit(solution)/shard_map/unpack/pallas_call | solution.py:306
  (7 shorter events, 0.0 us)
Async XLA Ops:
  2.2 3.7 %copy-start = (bf16[12,4,15625]{2,1,0:T(4,128)(2,1)S(1)}, bf16[12,4,15625]{2,1,0:T(4,128)(2,1)}, u32[]{:S(2)}) copy-start(bf16[12,4,15625]{2,1,0:T(4,128)(2,1)} %param.12) | copy-start | bytes 4500004
  5.4 4.1 %collective-permute-start = (bf16[16,400]{1,0:T(8,128)(2,1)}, bf16[16,400]{1,0:T(8,128)(2,1)S(1)}, u32[]{:S(2)}, u32[]{:S(2)}) collective-permute-start(bf16[16,400]{1,0:T(8,128)(2,1)} %get-tuple-element.9), channel_id=1, source_target_pairs={{0,8},{8,16},{16,24},{24,0},{1,9},{9,17},{17,25},{25,1},{2,10},{10... | collective-permute-start | bytes 38408 | tf_op jit(solution)/shard_map/ppermute | solution.py:334
  9.4 0.6 %copy-start.8 = (bf16[16,400]{1,0:T(8,128)(2,1)}, bf16[16,400]{1,0:T(8,128)(2,1)S(1)}, u32[]{:S(2)}) copy-start(bf16[16,400]{1,0:T(8,128)(2,1)S(1)} %collective-permute-done.minus_ref) | copy-start | bytes 38404
  21.7 6.2 %collective-permute-start.4 = (bf16[1,9,32,128]{3,2,1,0:T(8,128)(2,1)}, bf16[1,9,32,128]{3,2,1,0:T(8,128)(2,1)S(1)}, u32[]{:S(2)}, u32[]{:S(2)}) collective-permute-start(bf16[1,9,32,128]{3,2,1,0:T(8,128)(2,1)} %get-tuple-element.12), channel_id=1, source_target_pairs={{0,1},{1,0},{2,3},{3,2},{4,5},{5,4},{6,7},{7,6},{8,9},{9,8},{10,11... | collective-permute-start | bytes 221192 | tf_op jit(solution)/shard_map/ppermute | solution.py:363
  24.0 8.4 %collective-permute-start.3 = (bf16[1,9,32,128]{3,2,1,0:T(8,128)(2,1)}, bf16[1,9,32,128]{3,2,1,0:T(8,128)(2,1)S(1)}, u32[]{:S(2)}, u32[]{:S(2)}) collective-permute-start(bf16[1,9,32,128]{3,2,1,0:T(8,128)(2,1)} %get-tuple-element.11.refs_0_), channel_id=1, source_target_pairs={{6,0},{7,1},{14,8},{15,9},{22,16},{23,17},{30,24},{31,25}} | collective-permute-start | bytes 221192 | tf_op jit(solution)/shard_map/ppermute | solution.py:368
  25.3 8.4 %collective-permute-start.2 = (bf16[1,9,32,128]{3,2,1,0:T(8,128)(2,1)}, bf16[1,9,32,128]{3,2,1,0:T(8,128)(2,1)S(1)}, u32[]{:S(2)}, u32[]{:S(2)}) collective-permute-start(bf16[1,9,32,128]{3,2,1,0:T(8,128)(2,1)} %get-tuple-element.11.refs_0_), channel_id=1, source_target_pairs={{4,0},{5,1},{12,8},{13,9},{20,16},{21,17},{28,24},{29,25}} | collective-permute-start | bytes 221192 | tf_op jit(solution)/shard_map/ppermute | solution.py:368
  26.6 11.4 %collective-permute-start.1 = (bf16[1,9,32,128]{3,2,1,0:T(8,128)(2,1)}, bf16[1,9,32,128]{3,2,1,0:T(8,128)(2,1)S(1)}, u32[]{:S(2)}, u32[]{:S(2)}) collective-permute-start(bf16[1,9,32,128]{3,2,1,0:T(8,128)(2,1)} %get-tuple-element.11.refs_0_), channel_id=1, source_target_pairs={{2,0},{3,1},{10,8},{11,9},{18,16},{19,17},{26,24},{27,25}} | collective-permute-start | bytes 221192 | tf_op jit(solution)/shard_map/ppermute | solution.py:368
  27.9 11.6 %copy-start.1 = (bf16[1,9,32,128]{3,2,1,0:T(8,128)(2,1)}, bf16[1,9,32,128]{3,2,1,0:T(8,128)(2,1)S(1)}, u32[]{:S(2)}) copy-start(bf16[1,9,32,128]{3,2,1,0:T(8,128)(2,1)S(1)} %collective-permute-done.4.refs_4_) | copy-start | bytes 221188
  27.9 10.1 %collective-permute-start.7 = (bf16[1,9,32,128]{3,2,1,0:T(8,128)(2,1)S(1)}, bf16[1,9,32,128]{3,2,1,0:T(8,128)(2,1)S(1)}, u32[]{:S(2)}, u32[]{:S(2)}) collective-permute-start(bf16[1,9,32,128]{3,2,1,0:T(8,128)(2,1)S(1)} %collective-permute-done.4.refs_4_), channel_id=1, source_target_pairs={{6,0},{7,1},{14,8},{15,9},{22,16},{23,17},{30,24},{31,25}} | collective-permute-start | bytes 221192 | tf_op jit(solution)/shard_map/ppermute | solution.py:368
  29.2 8.8 %collective-permute-start.6 = (bf16[1,9,32,128]{3,2,1,0:T(8,128)(2,1)S(1)}, bf16[1,9,32,128]{3,2,1,0:T(8,128)(2,1)S(1)}, u32[]{:S(2)}, u32[]{:S(2)}) collective-permute-start(bf16[1,9,32,128]{3,2,1,0:T(8,128)(2,1)S(1)} %collective-permute-done.4.refs_4_), channel_id=1, source_target_pairs={{4,0},{5,1},{12,8},{13,9},{20,16},{21,17},{28,24},{29,25}} | collective-permute-start | bytes 221192 | tf_op jit(solution)/shard_map/ppermute | solution.py:368
  32.5 7.1 %copy-start.2 = (bf16[1,9,32,128]{3,2,1,0:T(8,128)(2,1)}, bf16[1,9,32,128]{3,2,1,0:T(8,128)(2,1)S(1)}, u32[]{:S(2)}) copy-start(bf16[1,9,32,128]{3,2,1,0:T(8,128)(2,1)S(1)} %collective-permute-done.3.refs_3_) | copy-start | bytes 221188
  32.5 7.1 %collective-permute-start.5 = (bf16[1,9,32,128]{3,2,1,0:T(8,128)(2,1)S(1)}, bf16[1,9,32,128]{3,2,1,0:T(8,128)(2,1)S(1)}, u32[]{:S(2)}, u32[]{:S(2)}) collective-permute-start(bf16[1,9,32,128]{3,2,1,0:T(8,128)(2,1)S(1)} %collective-permute-done.4.refs_4_), channel_id=1, source_target_pairs={{2,0},{3,1},{10,8},{11,9},{18,16},{19,17},{26,24},{27,25}} | collective-permute-start | bytes 221192 | tf_op jit(solution)/shard_map/ppermute | solution.py:368
  33.8 5.8 %copy-start.3 = (bf16[1,9,32,128]{3,2,1,0:T(8,128)(2,1)}, bf16[1,9,32,128]{3,2,1,0:T(8,128)(2,1)S(1)}, u32[]{:S(2)}) copy-start(bf16[1,9,32,128]{3,2,1,0:T(8,128)(2,1)S(1)} %collective-permute-done.2.refs_2_) | copy-start | bytes 221188
  38.1 1.5 %copy-start.4 = (bf16[1,9,32,128]{3,2,1,0:T(8,128)(2,1)}, bf16[1,9,32,128]{3,2,1,0:T(8,128)(2,1)S(1)}, u32[]{:S(2)}) copy-start(bf16[1,9,32,128]{3,2,1,0:T(8,128)(2,1)S(1)} %collective-permute-done.1.refs_1_) | copy-start | bytes 221188
  38.1 1.5 %copy-start.5 = (bf16[1,9,32,128]{3,2,1,0:T(8,128)(2,1)}, bf16[1,9,32,128]{3,2,1,0:T(8,128)(2,1)S(1)}, u32[]{:S(2)}) copy-start(bf16[1,9,32,128]{3,2,1,0:T(8,128)(2,1)S(1)} %collective-permute-done.7.refs_7_) | copy-start | bytes 221188
  38.1 1.5 %copy-start.6 = (bf16[1,9,32,128]{3,2,1,0:T(8,128)(2,1)}, bf16[1,9,32,128]{3,2,1,0:T(8,128)(2,1)S(1)}, u32[]{:S(2)}) copy-start(bf16[1,9,32,128]{3,2,1,0:T(8,128)(2,1)S(1)} %collective-permute-done.6.refs_6_) | copy-start | bytes 221188
  39.6 0.6 %copy-start.7 = (bf16[1,9,32,128]{3,2,1,0:T(8,128)(2,1)}, bf16[1,9,32,128]{3,2,1,0:T(8,128)(2,1)S(1)}, u32[]{:S(2)}) copy-start(bf16[1,9,32,128]{3,2,1,0:T(8,128)(2,1)S(1)} %collective-permute-done.5.refs_5_) | copy-start | bytes 221188

commit v4 on v3

--- a/solution.py
+++ b/solution.py
@@ -176,19 +176,16 @@
 
 
 def coarse_block(block, right, left):
-    half = LANES // 2
-    y = jnp.dot(block, right, preferred_element_type=F32)
-    z = y + pltpu.roll(y, half, 1)
-    lane = lax.broadcasted_iota(jnp.int32, z.shape, 1)
-    high = z.astype(BF16).astype(F32)
-    parts = jnp.where(lane < half, z, z - high).astype(BF16)
-    g = jnp.dot(left, parts, preferred_element_type=F32)
-    return g[:NCOARSE] + g[NCOARSE:] + pltpu.roll(g[:NCOARSE], half, 1)
+    w = jnp.dot(left, block, preferred_element_type=F32)
+    w = w[:NCOARSE] + w[NCOARSE:]
+    rest = w - w.astype(BF16).astype(F32)
+    g = jnp.dot(jnp.concatenate([w, rest], axis=0).astype(BF16), right, preferred_element_type=F32)
+    return g[:NCOARSE] + g[NCOARSE:] + pltpu.roll(g[:NCOARSE], LANES // 2, 1)
 
 
 def main_kernel(
-    where_ref, diag_hbm, side_hbm, table_hbm, right_ref, left_ref, minus_ref, plus_ref, owner_ref,
-    keep_ref, send_ref, blocks, side, table, stacked, products, coarse, rows, packed_scr, sems, *, many, owners_n,
+    diag_hbm, side_hbm, table_hbm, right_ref, left_ref, out_ref,
+    blocks, side, table, stacked, products, coarse, rows, sems, *, many,
 ):
     elems = blocks.shape[0]
     n_side = side.shape[0] // elems
@@ -198,23 +195,11 @@
     def block_copy(e):
         return pltpu.make_async_copy(diag_hbm.at[e], blocks.at[e], sems.at[e])
 
-    for e in range(many):
-        block_copy(e).start()
     side_copy.start()
     table_copy.start()
-    for e in range(many, elems):
+    for e in range(elems):
         block_copy(e).start()
     rows[...] = jnp.zeros_like(rows)
-    rows[:, :FACE] = minus_ref[...].astype(F32)
-    rows[:, FACE : 2 * FACE] = plus_ref[...].astype(F32)
-
-    def coarse_at(e):
-        g = coarse_block(blocks[e], right_ref[...], left_ref[...])
-        coarse[pl.ds(e * NCOARSE, NCOARSE), :] = g
-
-    for e in range(many):
-        block_copy(e).wait()
-        coarse_at(e)
     side_copy.wait()
     table_copy.wait()
     pitch = stacked.shape[0] // NV
@@ -229,20 +214,33 @@
         for i in range(many):
             block_copy(step * many + i).wait()
         for i in range(many):
-            coarse_at(step * many + i)
+            e = step * many + i
+            g = coarse_block(blocks[e], right_ref[...], left_ref[...])
+            coarse[pl.ds(e * NCOARSE, NCOARSE), :] = g
         return carry
 
-    lax.fori_loop(1, elems // many, some_blocks, 0)
+    lax.fori_loop(0, elems // many, some_blocks, 0)
     for c in range(NCOARSE):
         piece = coarse[pl.ds(c, elems, stride=NCOARSE), :]
         start = DIAG_AT + c * NCOARSE
         rows[:elems, start : start + NCOARSE] = piece[:, :NCOARSE]
+    out_ref[...] = rows[...].astype(BF16)
+
+
+def pack_kernel(where_ref, rows_ref, minus_ref, plus_ref, owner_ref, keep_ref, send_ref, head, packed_scr, *, owners_n):
+    elems = owner_ref.shape[1]
+    cut = head.shape[1]
+    head[...] = rows_ref[:, :cut].astype(F32)
+    head[:, :FACE] = minus_ref[...].astype(F32)
+    head[:, FACE : 2 * FACE] = plus_ref[...].astype(F32)
     most = keep_ref.shape[1]
     slots = owners_n * most
     placer = placement(owner_ref[...], where_ref[0], owners_n, most)
-    packed = jnp.dot(placer, rows[:elems].astype(BF16), preferred_element_type=F32)
+    first = jnp.dot(placer, head[:elems].astype(BF16), preferred_element_type=F32)
+    rest = jnp.dot(placer, rows_ref[:elems, cut:], preferred_element_type=F32)
     for j in range(ROW_TILES):
-        packed_scr[pl.ds(j, slots, stride=ROW_TILES), :] = packed[:, j * LANES : (j + 1) * LANES]
+        source, at = (first, j * LANES) if j * LANES < cut else (rest, j * LANES - cut)
+        packed_scr[pl.ds(j, slots, stride=ROW_TILES), :] = source[:, at : at + LANES]
     kept = most * ROW_TILES
     keep_ref[...] = packed_scr[:kept].astype(BF16).reshape(keep_ref.shape)
     send_ref[...] = packed_scr[kept:].astype(BF16).reshape(send_ref.shape)
@@ -337,9 +335,9 @@
     n_side = side_jac.shape[1]
     pitch = round_up(n_side * elems, 16)
     chunk = (most, ROW_TILES, LANES)
-    keep, send = call(
-        functools.partial(main_kernel, many=many, owners_n=owners_n),
-        (sds((1,) + chunk, BF16), sds((owners_n - 1,) + chunk, BF16)),
+    rows = call(
+        functools.partial(main_kernel, many=many),
+        sds((pad, ROW_TILES * LANES), BF16),
         [
             pltpu.VMEM((elems, nf, nf), BF16),
             pltpu.VMEM((n_side * elems, length), BF16),
@@ -348,12 +346,22 @@
             pltpu.VMEM((NV * pitch, LANES), F32),
             pltpu.VMEM((elems * NCOARSE, LANES), F32),
             pltpu.VMEM((pad, ROW_TILES * LANES), F32),
-            pltpu.VMEM((owners_n * most * ROW_TILES, LANES), F32),
             pltpu.SemaphoreType.DMA((elems + 2,)),
         ],
-        where, diag_jac, side_jac.reshape(n_side * elems, length), table, right, left, minus, plus, owner[None, :],
-        in_specs=[SMALL] + [pl.BlockSpec(memory_space=pl.ANY)] * 3 + [VMEM] * 5,
+        diag_jac, side_jac.reshape(n_side * elems, length), table, right, left,
+        in_specs=[pl.BlockSpec(memory_space=pl.ANY)] * 3 + [VMEM] * 2,
         name="main",
+    )
+    keep, send = call(
+        functools.partial(pack_kernel, owners_n=owners_n),
+        (sds((1,) + chunk, BF16), sds((owners_n - 1,) + chunk, BF16)),
+        [
+            pltpu.VMEM((pad, round_up(2 * FACE, LANES)), F32),
+            pltpu.VMEM((owners_n * most * ROW_TILES, LANES), F32),
+        ],
+        where, rows, minus, plus, owner[None, :],
+        in_specs=[SMALL] + [VMEM] * 4,
+        name="pack",
     )
 
     groups = grp_size // owners_n

time: 44.2 us -> 42.8 us (0.968)
  Pallas kernels: 18.5 us -> 17.5 us
  waiting for transfers between devices: 9.69 us -> 9.08 us
    ppermute x1, waiting for transfers between devices: 2 us -> 0.01 us  [shards(): lax.ppermute(sent, 'slab', [(i, (i + 1) % slab_size) for i in range(slab_...]
    ppermute x6, waiting for transfers between devices: 7.68 us -> 9.08 us  [to_owners(): lax.ppermute(array, 'grp', [(a * owners_n + o, o) for o in range(owners_n)])]
    pallas_call x3 -> x4, Pallas kernels: 18.5 us -> 17.5 us  [call(): pl.pallas_call(kernel, out_shape=out_shape, scratch_shapes=scratch, **kwa...]
  transfers between devices with their start and end apart: 8 -> 8, of which waited for: 4 -> 4; matrix products, arithmetic and copies ran while one was open for 4% -> 4% of each run, Pallas kernels for 0% -> 20%
where the time goes in v4:
time: 42.8 us; the launch traced here: 42.4 us
  Pallas kernels  17.5 us (41%)
  starting transfers between devices  10.7 us (25%)
  waiting for transfers between devices  9.08 us (21%)
  local copies, waits for them, and re-layouts  4.99 us (12%)
    pallas_call x4, Pallas kernels, call(): pl.pallas_call(kernel, out_shape=out_shape, scratch_shapes=scratch, **kwa...  17.5 us
    ppermute x6, waiting for transfers between devices, to_owners(): lax.ppermute(array, 'grp', [(a * owners_n + o, o) for o in range(owners_n)])  9.08 us
    ppermute x6, starting transfers between devices, to_owners(): lax.ppermute(array, 'grp', [(a * owners_n + o, o) for o in range(owners_n)])  7.73 us
    unnamed x19, local copies, waits for them, and re-layouts  3.42 us
    ppermute x1, starting transfers between devices, shards(): arrived.append(lax.ppermute(send[j - 1:j], 'grp', pairs))  2.49 us
    reshape x1, local copies, waits for them, and re-layouts, shards(): side_jac.reshape(n_side * elems, length)  1.57 us
  transfers between devices with their start and end apart: 8, of which 4 were waited for; matrix products, arithmetic and copies ran while one was open for 4% of the time, Pallas kernels for 20%

profile of v4, /device:TPU:0, one launch (start us, length us, event | category | flops | bytes accessed | tf_op | source)
XLA Modules:
  0.0 42.4 jit_solution(1628545931739072579)
XLA Ops:
  0.0 2.2 %copy.13 = bf16[12,2,15625]{2,0,1:T(8,128)(2,1)} copy(bf16[12,2,15625]{2,1,0:T(2,128)(2,1)} %param.11) | data formatting | bytes 1500000 | tf_op args[1]
  2.2 3.2 %xface.1 = (bf16[16,400]{1,0:T(8,128)(2,1)}, bf16[16,400]{1,0:T(8,128)(2,1)}) custom-call(bf16[2,12,15625]{2,1,0:T(8,128)(2,1)} %bitcast.7, bf16[3125,256]{1,0:T(8,128)(2,1)} %constant.14.clone.table_hbm.table_ref, bf16[2,80,512]{2,1,0:T(8,128)(2,1)} %constant.17.clone.turn_ref, s32[1,12]{1,0:T(1,128)} %bitcast.8), custom_call_target="tpu_custom_call" | custom-call | tf_op jit(solution)/shard_map/xface/pallas_call | solution.py:304
  5.4 0.5 %collective-permute-start = (bf16[16,400]{1,0:T(8,128)(2,1)}, bf16[16,400]{1,0:T(8,128)(2,1)S(1)}, u32[]{:S(2)}, u32[]{:S(2)}) collective-permute-start(bf16[16,400]{1,0:T(8,128)(2,1)} %get-tuple-element.9), channel_id=1, source_target_pairs={{0,8},{8,16},{16,24},{24,0},{1,9},{9,17},{17,25},{25,1},{2,10},{10... | collective-permute-start | bytes 38408 | tf_op jit(solution)/shard_map/ppermute | solution.py:332
  5.9 0.0 copy-done
  5.9 1.6 %reshape.3.side_hbm = bf16[48,15625]{1,0:T(8,128)(2,1)} reshape(bf16[12,4,15625]{2,1,0:T(4,128)(2,1)S(1)} %copy-done) | data formatting | bytes 3000000 | tf_op jit(solution)/shard_map/reshape | solution.py:351
  7.4 8.6 %main.1.rows_ref = bf16[16,4096]{1,0:T(8,128)(2,1)} custom-call(bf16[12,625,625]{2,1,0:T(8,128)(2,1)} %diag_hbm.1, bf16[48,15625]{1,0:T(8,128)(2,1)} %reshape.3.side_hbm, bf16[3125,256]{1,0:T(8,128)(2,1)} %constant.14.clone.table_hbm.table_ref, bf16[625,128]{1,0:T(8,128)(2,1)} %constant.15.clone.right_ref, bf16[80,625]{1,0:T(8,128)(2,1)} %constant.16.clone.left_ref), custom_call_target="tpu_custom_call" | custom-call | tf_op jit(solution)/shard_map/main/pallas_call | solution.py:304
  16.1 0.0 collective-permute-done.minus_ref
  16.1 0.0 copy-start.8
  16.1 0.6 %copy-done.8 = bf16[16,400]{1,0:T(8,128)(2,1)} copy-done((bf16[16,400]{1,0:T(8,128)(2,1)}, bf16[16,400]{1,0:T(8,128)(2,1)S(1)}, u32[]{:S(2)}) %copy-start.8) | copy-done | bytes 12824
  16.7 2.0 %pack.1 = (bf16[1,9,32,128]{3,2,1,0:T(8,128)(2,1)}, bf16[1,9,32,128]{3,2,1,0:T(8,128)(2,1)}) custom-call(s32[1]{0:T(128)} %bitcast.where_ref, bf16[16,4096]{1,0:T(8,128)(2,1)} %main.1.rows_ref, bf16[16,400]{1,0:T(8,128)(2,1)} %copy-done.8, bf16[16,400]{1,0:T(8,128)(2,1)} %get-tuple-element.10.plus_ref, s32[1,12]{1,0:T(1,128)} %bitcast.9), custom_call_target="tpu_custom_call" | custom-call | tf_op jit(solution)/shard_map/pack/pallas_call | solution.py:304
  18.7 2.5 %collective-permute-start.4 = (bf16[1,9,32,128]{3,2,1,0:T(8,128)(2,1)}, bf16[1,9,32,128]{3,2,1,0:T(8,128)(2,1)S(1)}, u32[]{:S(2)}, u32[]{:S(2)}) collective-permute-start(bf16[1,9,32,128]{3,2,1,0:T(8,128)(2,1)} %get-tuple-element.12), channel_id=1, source_target_pairs={{0,1},{1,0},{2,3},{3,2},{4,5},{5,4},{6,7},{7,6},{8,9},{9,8},{10,11... | collective-permute-start | bytes 221192 | tf_op jit(solution)/shard_map/ppermute | solution.py:371
  21.2 1.3 %collective-permute-start.3 = (bf16[1,9,32,128]{3,2,1,0:T(8,128)(2,1)}, bf16[1,9,32,128]{3,2,1,0:T(8,128)(2,1)S(1)}, u32[]{:S(2)}, u32[]{:S(2)}) collective-permute-start(bf16[1,9,32,128]{3,2,1,0:T(8,128)(2,1)} %get-tuple-element.11.refs_0_), channel_id=1, source_target_pairs={{6,0},{7,1},{14,8},{15,9},{22,16},{23,17},{30,24},{31,25}} | collective-permute-start | bytes 221192 | tf_op jit(solution)/shard_map/ppermute | solution.py:376
  22.5 1.3 %collective-permute-start.2 = (bf16[1,9,32,128]{3,2,1,0:T(8,128)(2,1)}, bf16[1,9,32,128]{3,2,1,0:T(8,128)(2,1)S(1)}, u32[]{:S(2)}, u32[]{:S(2)}) collective-permute-start(bf16[1,9,32,128]{3,2,1,0:T(8,128)(2,1)} %get-tuple-element.11.refs_0_), channel_id=1, source_target_pairs={{4,0},{5,1},{12,8},{13,9},{20,16},{21,17},{28,24},{29,25}} | collective-permute-start | bytes 221192 | tf_op jit(solution)/shard_map/ppermute | solution.py:376
  23.8 1.3 %collective-permute-start.1 = (bf16[1,9,32,128]{3,2,1,0:T(8,128)(2,1)}, bf16[1,9,32,128]{3,2,1,0:T(8,128)(2,1)S(1)}, u32[]{:S(2)}, u32[]{:S(2)}) collective-permute-start(bf16[1,9,32,128]{3,2,1,0:T(8,128)(2,1)} %get-tuple-element.11.refs_0_), channel_id=1, source_target_pairs={{2,0},{3,1},{10,8},{11,9},{18,16},{19,17},{26,24},{27,25}} | collective-permute-start | bytes 221192 | tf_op jit(solution)/shard_map/ppermute | solution.py:376
  25.1 0.0 collective-permute-done.4.refs_4_
  25.1 0.0 copy-start.1
  25.1 1.3 %collective-permute-start.7 = (bf16[1,9,32,128]{3,2,1,0:T(8,128)(2,1)S(1)}, bf16[1,9,32,128]{3,2,1,0:T(8,128)(2,1)S(1)}, u32[]{:S(2)}, u32[]{:S(2)}) collective-permute-start(bf16[1,9,32,128]{3,2,1,0:T(8,128)(2,1)S(1)} %collective-permute-done.4.refs_4_), channel_id=1, source_target_pairs={{6,0},{7,1},{14,8},{15,9},{22,16},{23,17},{30,24},{31,25}} | collective-permute-start | bytes 221192 | tf_op jit(solution)/shard_map/ppermute | solution.py:376
  26.4 1.3 %collective-permute-start.6 = (bf16[1,9,32,128]{3,2,1,0:T(8,128)(2,1)S(1)}, bf16[1,9,32,128]{3,2,1,0:T(8,128)(2,1)S(1)}, u32[]{:S(2)}, u32[]{:S(2)}) collective-permute-start(bf16[1,9,32,128]{3,2,1,0:T(8,128)(2,1)S(1)} %collective-permute-done.4.refs_4_), channel_id=1, source_target_pairs={{4,0},{5,1},{12,8},{13,9},{20,16},{21,17},{28,24},{29,25}} | collective-permute-start | bytes 221192 | tf_op jit(solution)/shard_map/ppermute | solution.py:376
  27.7 2.3 %collective-permute-done.3.refs_3_ = bf16[1,9,32,128]{3,2,1,0:T(8,128)(2,1)S(1)} collective-permute-done((bf16[1,9,32,128]{3,2,1,0:T(8,128)(2,1)}, bf16[1,9,32,128]{3,2,1,0:T(8,128)(2,1)S(1)}, u32[]{:S(2)}, u32[]{:S(2)}) %collective-permute-start.3) | collective-permute-done | bytes 73760 | tf_op jit(solution)/shard_map/ppermute | solution.py:376
  30.0 1.3 %collective-permute-start.5 = (bf16[1,9,32,128]{3,2,1,0:T(8,128)(2,1)S(1)}, bf16[1,9,32,128]{3,2,1,0:T(8,128)(2,1)S(1)}, u32[]{:S(2)}, u32[]{:S(2)}) collective-permute-start(bf16[1,9,32,128]{3,2,1,0:T(8,128)(2,1)S(1)} %collective-permute-done.4.refs_4_), channel_id=1, source_target_pairs={{2,0},{3,1},{10,8},{11,9},{18,16},{19,17},{26,24},{27,25}} | collective-permute-start | bytes 221192 | tf_op jit(solution)/shard_map/ppermute | solution.py:376
  31.3 0.6 %collective-permute-done.2.refs_2_ = bf16[1,9,32,128]{3,2,1,0:T(8,128)(2,1)S(1)} collective-permute-done((bf16[1,9,32,128]{3,2,1,0:T(8,128)(2,1)}, bf16[1,9,32,128]{3,2,1,0:T(8,128)(2,1)S(1)}, u32[]{:S(2)}, u32[]{:S(2)}) %collective-permute-start.2) | collective-permute-done | bytes 73760 | tf_op jit(solution)/shard_map/ppermute | solution.py:376
  31.9 4.6 %collective-permute-done.1.refs_1_ = bf16[1,9,32,128]{3,2,1,0:T(8,128)(2,1)S(1)} collective-permute-done((bf16[1,9,32,128]{3,2,1,0:T(8,128)(2,1)}, bf16[1,9,32,128]{3,2,1,0:T(8,128)(2,1)S(1)}, u32[]{:S(2)}, u32[]{:S(2)}) %collective-permute-start.1) | collective-permute-done | bytes 73760 | tf_op jit(solution)/shard_map/ppermute | solution.py:376
  36.5 0.0 collective-permute-done.7.refs_7_
  36.5 0.0 collective-permute-done.6.refs_6_
  36.5 0.0 copy-start.6
  36.5 1.6 %collective-permute-done.5.refs_5_ = bf16[1,9,32,128]{3,2,1,0:T(8,128)(2,1)S(1)} collective-permute-done((bf16[1,9,32,128]{3,2,1,0:T(8,128)(2,1)S(1)}, bf16[1,9,32,128]{3,2,1,0:T(8,128)(2,1)S(1)}, u32[]{:S(2)}, u32[]{:S(2)}) %collective-permute-start.5) | collective-permute-done | bytes 73760 | tf_op jit(solution)/shard_map/ppermute | solution.py:376
  38.1 0.0 copy-done.1
  38.1 0.0 copy-done.2
  38.1 0.0 copy-done.3
  38.1 0.0 copy-done.4
  38.1 0.6 %copy-done.7 = bf16[1,9,32,128]{3,2,1,0:T(8,128)(2,1)} copy-done((bf16[1,9,32,128]{3,2,1,0:T(8,128)(2,1)}, bf16[1,9,32,128]{3,2,1,0:T(8,128)(2,1)S(1)}, u32[]{:S(2)}) %copy-start.7) | copy-done | bytes 73752
  38.8 3.7 %unpack.1 = bf16[7,72,1600]{2,1,0:T(8,128)(2,1)} custom-call(s32[1]{0:T(128)} %bitcast.where_ref, bf16[1,9,32,128]{3,2,1,0:T(8,128)(2,1)} %get-tuple-element.11.refs_0_, bf16[1,9,32,128]{3,2,1,0:T(8,128)(2,1)} %copy-done.4, bf16[1,9,32,128]{3,2,1,0:T(8,128)(2,1)} %copy-done.3, bf16[1,9,32,128]{3,2,1,0:T(8,128)(2,1)} %copy-done.2, ...), custom_call_target="tpu_custom_call" | custom-call | tf_op jit(solution)/shard_map/unpack/pallas_call | solution.py:304
  (8 shorter events, 0.0 us)
Async XLA Ops:
  2.2 3.7 %copy-start = (bf16[12,4,15625]{2,1,0:T(4,128)(2,1)S(1)}, bf16[12,4,15625]{2,1,0:T(4,128)(2,1)}, u32[]{:S(2)}) copy-start(bf16[12,4,15625]{2,1,0:T(4,128)(2,1)} %param.12) | copy-start | bytes 4500004
  5.4 10.7 %collective-permute-start = (bf16[16,400]{1,0:T(8,128)(2,1)}, bf16[16,400]{1,0:T(8,128)(2,1)S(1)}, u32[]{:S(2)}, u32[]{:S(2)}) collective-permute-start(bf16[16,400]{1,0:T(8,128)(2,1)} %get-tuple-element.9), channel_id=1, source_target_pairs={{0,8},{8,16},{16,24},{24,0},{1,9},{9,17},{17,25},{25,1},{2,10},{10... | collective-permute-start | bytes 38408 | tf_op jit(solution)/shard_map/ppermute | solution.py:332
  16.1 0.6 %copy-start.8 = (bf16[16,400]{1,0:T(8,128)(2,1)}, bf16[16,400]{1,0:T(8,128)(2,1)S(1)}, u32[]{:S(2)}) copy-start(bf16[16,400]{1,0:T(8,128)(2,1)S(1)} %collective-permute-done.minus_ref) | copy-start | bytes 38404
  18.7 6.4 %collective-permute-start.4 = (bf16[1,9,32,128]{3,2,1,0:T(8,128)(2,1)}, bf16[1,9,32,128]{3,2,1,0:T(8,128)(2,1)S(1)}, u32[]{:S(2)}, u32[]{:S(2)}) collective-permute-start(bf16[1,9,32,128]{3,2,1,0:T(8,128)(2,1)} %get-tuple-element.12), channel_id=1, source_target_pairs={{0,1},{1,0},{2,3},{3,2},{4,5},{5,4},{6,7},{7,6},{8,9},{9,8},{10,11... | collective-permute-start | bytes 221192 | tf_op jit(solution)/shard_map/ppermute | solution.py:371
  21.2 8.8 %collective-permute-start.3 = (bf16[1,9,32,128]{3,2,1,0:T(8,128)(2,1)}, bf16[1,9,32,128]{3,2,1,0:T(8,128)(2,1)S(1)}, u32[]{:S(2)}, u32[]{:S(2)}) collective-permute-start(bf16[1,9,32,128]{3,2,1,0:T(8,128)(2,1)} %get-tuple-element.11.refs_0_), channel_id=1, source_target_pairs={{6,0},{7,1},{14,8},{15,9},{22,16},{23,17},{30,24},{31,25}} | collective-permute-start | bytes 221192 | tf_op jit(solution)/shard_map/ppermute | solution.py:376
  22.5 9.4 %collective-permute-start.2 = (bf16[1,9,32,128]{3,2,1,0:T(8,128)(2,1)}, bf16[1,9,32,128]{3,2,1,0:T(8,128)(2,1)S(1)}, u32[]{:S(2)}, u32[]{:S(2)}) collective-permute-start(bf16[1,9,32,128]{3,2,1,0:T(8,128)(2,1)} %get-tuple-element.11.refs_0_), channel_id=1, source_target_pairs={{4,0},{5,1},{12,8},{13,9},{20,16},{21,17},{28,24},{29,25}} | collective-permute-start | bytes 221192 | tf_op jit(solution)/shard_map/ppermute | solution.py:376
  23.8 12.7 %collective-permute-start.1 = (bf16[1,9,32,128]{3,2,1,0:T(8,128)(2,1)}, bf16[1,9,32,128]{3,2,1,0:T(8,128)(2,1)S(1)}, u32[]{:S(2)}, u32[]{:S(2)}) collective-permute-start(bf16[1,9,32,128]{3,2,1,0:T(8,128)(2,1)} %get-tuple-element.11.refs_0_), channel_id=1, source_target_pairs={{2,0},{3,1},{10,8},{11,9},{18,16},{19,17},{26,24},{27,25}} | collective-permute-start | bytes 221192 | tf_op jit(solution)/shard_map/ppermute | solution.py:376
  25.1 13.0 %copy-start.1 = (bf16[1,9,32,128]{3,2,1,0:T(8,128)(2,1)}, bf16[1,9,32,128]{3,2,1,0:T(8,128)(2,1)S(1)}, u32[]{:S(2)}) copy-start(bf16[1,9,32,128]{3,2,1,0:T(8,128)(2,1)S(1)} %collective-permute-done.4.refs_4_) | copy-start | bytes 221188
  25.1 11.4 %collective-permute-start.7 = (bf16[1,9,32,128]{3,2,1,0:T(8,128)(2,1)S(1)}, bf16[1,9,32,128]{3,2,1,0:T(8,128)(2,1)S(1)}, u32[]{:S(2)}, u32[]{:S(2)}) collective-permute-start(bf16[1,9,32,128]{3,2,1,0:T(8,128)(2,1)S(1)} %collective-permute-done.4.refs_4_), channel_id=1, source_target_pairs={{6,0},{7,1},{14,8},{15,9},{22,16},{23,17},{30,24},{31,25}} | collective-permute-start | bytes 221192 | tf_op jit(solution)/shard_map/ppermute | solution.py:376
  26.4 10.1 %collective-permute-start.6 = (bf16[1,9,32,128]{3,2,1,0:T(8,128)(2,1)S(1)}, bf16[1,9,32,128]{3,2,1,0:T(8,128)(2,1)S(1)}, u32[]{:S(2)}, u32[]{:S(2)}) collective-permute-start(bf16[1,9,32,128]{3,2,1,0:T(8,128)(2,1)S(1)} %collective-permute-done.4.refs_4_), channel_id=1, source_target_pairs={{4,0},{5,1},{12,8},{13,9},{20,16},{21,17},{28,24},{29,25}} | collective-permute-start | bytes 221192 | tf_op jit(solution)/shard_map/ppermute | solution.py:376
  30.0 8.1 %copy-start.2 = (bf16[1,9,32,128]{3,2,1,0:T(8,128)(2,1)}, bf16[1,9,32,128]{3,2,1,0:T(8,128)(2,1)S(1)}, u32[]{:S(2)}) copy-start(bf16[1,9,32,128]{3,2,1,0:T(8,128)(2,1)S(1)} %collective-permute-done.3.refs_3_) | copy-start | bytes 221188
  30.0 8.1 %collective-permute-start.5 = (bf16[1,9,32,128]{3,2,1,0:T(8,128)(2,1)S(1)}, bf16[1,9,32,128]{3,2,1,0:T(8,128)(2,1)S(1)}, u32[]{:S(2)}, u32[]{:S(2)}) collective-permute-start(bf16[1,9,32,128]{3,2,1,0:T(8,128)(2,1)S(1)} %collective-permute-done.4.refs_4_), channel_id=1, source_target_pairs={{2,0},{3,1},{10,8},{11,9},{18,16},{19,17},{26,24},{27,25}} | collective-permute-start | bytes 221192 | tf_op jit(solution)/shard_map/ppermute | solution.py:376
  31.9 6.2 %copy-start.3 = (bf16[1,9,32,128]{3,2,1,0:T(8,128)(2,1)}, bf16[1,9,32,128]{3,2,1,0:T(8,128)(2,1)S(1)}, u32[]{:S(2)}) copy-start(bf16[1,9,32,128]{3,2,1,0:T(8,128)(2,1)S(1)} %collective-permute-done.2.refs_2_) | copy-start | bytes 221188
  36.5 1.6 %copy-start.4 = (bf16[1,9,32,128]{3,2,1,0:T(8,128)(2,1)}, bf16[1,9,32,128]{3,2,1,0:T(8,128)(2,1)S(1)}, u32[]{:S(2)}) copy-start(bf16[1,9,32,128]{3,2,1,0:T(8,128)(2,1)S(1)} %collective-permute-done.1.refs_1_) | copy-start | bytes 221188
  36.5 1.6 %copy-start.5 = (bf16[1,9,32,128]{3,2,1,0:T(8,128)(2,1)}, bf16[1,9,32,128]{3,2,1,0:T(8,128)(2,1)S(1)}, u32[]{:S(2)}) copy-start(bf16[1,9,32,128]{3,2,1,0:T(8,128)(2,1)S(1)} %collective-permute-done.7.refs_7_) | copy-start | bytes 221188
  36.5 1.6 %copy-start.6 = (bf16[1,9,32,128]{3,2,1,0:T(8,128)(2,1)}, bf16[1,9,32,128]{3,2,1,0:T(8,128)(2,1)S(1)}, u32[]{:S(2)}) copy-start(bf16[1,9,32,128]{3,2,1,0:T(8,128)(2,1)S(1)} %collective-permute-done.6.refs_6_) | copy-start | bytes 221188
  38.1 0.6 %copy-start.7 = (bf16[1,9,32,128]{3,2,1,0:T(8,128)(2,1)}, bf16[1,9,32,128]{3,2,1,0:T(8,128)(2,1)S(1)}, u32[]{:S(2)}) copy-start(bf16[1,9,32,128]{3,2,1,0:T(8,128)(2,1)S(1)} %collective-permute-done.5.refs_5_) | copy-start | bytes 221188

commit v5 on v4

--- a/solution.py
+++ b/solution.py
@@ -14,6 +14,7 @@
 PM = 2
 PC = 1
 LANES = 128
+GROUPS = 4
 F32 = jnp.float32
 BF16 = jnp.bfloat16
 VMEM = pl.BlockSpec(memory_space=pltpu.VMEM)
@@ -67,10 +68,7 @@
     face = np.kron(LINE, LINE)
     table = np.kron(face, np.kron(np.eye(NV), face))
     leading, remainder = split(table)
-    out = np.zeros((table.shape[0], 2 * LANES), BF16)
-    out[:, :UNIT] = leading
-    out[:, LANES : LANES + UNIT] = remainder
-    return out
+    return np.concatenate([leading.T, remainder.T], axis=0)
 
 
 def diag_tables():
@@ -128,15 +126,15 @@
 
 
 def face_product(pieces, pitch, table, stacked, products):
-    width = table.shape[0]
+    width = table.shape[1]
     if sum(x.shape[0] for _, x in pieces) < pitch:
         stacked[...] = jnp.zeros_like(stacked)
     for v in range(NV):
         for start, x in pieces:
             at = v * pitch + start
             stacked[at : at + x.shape[0], :] = x[:, v * width : (v + 1) * width]
-    y = jnp.dot(stacked[...], table[...], preferred_element_type=F32)
-    products[...] = y[:, :LANES] + y[:, LANES:]
+    y = lax.dot_general(stacked[...], table[...], (((1,), (1,)), ((), ())), preferred_element_type=F32)
+    products[:, :UNIT] = y[:, :UNIT] + y[:, UNIT:]
 
 
 def as_column(row, count):
@@ -156,23 +154,46 @@
     return jnp.where(slot == dest, 1.0, 0.0).astype(BF16)
 
 
-def xface_kernel(x_ref, table_ref, turn_ref, orient_ref, plus_ref, sent_ref, stacked, products, scratch):
-    pitch = stacked.shape[0] // NV
-    elems = pitch // 2
-    face_product([(f * elems, x_ref.at[f]) for f in range(2)], pitch, table_ref, stacked, products)
-    orient = as_column(orient_ref[...], elems)
-    for which, out_ref in enumerate((plus_ref, sent_ref)):
-        starts = [v * pitch + which * elems for v in range(NV)]
-        units = [products[s : s + elems, :] for s in starts]
+def faces_kernel(
+    x_hbm, side_hbm, table_hbm, turn_ref, orient_ref, plus_ref, sent_ref, out_ref,
+    x, side, table, x_stacked, x_products, stacked, products, scratch, rows, sems,
+):
+    copies = [
+        pltpu.make_async_copy(source, target, sems.at[i])
+        for i, (source, target) in enumerate([(table_hbm, table), (x_hbm, x), (side_hbm, side)])
+    ]
+    for copy in copies:
+        copy.start()
+    x_pitch = x_stacked.shape[0] // NV
+    pad = x_pitch // 2
+    orient = as_column(orient_ref[...], pad)
+    copies[0].wait()
+    copies[1].wait()
+    face_product([(f * pad, x.at[f]) for f in range(2)], x_pitch, table, x_stacked, x_products)
+    for which, turned_ref in enumerate((plus_ref, sent_ref)):
+        starts = [v * x_pitch + which * pad for v in range(NV)]
+        units = [x_products[s : s + pad, :] for s in starts]
         mine = jnp.concatenate(units, axis=0)[:, :UNIT].astype(BF16)
         turned = jnp.dot(mine, turn_ref[which], preferred_element_type=F32)
         for v in range(NV):
-            piece = turned[v * elems : (v + 1) * elems]
-            total = jnp.zeros((elems, LANES), F32)
+            piece = turned[v * pad : (v + 1) * pad]
+            total = jnp.zeros((pad, LANES), F32)
             for o in range(4):
                 total = jnp.where(orient == o, piece[:, o * LANES : (o + 1) * LANES], total)
             scratch[:, v * UNIT : (v + 1) * UNIT] = total[:, :UNIT]
-        out_ref[...] = scratch[...].astype(BF16)
+        turned_ref[...] = scratch[...].astype(BF16)
+    rows[...] = jnp.zeros_like(rows)
+    copies[2].wait()
+    elems = x.shape[1]
+    n_side = side.shape[0] // elems
+    pitch = stacked.shape[0] // NV
+    face_product([(0, side)], pitch, table, stacked, products)
+    for f in range(n_side):
+        for v in range(NV):
+            start = f * FACE + v * UNIT
+            unit = products[pl.ds(v * pitch + f, elems, stride=n_side), :]
+            rows[:elems, start : start + UNIT] = unit[:, :UNIT]
+    out_ref[...] = rows[...].astype(BF16)
 
 
 def coarse_block(block, right, left):
@@ -183,32 +204,15 @@
     return g[:NCOARSE] + g[NCOARSE:] + pltpu.roll(g[:NCOARSE], LANES // 2, 1)
 
 
-def main_kernel(
-    diag_hbm, side_hbm, table_hbm, right_ref, left_ref, out_ref,
-    blocks, side, table, stacked, products, coarse, rows, sems, *, many,
-):
+def diag_kernel(diag_hbm, right_ref, left_ref, out_ref, blocks, coarse, rows, sems, *, many):
     elems = blocks.shape[0]
-    n_side = side.shape[0] // elems
-    side_copy = pltpu.make_async_copy(side_hbm, side, sems.at[elems])
-    table_copy = pltpu.make_async_copy(table_hbm, table, sems.at[elems + 1])
 
     def block_copy(e):
         return pltpu.make_async_copy(diag_hbm.at[e], blocks.at[e], sems.at[e])
 
-    side_copy.start()
-    table_copy.start()
     for e in range(elems):
         block_copy(e).start()
     rows[...] = jnp.zeros_like(rows)
-    side_copy.wait()
-    table_copy.wait()
-    pitch = stacked.shape[0] // NV
-    face_product([(0, side)], pitch, table, stacked, products)
-    for f in range(n_side):
-        for v in range(NV):
-            start = (2 + f) * FACE + v * UNIT
-            unit = products[pl.ds(v * pitch + f, elems, stride=n_side), :]
-            rows[:elems, start : start + UNIT] = unit[:, :UNIT]
 
     def some_blocks(step, carry):
         for i in range(many):
@@ -222,25 +226,26 @@
     lax.fori_loop(0, elems // many, some_blocks, 0)
     for c in range(NCOARSE):
         piece = coarse[pl.ds(c, elems, stride=NCOARSE), :]
-        start = DIAG_AT + c * NCOARSE
-        rows[:elems, start : start + NCOARSE] = piece[:, :NCOARSE]
+        rows[:elems, c * NCOARSE : (c + 1) * NCOARSE] = piece[:, :NCOARSE]
     out_ref[...] = rows[...].astype(BF16)
 
 
-def pack_kernel(where_ref, rows_ref, minus_ref, plus_ref, owner_ref, keep_ref, send_ref, head, packed_scr, *, owners_n):
+def pack_kernel(
+    where_ref, minus_ref, plus_ref, side_ref, diag_ref, owner_ref, keep_ref, send_ref, rows, packed_scr, *, owners_n,
+):
     elems = owner_ref.shape[1]
-    cut = head.shape[1]
-    head[...] = rows_ref[:, :cut].astype(F32)
-    head[:, :FACE] = minus_ref[...].astype(F32)
-    head[:, FACE : 2 * FACE] = plus_ref[...].astype(F32)
+    rows[...] = jnp.zeros_like(rows)
+    start = 0
+    for ref in (minus_ref, plus_ref, side_ref):
+        rows[:, start : start + ref.shape[1]] = ref[...].astype(F32)
+        start += ref.shape[1]
+    rows[:, DIAG_AT : DIAG_AT + diag_ref.shape[1]] = diag_ref[...].astype(F32)
     most = keep_ref.shape[1]
     slots = owners_n * most
     placer = placement(owner_ref[...], where_ref[0], owners_n, most)
-    first = jnp.dot(placer, head[:elems].astype(BF16), preferred_element_type=F32)
-    rest = jnp.dot(placer, rows_ref[:elems, cut:], preferred_element_type=F32)
+    packed = jnp.dot(placer, rows[:elems].astype(BF16), preferred_element_type=F32)
     for j in range(ROW_TILES):
-        source, at = (first, j * LANES) if j * LANES < cut else (rest, j * LANES - cut)
-        packed_scr[pl.ds(j, slots, stride=ROW_TILES), :] = source[:, at : at + LANES]
+        packed_scr[pl.ds(j, slots, stride=ROW_TILES), :] = packed[:, j * LANES : (j + 1) * LANES]
     kept = most * ROW_TILES
     keep_ref[...] = packed_scr[:kept].astype(BF16).reshape(keep_ref.shape)
     send_ref[...] = packed_scr[kept:].astype(BF16).reshape(send_ref.shape)
@@ -311,56 +316,62 @@
     pad = round_up(elems, 16)
     grp_size = lax.axis_size("grp")
     slab_size = lax.axis_size("slab")
-    owners_n = grp_size // 4
+    owners_n = grp_size // GROUPS
     most = max(2, 3 * elems // (2 * owners_n))
     where = lax.axis_index("grp").astype(jnp.int32)[None]
     table = jnp.asarray(face_table())
     right, left = (jnp.asarray(t) for t in diag_tables())
 
     sds = jax.ShapeDtypeStruct
-    width = table.shape[0]
-    plus, sent = call(
-        xface_kernel,
-        (sds((pad, FACE), BF16), sds((pad, FACE), BF16)),
-        [
-            pltpu.VMEM((NV * 2 * pad, width), BF16),
-            pltpu.VMEM((NV * 2 * pad, LANES), F32),
-            pltpu.VMEM((pad, FACE), F32),
-        ],
-        jnp.transpose(xface_jac, (1, 0, 2)), table, jnp.asarray(turn_tables()), orient[None, :], name="xface",
-    )
-    minus = lax.ppermute(sent, "slab", [(i, (i + 1) % slab_size) for i in range(slab_size)])
-
+    width = table.shape[1]
     many = max(n for n in range(1, 4) if elems % n == 0)
     n_side = side_jac.shape[1]
     pitch = round_up(n_side * elems, 16)
-    chunk = (most, ROW_TILES, LANES)
-    rows = call(
-        functools.partial(main_kernel, many=many),
-        sds((pad, ROW_TILES * LANES), BF16),
+    hbm = pl.BlockSpec(memory_space=pl.ANY)
+    plus, sent, side = call(
+        faces_kernel,
+        (sds((pad, FACE), BF16), sds((pad, FACE), BF16), sds((pad, n_side * FACE), BF16)),
+        [
+            pltpu.VMEM((2, elems, length), BF16),
+            pltpu.VMEM((n_side * elems, length), BF16),
+            pltpu.VMEM(table.shape, BF16),
+            pltpu.VMEM((NV * 2 * pad, width), BF16),
+            pltpu.VMEM((NV * 2 * pad, LANES), F32),
+            pltpu.VMEM((NV * pitch, width), BF16),
+            pltpu.VMEM((NV * pitch, LANES), F32),
+            pltpu.VMEM((pad, FACE), F32),
+            pltpu.VMEM((pad, n_side * FACE), F32),
+            pltpu.SemaphoreType.DMA((3,)),
+        ],
+        jnp.transpose(xface_jac, (1, 0, 2)), side_jac.reshape(n_side * elems, length), table,
+        jnp.asarray(turn_tables()), orient[None, :],
+        in_specs=[hbm] * 3 + [VMEM] * 2,
+        name="faces",
+    )
+    minus = lax.ppermute(sent, "slab", [(i, (i + 1) % slab_size) for i in range(slab_size)])
+    diag = call(
+        functools.partial(diag_kernel, many=many),
+        sds((pad, NCOARSE * NCOARSE), BF16),
         [
             pltpu.VMEM((elems, nf, nf), BF16),
-            pltpu.VMEM((n_side * elems, length), BF16),
-            pltpu.VMEM(table.shape, BF16),
-            pltpu.VMEM((NV * pitch, width), BF16),
-            pltpu.VMEM((NV * pitch, LANES), F32),
             pltpu.VMEM((elems * NCOARSE, LANES), F32),
-            pltpu.VMEM((pad, ROW_TILES * LANES), F32),
-            pltpu.SemaphoreType.DMA((elems + 2,)),
+            pltpu.VMEM((pad, NCOARSE * NCOARSE), F32),
+            pltpu.SemaphoreType.DMA((elems,)),
         ],
-        diag_jac, side_jac.reshape(n_side * elems, length), table, right, left,
-        in_specs=[pl.BlockSpec(memory_space=pl.ANY)] * 3 + [VMEM] * 2,
-        name="main",
+        diag_jac, right, left,
+        in_specs=[hbm] + [VMEM] * 2,
+        name="diag",
     )
+    chunk = (most, ROW_TILES, LANES)
     keep, send = call(
         functools.partial(pack_kernel, owners_n=owners_n),
         (sds((1,) + chunk, BF16), sds((owners_n - 1,) + chunk, BF16)),
         [
-            pltpu.VMEM((pad, round_up(2 * FACE, LANES)), F32),
+            pltpu.VMEM((pad, ROW_TILES * LANES), F32),
             pltpu.VMEM((owners_n * most * ROW_TILES, LANES), F32),
         ],
-        where, rows, minus, plus, owner[None, :],
-        in_specs=[SMALL] + [VMEM] * 4,
+        where, minus, plus, side, diag, owner[None, :],
+        in_specs=[SMALL] + [VMEM] * 5,
         name="pack",
     )
 
@@ -372,9 +383,11 @@
     arrived = jnp.concatenate(arrived, axis=0) if len(arrived) > 1 else arrived[0]
 
     def to_owners(array):
-        return [array] + [
-            lax.ppermute(array, "grp", [(a * owners_n + o, o) for o in range(owners_n)]) for a in range(1, groups)
-        ]
+        results = [array]
+        for a in range(1, groups):
+            pairs = [(a * owners_n + o, o) for o in range(owners_n)]
+            results.append(lax.ppermute(array, "grp", pairs))
+        return results
 
     kept = to_owners(keep)
     others = to_owners(arrived)

time: 42.8 us -> 42.6 us (level)
  waiting for transfers between devices: 9.08 us -> 7.91 us
  Pallas kernels: 17.5 us -> 18.4 us
    reshape x1, local copies, waits for them, and re-layouts: 1.57 us -> 2.76 us  [shards(): side_jac.reshape(n_side * elems, length)]
    ppermute x6, waiting for transfers between devices: 9.08 us -> 7.91 us  [to_owners(): results.append(lax.ppermute(array, 'grp', pairs))]
    unnamed x19, local copies, waits for them, and re-layouts: 3.42 us -> 2.31 us
    pallas_call x4, Pallas kernels: 17.5 us -> 18.4 us  [call(): pl.pallas_call(kernel, out_shape=out_shape, scratch_shapes=scratch, **kwa...]
  transfers between devices with their start and end apart: 8 -> 8, of which waited for: 4 -> 5; matrix products, arithmetic and copies ran while one was open for 4% -> 0% of each run, Pallas kernels for 20% -> 18%
where the time goes in v5:
time: 42.6 us; the launch traced here: 42.3 us
  Pallas kernels  18.4 us (43%)
  starting transfers between devices  10.8 us (25%)
  waiting for transfers between devices  7.91 us (19%)
  local copies, waits for them, and re-layouts  5.07 us (12%)
    pallas_call x4, Pallas kernels, call(): pl.pallas_call(kernel, out_shape=out_shape, scratch_shapes=scratch, **kwa...  18.4 us
    ppermute x6, waiting for transfers between devices, to_owners(): results.append(lax.ppermute(array, 'grp', pairs))  7.91 us
    ppermute x6, starting transfers between devices, to_owners(): results.append(lax.ppermute(array, 'grp', pairs))  7.73 us
    reshape x1, local copies, waits for them, and re-layouts, shards(): side_jac.reshape(n_side * elems, length)  2.76 us
    ppermute x1, starting transfers between devices, shards(): arrived.append(lax.ppermute(send[j - 1:j], 'grp', pairs))  2.49 us
    unnamed x19, local copies, waits for them, and re-layouts  2.31 us
  transfers between devices with their start and end apart: 8, of which 5 were waited for; matrix products, arithmetic and copies ran while one was open for 0% of the time, Pallas kernels for 18%

profile of v5, /device:TPU:0, one launch (start us, length us, event | category | flops | bytes accessed | tf_op | source)
XLA Modules:
  0.0 42.3 jit_solution(13619648144023508267)
XLA Ops:
  0.0 2.8 %reshape.3.side_hbm = bf16[48,15625]{1,0:T(8,128)(2,1)} reshape(bf16[12,4,15625]{2,1,0:T(4,128)(2,1)} %param.12) | data formatting | bytes 3000000 | tf_op jit(solution)/shard_map/reshape | solution.py:346
  2.8 0.0 copy-done
  2.8 1.1 %copy.13 = bf16[12,2,15625]{2,0,1:T(8,128)(2,1)} copy(bf16[12,2,15625]{2,1,0:T(2,128)(2,1)S(1)} %copy-done) | data formatting | bytes 1500000 | tf_op args[1]
  3.8 5.2 %faces.1 = (bf16[16,400]{1,0:T(8,128)(2,1)}, bf16[16,400]{1,0:T(8,128)(2,1)}, bf16[16,1600]{1,0:T(8,128)(2,1)}) custom-call(bf16[2,12,15625]{2,1,0:T(8,128)(2,1)} %bitcast.7, bf16[48,15625]{1,0:T(8,128)(2,1)} %reshape.3.side_hbm, bf16[160,3125]{1,0:T(8,128)(2,1)} %constant.14.clone.table_hbm, bf16[2,80,512]{2,1,0:T(8,128)(2,1)} %constant.17.clone.turn_ref, ...), custom_call_target="tpu_custom_call" | custom-call | tf_op jit(solution)/shard_map/faces/pallas_call | solution.py:309
  9.0 0.5 %collective-permute-start = (bf16[16,400]{1,0:T(8,128)(2,1)}, bf16[16,400]{1,0:T(8,128)(2,1)S(1)}, u32[]{:S(2)}, u32[]{:S(2)}) collective-permute-start(bf16[16,400]{1,0:T(8,128)(2,1)} %get-tuple-element.10), channel_id=1, source_target_pairs={{0,8},{8,16},{16,24},{24,0},{1,9},{9,17},{17,25},{25,1},{2,10},{10... | collective-permute-start | bytes 38408 | tf_op jit(solution)/shard_map/ppermute | solution.py:351
  9.5 7.6 %diag.1.diag_ref = bf16[16,1600]{1,0:T(8,128)(2,1)} custom-call(bf16[12,625,625]{2,1,0:T(8,128)(2,1)} %diag_hbm.1, bf16[625,128]{1,0:T(8,128)(2,1)} %constant.15.clone.right_ref, bf16[80,625]{1,0:T(8,128)(2,1)} %constant.16.clone.left_ref), custom_call_target="tpu_custom_call" | custom-call | tf_op jit(solution)/shard_map/diag/pallas_call | solution.py:309
  17.2 0.0 collective-permute-done.minus_ref
  17.2 0.0 copy-start.8
  17.2 0.6 %copy-done.8 = bf16[16,400]{1,0:T(8,128)(2,1)} copy-done((bf16[16,400]{1,0:T(8,128)(2,1)}, bf16[16,400]{1,0:T(8,128)(2,1)S(1)}, u32[]{:S(2)}) %copy-start.8) | copy-done | bytes 12824
  17.8 1.9 %pack.1 = (bf16[1,9,32,128]{3,2,1,0:T(8,128)(2,1)}, bf16[1,9,32,128]{3,2,1,0:T(8,128)(2,1)}) custom-call(s32[1]{0:T(128)} %bitcast.where_ref, bf16[16,400]{1,0:T(8,128)(2,1)} %copy-done.8, bf16[16,400]{1,0:T(8,128)(2,1)} %get-tuple-element.11.plus_ref, bf16[16,1600]{1,0:T(8,128)(2,1)} %get-tuple-element.12.side_ref, bf16[16,1600]{1,0:T(8,128)(2,1)} %diag.1.diag_ref, ...), custom_call_target="tpu_custom_call" | custom-call | tf_op jit(solution)/shard_map/pack/pallas_call | solution.py:309
  19.7 2.5 %collective-permute-start.4 = (bf16[1,9,32,128]{3,2,1,0:T(8,128)(2,1)}, bf16[1,9,32,128]{3,2,1,0:T(8,128)(2,1)S(1)}, u32[]{:S(2)}, u32[]{:S(2)}) collective-permute-start(bf16[1,9,32,128]{3,2,1,0:T(8,128)(2,1)} %get-tuple-element.14), channel_id=1, source_target_pairs={{0,1},{1,0},{2,3},{3,2},{4,5},{5,4},{6,7},{7,6},{8,9},{9,8},{10,11... | collective-permute-start | bytes 221192 | tf_op jit(solution)/shard_map/ppermute | solution.py:382
  22.2 1.3 %collective-permute-start.1 = (bf16[1,9,32,128]{3,2,1,0:T(8,128)(2,1)}, bf16[1,9,32,128]{3,2,1,0:T(8,128)(2,1)S(1)}, u32[]{:S(2)}, u32[]{:S(2)}) collective-permute-start(bf16[1,9,32,128]{3,2,1,0:T(8,128)(2,1)} %get-tuple-element.13.refs_0_), channel_id=1, source_target_pairs={{2,0},{3,1},{10,8},{11,9},{18,16},{19,17},{26,24},{27,25}} | collective-permute-start | bytes 221192 | tf_op jit(solution)/shard_map/ppermute | solution.py:389
  23.5 1.3 %collective-permute-start.2 = (bf16[1,9,32,128]{3,2,1,0:T(8,128)(2,1)}, bf16[1,9,32,128]{3,2,1,0:T(8,128)(2,1)S(1)}, u32[]{:S(2)}, u32[]{:S(2)}) collective-permute-start(bf16[1,9,32,128]{3,2,1,0:T(8,128)(2,1)} %get-tuple-element.13.refs_0_), channel_id=1, source_target_pairs={{4,0},{5,1},{12,8},{13,9},{20,16},{21,17},{28,24},{29,25}} | collective-permute-start | bytes 221192 | tf_op jit(solution)/shard_map/ppermute | solution.py:389
  24.8 1.3 %collective-permute-start.3 = (bf16[1,9,32,128]{3,2,1,0:T(8,128)(2,1)}, bf16[1,9,32,128]{3,2,1,0:T(8,128)(2,1)S(1)}, u32[]{:S(2)}, u32[]{:S(2)}) collective-permute-start(bf16[1,9,32,128]{3,2,1,0:T(8,128)(2,1)} %get-tuple-element.13.refs_0_), channel_id=1, source_target_pairs={{6,0},{7,1},{14,8},{15,9},{22,16},{23,17},{30,24},{31,25}} | collective-permute-start | bytes 221192 | tf_op jit(solution)/shard_map/ppermute | solution.py:389
  26.1 0.0 collective-permute-done.4.refs_4_
  26.1 0.0 copy-start.1
  26.1 1.3 %collective-permute-start.5 = (bf16[1,9,32,128]{3,2,1,0:T(8,128)(2,1)S(1)}, bf16[1,9,32,128]{3,2,1,0:T(8,128)(2,1)S(1)}, u32[]{:S(2)}, u32[]{:S(2)}) collective-permute-start(bf16[1,9,32,128]{3,2,1,0:T(8,128)(2,1)S(1)} %collective-permute-done.4.refs_4_), channel_id=1, source_target_pairs={{2,0},{3,1},{10,8},{11,9},{18,16},{19,17},{26,24},{27,25}} | collective-permute-start | bytes 221192 | tf_op jit(solution)/shard_map/ppermute | solution.py:389
  27.4 1.3 %collective-permute-start.6 = (bf16[1,9,32,128]{3,2,1,0:T(8,128)(2,1)S(1)}, bf16[1,9,32,128]{3,2,1,0:T(8,128)(2,1)S(1)}, u32[]{:S(2)}, u32[]{:S(2)}) collective-permute-start(bf16[1,9,32,128]{3,2,1,0:T(8,128)(2,1)S(1)} %collective-permute-done.4.refs_4_), channel_id=1, source_target_pairs={{4,0},{5,1},{12,8},{13,9},{20,16},{21,17},{28,24},{29,25}} | collective-permute-start | bytes 221192 | tf_op jit(solution)/shard_map/ppermute | solution.py:389
  28.7 0.4 collective-permute-done.1.refs_1_
  29.1 1.3 %collective-permute-start.7 = (bf16[1,9,32,128]{3,2,1,0:T(8,128)(2,1)S(1)}, bf16[1,9,32,128]{3,2,1,0:T(8,128)(2,1)S(1)}, u32[]{:S(2)}, u32[]{:S(2)}) collective-permute-start(bf16[1,9,32,128]{3,2,1,0:T(8,128)(2,1)S(1)} %collective-permute-done.4.refs_4_), channel_id=1, source_target_pairs={{6,0},{7,1},{14,8},{15,9},{22,16},{23,17},{30,24},{31,25}} | collective-permute-start | bytes 221192 | tf_op jit(solution)/shard_map/ppermute | solution.py:389
  30.3 0.9 %collective-permute-done.2.refs_2_ = bf16[1,9,32,128]{3,2,1,0:T(8,128)(2,1)S(1)} collective-permute-done((bf16[1,9,32,128]{3,2,1,0:T(8,128)(2,1)}, bf16[1,9,32,128]{3,2,1,0:T(8,128)(2,1)S(1)}, u32[]{:S(2)}, u32[]{:S(2)}) %collective-permute-start.2) | collective-permute-done | bytes 73760 | tf_op jit(solution)/shard_map/ppermute | solution.py:389
  31.3 2.3 %collective-permute-done.3.refs_3_ = bf16[1,9,32,128]{3,2,1,0:T(8,128)(2,1)S(1)} collective-permute-done((bf16[1,9,32,128]{3,2,1,0:T(8,128)(2,1)}, bf16[1,9,32,128]{3,2,1,0:T(8,128)(2,1)S(1)}, u32[]{:S(2)}, u32[]{:S(2)}) %collective-permute-start.3) | collective-permute-done | bytes 73760 | tf_op jit(solution)/shard_map/ppermute | solution.py:389
  33.6 2.5 %collective-permute-done.5.refs_5_ = bf16[1,9,32,128]{3,2,1,0:T(8,128)(2,1)S(1)} collective-permute-done((bf16[1,9,32,128]{3,2,1,0:T(8,128)(2,1)S(1)}, bf16[1,9,32,128]{3,2,1,0:T(8,128)(2,1)S(1)}, u32[]{:S(2)}, u32[]{:S(2)}) %collective-permute-start.5) | collective-permute-done | bytes 73760 | tf_op jit(solution)/shard_map/ppermute | solution.py:389
  36.1 0.0 collective-permute-done.6.refs_6_
  36.1 1.8 %collective-permute-done.7.refs_7_ = bf16[1,9,32,128]{3,2,1,0:T(8,128)(2,1)S(1)} collective-permute-done((bf16[1,9,32,128]{3,2,1,0:T(8,128)(2,1)S(1)}, bf16[1,9,32,128]{3,2,1,0:T(8,128)(2,1)S(1)}, u32[]{:S(2)}, u32[]{:S(2)}) %collective-permute-start.7) | collective-permute-done | bytes 73760 | tf_op jit(solution)/shard_map/ppermute | solution.py:389
  37.9 0.0 copy-done.1
  37.9 0.0 copy-done.2
  37.9 0.0 copy-done.3
  37.9 0.0 copy-done.4
  37.9 0.0 copy-done.5
  38.0 0.6 %copy-done.7 = bf16[1,9,32,128]{3,2,1,0:T(8,128)(2,1)} copy-done((bf16[1,9,32,128]{3,2,1,0:T(8,128)(2,1)}, bf16[1,9,32,128]{3,2,1,0:T(8,128)(2,1)S(1)}, u32[]{:S(2)}) %copy-start.7) | copy-done | bytes 73752
  38.6 3.7 %unpack.1 = bf16[7,72,1600]{2,1,0:T(8,128)(2,1)} custom-call(s32[1]{0:T(128)} %bitcast.where_ref, bf16[1,9,32,128]{3,2,1,0:T(8,128)(2,1)} %get-tuple-element.13.refs_0_, bf16[1,9,32,128]{3,2,1,0:T(8,128)(2,1)} %copy-done.2, bf16[1,9,32,128]{3,2,1,0:T(8,128)(2,1)} %copy-done.3, bf16[1,9,32,128]{3,2,1,0:T(8,128)(2,1)} %copy-done.4, ...), custom_call_target="tpu_custom_call" | custom-call | tf_op jit(solution)/shard_map/unpack/pallas_call | solution.py:309
  (8 shorter events, 0.0 us)
Async XLA Ops:
  0.0 2.8 %copy-start = (bf16[12,2,15625]{2,1,0:T(2,128)(2,1)S(1)}, bf16[12,2,15625]{2,1,0:T(2,128)(2,1)}, u32[]{:S(2)}) copy-start(bf16[12,2,15625]{2,1,0:T(2,128)(2,1)} %param.11) | copy-start | bytes 2250004
  9.0 8.2 %collective-permute-start = (bf16[16,400]{1,0:T(8,128)(2,1)}, bf16[16,400]{1,0:T(8,128)(2,1)S(1)}, u32[]{:S(2)}, u32[]{:S(2)}) collective-permute-start(bf16[16,400]{1,0:T(8,128)(2,1)} %get-tuple-element.10), channel_id=1, source_target_pairs={{0,8},{8,16},{16,24},{24,0},{1,9},{9,17},{17,25},{25,1},{2,10},{10... | collective-permute-start | bytes 38408 | tf_op jit(solution)/shard_map/ppermute | solution.py:351
  17.2 0.6 %copy-start.8 = (bf16[16,400]{1,0:T(8,128)(2,1)}, bf16[16,400]{1,0:T(8,128)(2,1)S(1)}, u32[]{:S(2)}) copy-start(bf16[16,400]{1,0:T(8,128)(2,1)S(1)} %collective-permute-done.minus_ref) | copy-start | bytes 38404
  19.7 6.4 %collective-permute-start.4 = (bf16[1,9,32,128]{3,2,1,0:T(8,128)(2,1)}, bf16[1,9,32,128]{3,2,1,0:T(8,128)(2,1)S(1)}, u32[]{:S(2)}, u32[]{:S(2)}) collective-permute-start(bf16[1,9,32,128]{3,2,1,0:T(8,128)(2,1)} %get-tuple-element.14), channel_id=1, source_target_pairs={{0,1},{1,0},{2,3},{3,2},{4,5},{5,4},{6,7},{7,6},{8,9},{9,8},{10,11... | collective-permute-start | bytes 221192 | tf_op jit(solution)/shard_map/ppermute | solution.py:382
  22.2 6.9 %collective-permute-start.1 = (bf16[1,9,32,128]{3,2,1,0:T(8,128)(2,1)}, bf16[1,9,32,128]{3,2,1,0:T(8,128)(2,1)S(1)}, u32[]{:S(2)}, u32[]{:S(2)}) collective-permute-start(bf16[1,9,32,128]{3,2,1,0:T(8,128)(2,1)} %get-tuple-element.13.refs_0_), channel_id=1, source_target_pairs={{2,0},{3,1},{10,8},{11,9},{18,16},{19,17},{26,24},{27,25}} | collective-permute-start | bytes 221192 | tf_op jit(solution)/shard_map/ppermute | solution.py:389
  23.5 7.8 %collective-permute-start.2 = (bf16[1,9,32,128]{3,2,1,0:T(8,128)(2,1)}, bf16[1,9,32,128]{3,2,1,0:T(8,128)(2,1)S(1)}, u32[]{:S(2)}, u32[]{:S(2)}) collective-permute-start(bf16[1,9,32,128]{3,2,1,0:T(8,128)(2,1)} %get-tuple-element.13.refs_0_), channel_id=1, source_target_pairs={{4,0},{5,1},{12,8},{13,9},{20,16},{21,17},{28,24},{29,25}} | collective-permute-start | bytes 221192 | tf_op jit(solution)/shard_map/ppermute | solution.py:389
  24.8 8.8 %collective-permute-start.3 = (bf16[1,9,32,128]{3,2,1,0:T(8,128)(2,1)}, bf16[1,9,32,128]{3,2,1,0:T(8,128)(2,1)S(1)}, u32[]{:S(2)}, u32[]{:S(2)}) collective-permute-start(bf16[1,9,32,128]{3,2,1,0:T(8,128)(2,1)} %get-tuple-element.13.refs_0_), channel_id=1, source_target_pairs={{6,0},{7,1},{14,8},{15,9},{22,16},{23,17},{30,24},{31,25}} | collective-permute-start | bytes 221192 | tf_op jit(solution)/shard_map/ppermute | solution.py:389
  26.1 11.8 %copy-start.1 = (bf16[1,9,32,128]{3,2,1,0:T(8,128)(2,1)}, bf16[1,9,32,128]{3,2,1,0:T(8,128)(2,1)S(1)}, u32[]{:S(2)}) copy-start(bf16[1,9,32,128]{3,2,1,0:T(8,128)(2,1)S(1)} %collective-permute-done.4.refs_4_) | copy-start | bytes 221188
  26.1 10.0 %collective-permute-start.5 = (bf16[1,9,32,128]{3,2,1,0:T(8,128)(2,1)S(1)}, bf16[1,9,32,128]{3,2,1,0:T(8,128)(2,1)S(1)}, u32[]{:S(2)}, u32[]{:S(2)}) collective-permute-start(bf16[1,9,32,128]{3,2,1,0:T(8,128)(2,1)S(1)} %collective-permute-done.4.refs_4_), channel_id=1, source_target_pairs={{2,0},{3,1},{10,8},{11,9},{18,16},{19,17},{26,24},{27,25}} | collective-permute-start | bytes 221192 | tf_op jit(solution)/shard_map/ppermute | solution.py:389
  27.4 8.7 %collective-permute-start.6 = (bf16[1,9,32,128]{3,2,1,0:T(8,128)(2,1)S(1)}, bf16[1,9,32,128]{3,2,1,0:T(8,128)(2,1)S(1)}, u32[]{:S(2)}, u32[]{:S(2)}) collective-permute-start(bf16[1,9,32,128]{3,2,1,0:T(8,128)(2,1)S(1)} %collective-permute-done.4.refs_4_), channel_id=1, source_target_pairs={{4,0},{5,1},{12,8},{13,9},{20,16},{21,17},{28,24},{29,25}} | collective-permute-start | bytes 221192 | tf_op jit(solution)/shard_map/ppermute | solution.py:389
  29.1 8.9 %copy-start.2 = (bf16[1,9,32,128]{3,2,1,0:T(8,128)(2,1)}, bf16[1,9,32,128]{3,2,1,0:T(8,128)(2,1)S(1)}, u32[]{:S(2)}) copy-start(bf16[1,9,32,128]{3,2,1,0:T(8,128)(2,1)S(1)} %collective-permute-done.1.refs_1_) | copy-start | bytes 221188
  29.1 8.8 %collective-permute-start.7 = (bf16[1,9,32,128]{3,2,1,0:T(8,128)(2,1)S(1)}, bf16[1,9,32,128]{3,2,1,0:T(8,128)(2,1)S(1)}, u32[]{:S(2)}, u32[]{:S(2)}) collective-permute-start(bf16[1,9,32,128]{3,2,1,0:T(8,128)(2,1)S(1)} %collective-permute-done.4.refs_4_), channel_id=1, source_target_pairs={{6,0},{7,1},{14,8},{15,9},{22,16},{23,17},{30,24},{31,25}} | collective-permute-start | bytes 221192 | tf_op jit(solution)/shard_map/ppermute | solution.py:389
  31.3 6.7 %copy-start.3 = (bf16[1,9,32,128]{3,2,1,0:T(8,128)(2,1)}, bf16[1,9,32,128]{3,2,1,0:T(8,128)(2,1)S(1)}, u32[]{:S(2)}) copy-start(bf16[1,9,32,128]{3,2,1,0:T(8,128)(2,1)S(1)} %collective-permute-done.2.refs_2_) | copy-start | bytes 221188
  33.6 4.4 %copy-start.4 = (bf16[1,9,32,128]{3,2,1,0:T(8,128)(2,1)}, bf16[1,9,32,128]{3,2,1,0:T(8,128)(2,1)S(1)}, u32[]{:S(2)}) copy-start(bf16[1,9,32,128]{3,2,1,0:T(8,128)(2,1)S(1)} %collective-permute-done.3.refs_3_) | copy-start | bytes 221188
  36.1 1.9 %copy-start.5 = (bf16[1,9,32,128]{3,2,1,0:T(8,128)(2,1)}, bf16[1,9,32,128]{3,2,1,0:T(8,128)(2,1)S(1)}, u32[]{:S(2)}) copy-start(bf16[1,9,32,128]{3,2,1,0:T(8,128)(2,1)S(1)} %collective-permute-done.5.refs_5_) | copy-start | bytes 221188
  36.1 1.9 %copy-start.6 = (bf16[1,9,32,128]{3,2,1,0:T(8,128)(2,1)}, bf16[1,9,32,128]{3,2,1,0:T(8,128)(2,1)S(1)}, u32[]{:S(2)}) copy-start(bf16[1,9,32,128]{3,2,1,0:T(8,128)(2,1)S(1)} %collective-permute-done.6.refs_6_) | copy-start | bytes 221188
  37.9 0.6 %copy-start.7 = (bf16[1,9,32,128]{3,2,1,0:T(8,128)(2,1)}, bf16[1,9,32,128]{3,2,1,0:T(8,128)(2,1)S(1)}, u32[]{:S(2)}) copy-start(bf16[1,9,32,128]{3,2,1,0:T(8,128)(2,1)S(1)} %collective-permute-done.7.refs_7_) | copy-start | bytes 221188
